TPU v7x, 512 devices: a whole 4x8x8 slice. The times are simulated.
512 devices in a mesh: dp: 32 (over x, z), tensor: 16 (over y, core).
Axes of the slice: x: 4, y: 8, z: 8, core: 2. Of those that a mesh axis runs over, the one named last changes fastest.
Arguments:
- activations: bfloat16 [8192, 4096], P('dp'), may hold values from -6 to 6
- grad_output: bfloat16 [8192, 14336], P('dp', 'tensor'), may hold values from -6 to 6
- weight: bfloat16 [4096, 14336], P('dp', 'tensor'), may hold values from -0.09375 to 0.09375
- start_basis: float32 [14336, 64], P('tensor'), may hold values from -6 to 6
Outputs:
- input_grad: bfloat16 [8192, 4096], P('dp', 'tensor')
- right_basis: float32 [14336, 64], P('tensor')
- new_weight: float32 [4096, 14336], P('dp', 'tensor')
All inputs are finite; a program needn't handle non-finite values.
Results may differ from a plain program's by a relative error of at most 0.018.
Values may be sent and summed in bfloat16 or wider, within the bound.
No kernel may reach another device: no remote copies, remote signals or barrier semaphores. Data moves between devices by JAX's collectives and lax.ppermute only.
A program may use at most 128 MiB of HBM per device.

v0:
```python
import jax
import jax.numpy as jnp
from jax import lax
from jax.sharding import Mesh
from jax.sharding import PartitionSpec as P

DP = ("x", "z")
TENSOR = ("y", "c")
HIGH = lax.Precision.HIGHEST

learn_rate = 0.001


def swap(parts, axis):
    return lax.all_to_all(parts, axis, split_axis=0, concat_axis=0, tiled=True)


def share(x, axis):
    return swap(jnp.broadcast_to(x[None], (lax.axis_size(axis), *x.shape)), axis)


def input_gradient(grad_output, weight):
    n_x, n_z, n_y = (lax.axis_size(a) for a in ("x", "z", "y"))
    rows, hidden = weight.shape
    tokens = grad_output.shape[0]
    half = rows // 2
    halves = swap(weight.reshape(2, half, hidden), "c")
    weights = share(halves, "z")
    grads = share(grad_output, ("x", "c")).reshape(n_x, 2, tokens, hidden)
    weights = weights.reshape(2, n_z // 2, 2, half, hidden)
    partial = jnp.einsum("xkth,gzkrh->xgtzr", grads, weights, preferred_element_type=jnp.float32)
    parts = partial.astype(jnp.bfloat16).reshape(n_y, tokens, n_z // 2 * half)
    arrived = swap(parts, "y")
    summed = arrived.astype(jnp.float32).sum(axis=0).astype(jnp.bfloat16)
    pair = summed.reshape(tokens, 2, n_z // 4, half)
    core = lax.axis_index("c")
    flip = core == 1
    keep = jnp.where(flip, pair[:, 1], pair[:, 0])
    give = jnp.where(flip, pair[:, 0], pair[:, 1])
    keep_to, give_to = [], []
    for x in range(n_x):
        for y in range(n_y):
            for c in range(2):
                here = (x * n_y + y) * 2 + c
                there = ((y // 2) * n_y + 2 * x + y % 2) * 2
                keep_to.append((here, there + c))
                give_to.append((here, there + 1 - c))
    axes = ("x", "y", "c")
    mine = lax.ppermute(keep, axes, keep_to)
    other = lax.ppermute(give, axes, give_to)
    first = jnp.where(flip, other, mine)
    second = jnp.where(flip, mine, other)
    return jnp.stack([first, second], axis=2).reshape(tokens, -1)


def body(activations, grad_output, weight, start_basis):
    n_d, n_t = lax.axis_size(DP), lax.axis_size(TENSOR)
    tokens, features = activations.shape
    hidden = grad_output.shape[1]
    rows = weight.shape[0]
    rank = start_basis.shape[1]
    few = rank // n_t
    f32 = jnp.float32
    input_grad = input_gradient(grad_output, weight)
    a32, g32 = activations.astype(f32), grad_output.astype(f32)
    mixed = lax.dot_general(start_basis, g32, (((0,), (1,)), ((), ())), precision=HIGH)
    mixed = swap(mixed.reshape(n_t, few, tokens), TENSOR).sum(axis=0)
    left_part = jnp.dot(mixed, a32, precision=HIGH)
    left_part = jnp.swapaxes(left_part.reshape(few, n_d, rows), 0, 1)
    left_mine = swap(left_part, DP).sum(axis=0)
    left_few = jnp.swapaxes(share(left_mine, DP), 0, 1).reshape(few, features)
    seen = lax.dot_general(left_few, a32, (((1,), (1,)), ((), ())), precision=HIGH)
    both = share(jnp.concatenate([seen, left_mine], axis=1), TENSOR).reshape(rank, tokens + rows)
    seen, left_rows = both[:, :tokens], both[:, tokens:]
    right_part = jnp.dot(seen, g32, precision=HIGH)
    gram_part = lax.dot_general(left_rows, left_rows, (((1,), (1,)), ((), ())), precision=HIGH)
    pad = jnp.zeros((rank, 128 - rank), f32)
    packed = jnp.concatenate([right_part, gram_part, pad], axis=1).reshape(n_d, rank // n_d, -1)
    packed = share(swap(packed, DP).sum(axis=0), DP).reshape(rank, -1)
    right, gram_matrix = packed[:, :hidden], packed[:, hidden : hidden + rank]
    lower = jnp.linalg.cholesky(gram_matrix)
    solved = jax.scipy.linalg.solve_triangular(
        lower, jnp.concatenate([right, left_rows], axis=1), lower=True
    )
    right, basis_rows = solved[:, :hidden], solved[:, hidden:]
    right_basis = right.T / jnp.sqrt(f32(tokens * n_d))
    update = lax.dot_general(basis_rows, right, (((0,), (0,)), ((), ())), precision=HIGH)
    new_weight = weight.astype(f32) - learn_rate * update
    return (input_grad, right_basis, new_weight)


def solution(mesh):
    finer = Mesh(mesh.devices.reshape(4, 8, 8, 2), ("x", "z", "y", "c"))
    in_specs = (P(DP, None), P(DP, TENSOR), P(DP, TENSOR), P(TENSOR, None))
    out_specs = (P(DP, TENSOR), P(TENSOR, None), P(DP, TENSOR))
    return jax.shard_map(body, mesh=finer, in_specs=in_specs, out_specs=out_specs, check_vma=False)
```

profile of v0, /device:TPU:96, one launch (start us, length us, event | category | flops | bytes accessed | tf_op | source)
XLA Modules:
  0.0 255.8 jit_solution(9842712855507770131)
XLA Ops:
  0.6 0.0 copy-start
  0.6 0.9 copy-done
  1.6 1.5 fusion.19
  3.1 0.7 reshape.66
  3.8 7.2 %all-to-all-start.4 = ((f32[16,4,256]{2,1,0:T(4,128)}), f32[16,4,256]{2,1,0:T(4,128)S(1)}, u32[]{:S(2)}, u32[]{:S(2)}) async-start(f32[16,4,256]{2,1,0:T(4,128)} %reshape.66), calls=%async_computation.4 | async-start | bytes 131072 | tf_op jit(solution)/shard_map/all_to_all | solution.py:15
  11.0 4.1 %copy.21 = bf16[4096,256]{1,0:T(8,128)(2,1)} copy(bf16[4096,256]{0,1:T(8,128)(2,1)} %bitcast.61) | data formatting | bytes 4194304 | tf_op jit(solution)/shard_map/dot_general | solution.py:68
  15.1 0.0 copy-start.1
  15.1 0.0 all-to-all-done.4
  15.1 3.5 %convolution_bitcast_fusion = f32[32,4,128]{2,1,0:T(4,128)S(1)} fusion(bf16[32,128,256]{2,1,0:T(8,128)(2,1)} %bitcast.62, f32[4,256]{1,0:T(4,128)S(1)} %reduce_sum.40), kind=kOutput, calls=%fused_computation.4 | convolution fusion | flops 50331648 | bytes 2166784 | tf_op jit(solution)/shard_map/dot_general | solution.py:68
  18.6 0.0 copy-start.2
  18.6 21.6 %all_to_all.50 = f32[32,4,128]{2,1,0:T(4,128)S(1)} all-to-all(f32[32,4,128]{2,1,0:T(4,128)S(1)} %convolution_bitcast_fusion), channel_id=1, replica_groups=mesh['x'=4,'z'=8,'y'=8,'c'=2] {'x','z'}, dimensions={0} | all-to-all | bytes 131072 | tf_op jit(solution)/shard_map/all_to_all | solution.py:15
  40.3 13.1 %all_to_all.51 = f32[32,4,128]{2,1,0:T(4,128)S(1)} all-to-all(f32[32,4,128]{2,1,0:T(4,128)S(1)} %broadcast_in_dim.15), channel_id=1, replica_groups=mesh['x'=4,'z'=8,'y'=8,'c'=2] {'x','z'}, dimensions={0} | all-to-all | bytes 131072 | tf_op jit(solution)/shard_map/all_to_all | solution.py:15
  53.4 0.0 copy-done.1
  53.4 1.7 fusion.9
  55.2 10.8 %all_to_all.52 = f32[16,4,384]{2,1,0:T(4,128)S(1)} all-to-all(f32[16,4,384]{2,1,0:T(4,128)S(1)} %broadcast_in_dim.16), channel_id=1, replica_groups=mesh['x'=4,'z'=8,'y'=8,'c'=2] {'y','c'}, dimensions={0} | all-to-all | bytes 196608 | tf_op jit(solution)/shard_map/all_to_all | solution.py:15
  66.0 3.4 %all-to-all-start = ((bf16[2,64,896]{2,1,0:T(8,128)(2,1)}), bf16[2,64,896]{2,1,0:T(8,128)(2,1)S(1)}, u32[]{:S(2)}, u32[]{:S(2)}) async-start(bf16[2,64,896]{2,1,0:T(8,128)(2,1)} %bitcast), calls=%async_computation | async-start | bytes 458752 | tf_op jit(solution)/shard_map/all_to_all | solution.py:15
  69.5 0.0 copy-done.2
  69.5 0.3 fusion.7
  69.9 0.2 fusion.17
  70.1 0.1 pad_maximum_fusion
  70.1 0.1 reshape.69
  70.3 0.7 all-to-all-done
  71.0 16.8 %all_to_all.53 = f32[32,2,1024]{2,1,0:T(2,128)S(1)} all-to-all(f32[32,2,1024]{2,1,0:T(2,128)S(1)} %reshape.69), channel_id=1, replica_groups=mesh['x'=4,'z'=8,'y'=8,'c'=2] {'x','z'}, dimensions={0} | all-to-all | bytes 524288 | tf_op jit(solution)/shard_map/all_to_all | solution.py:15
  87.7 0.5 broadcast_in_dim.14
  88.2 47.3 %all_to_all.54 = bf16[8,256,896]{2,1,0:T(8,128)(2,1)} all-to-all(bf16[8,256,896]{2,1,0:T(8,128)(2,1)S(1)} %broadcast_in_dim.14), channel_id=1, replica_groups=mesh['x'=4,'z'=8,'y'=8,'c'=2] {'x','c'}, dimensions={0} | all-to-all | bytes 7340032 | tf_op jit(solution)/shard_map/all_to_all | solution.py:15
  135.5 1.5 broadcast_in_dim.13
  137.0 3.6 %all-to-all-start.1 = ((bf16[8,2,64,896]{3,2,1,0:T(8,128)(2,1)}), bf16[8,2,64,896]{3,2,1,0:T(8,128)(2,1)S(1)}, u32[]{:S(2)}, u32[]{:S(2)}) async-start(bf16[8,2,64,896]{3,2,1,0:T(8,128)(2,1)} %broadcast_in_dim.13), calls=%async_computation.1 | async-start | bytes 3670016 | tf_op jit(solution)/shard_map/all_to_all | solution.py:15
  140.6 0.1 reduce_sum.42
  140.7 43.9 %all-to-all-done.1 = bf16[8,2,64,896]{3,2,1,0:T(8,128)(2,1)S(1)} async-done(((bf16[8,2,64,896]{3,2,1,0:T(8,128)(2,1)}), bf16[8,2,64,896]{3,2,1,0:T(8,128)(2,1)S(1)}, u32[]{:S(2)}, u32[]{:S(2)}) %all-to-all-start.1) | async-done | bytes 1835040 | tf_op jit(solution)/shard_map/all_to_all | solution.py:15
  184.7 0.8 broadcast_in_dim.18
  185.4 5.0 %all-to-all-start.9 = ((f32[32,2,1024]{2,1,0:T(2,128)}), f32[32,2,1024]{2,1,0:T(2,128)S(1)}, u32[]{:S(2)}, u32[]{:S(2)}) async-start(f32[32,2,1024]{2,1,0:T(2,128)} %broadcast_in_dim.18), calls=%async_computation.9 | async-start | bytes 524288 | tf_op jit(solution)/shard_map/all_to_all | solution.py:15
  190.4 4.1 %fusion = bf16[4,2,256,4,64]{2,4,0,3,1:T(8,128)(2,1)S(1)} fusion(bf16[2,4,2,64,896,1]{4,3,2,5,1,0:T(8,128)(2,1)S(1)} %bitcast.64, bf16[4,2,256,896,1,1]{3,2,1,0,5,4:T(8,128)(2,1)} %bitcast.63), kind=kOutput, calls=%fused_computation.1 | convolution fusion | flops 1879572480 | bytes 6553600 | tf_op jit(solution)/shard_map/xkth,gzkrh->xgtzr/dot_general | solution.py:31
  194.5 1.1 copy.11
  195.6 7.6 %all-to-all-done.9 = f32[32,2,1024]{2,1,0:T(2,128)S(1)} async-done(((f32[32,2,1024]{2,1,0:T(2,128)}), f32[32,2,1024]{2,1,0:T(2,128)S(1)}, u32[]{:S(2)}, u32[]{:S(2)}) %all-to-all-start.9) | async-done | bytes 262176 | tf_op jit(solution)/shard_map/all_to_all | solution.py:15
  203.2 8.1 %all-to-all-start.3 = ((bf16[8,256,256]{1,2,0:T(8,128)(2,1)}), bf16[8,256,256]{1,2,0:T(8,128)(2,1)S(1)}, u32[]{:S(2)}, u32[]{:S(2)}) async-start(bf16[8,256,256]{1,2,0:T(8,128)(2,1)} %bitcast.10), calls=%async_computation.3 | async-start | bytes 2097152 | tf_op jit(solution)/shard_map/all_to_all | solution.py:15
  211.4 0.2 reshape.70
  211.6 0.1 copy.22
  211.7 5.8 %cholesky.15 = f32[64,64]{1,0:T(8,128)S(1)} custom-call(f32[64,64]{1,0:T(8,128)S(1)} %fusion.14), custom_call_target="Cholesky" | custom-call | tf_op jit(solution)/shard_map/jit(cholesky)/cholesky | solution.py:81
  217.6 0.6 compare_reduce_fusion
  218.2 0.7 fusion.11
  218.9 4.9 %custom-call.7 = f32[1,64,64]{1,2,0:T(8,128)S(1)} custom-call(f32[1,64,64]{2,1,0:T(8,128)S(1)} %fusion.11), custom_call_target="InvertDiagBlocksLowerTriangular" | custom-call | tf_op jit(solution)/shard_map/jit(_solve_triangular)/triangular_solve | solution.py:82
  223.8 0.4 fusion.2
  224.2 2.3 fusion.1
  226.5 7.8 %all-to-all-done.3 = bf16[8,256,256]{1,2,0:T(8,128)(2,1)S(1)} async-done(((bf16[8,256,256]{1,2,0:T(8,128)(2,1)}), bf16[8,256,256]{1,2,0:T(8,128)(2,1)S(1)}, u32[]{:S(2)}, u32[]{:S(2)}) %all-to-all-start.3) | async-done | bytes 1048608 | tf_op jit(solution)/shard_map/all_to_all | solution.py:15
  234.3 0.1 reduce_sum.39
  234.5 7.8 %collective-permute-start = (bf16[256,2,64]{0,2,1:T(8,128)(2,1)S(1)}, bf16[256,2,64]{0,2,1:T(8,128)(2,1)S(1)}, u32[]{:S(2)}, u32[]{:S(2)}) collective-permute-start(bf16[256,2,64]{0,2,1:T(8,128)(2,1)S(1)} %get-tuple-element.8), channel_id=1, source_target_pairs={{0,1},{1,0},{2,3},{3,2},{4,129},{5,128},{6,131},{7,130},{8,257},{9... | collective-permute-start | bytes 196616 | tf_op jit(solution)/shard_map/ppermute | solution.py:50
  242.3 2.3 collective-permute-start.1
  244.6 0.7 multiply_bitcast_fusion
  245.3 1.2 collective-permute-done
  246.5 8.5 %collective-permute-done.1 = bf16[256,2,64]{0,2,1:T(8,128)(2,1)S(1)} collective-permute-done((bf16[256,2,64]{0,2,1:T(8,128)(2,1)S(1)}, bf16[256,2,64]{0,2,1:T(8,128)(2,1)S(1)}, u32[]{:S(2)}, u32[]{:S(2)}) %collective-permute-start.1) | collective-permute-done | bytes 65568 | tf_op jit(solution)/shard_map/ppermute | solution.py:49
  255.1 0.8 copy.17
  (16 shorter events, 0.3 us)
Async XLA Ops:
  0.6 0.9 copy-start
  3.8 11.3 %all-to-all-start.4 = ((f32[16,4,256]{2,1,0:T(4,128)}), f32[16,4,256]{2,1,0:T(4,128)S(1)}, u32[]{:S(2)}, u32[]{:S(2)}) async-start(f32[16,4,256]{2,1,0:T(4,128)} %reshape.66), calls=%async_computation.4 | async-start | bytes 131072 | tf_op jit(solution)/shard_map/all_to_all | solution.py:15
  15.1 38.3 %copy-start.1 = (bf16[256,4096]{1,0:T(8,128)(2,1)S(1)}, bf16[256,4096]{1,0:T(8,128)(2,1)}, u32[]{:S(2)}) copy-start(bf16[256,4096]{1,0:T(8,128)(2,1)} %param.4) | copy-start | bytes 6291460
  18.6 50.9 %copy-start.2 = (bf16[256,896]{1,0:T(8,128)(2,1)S(1)}, bf16[256,896]{1,0:T(8,128)(2,1)}, u32[]{:S(2)}) copy-start(bf16[256,896]{1,0:T(8,128)(2,1)} %param.5) | copy-start | bytes 1376260
  66.0 5.0 %all-to-all-start = ((bf16[2,64,896]{2,1,0:T(8,128)(2,1)}), bf16[2,64,896]{2,1,0:T(8,128)(2,1)S(1)}, u32[]{:S(2)}, u32[]{:S(2)}) async-start(bf16[2,64,896]{2,1,0:T(8,128)(2,1)} %bitcast), calls=%async_computation | async-start | bytes 458752 | tf_op jit(solution)/shard_map/all_to_all | solution.py:15
  137.0 47.6 %all-to-all-start.1 = ((bf16[8,2,64,896]{3,2,1,0:T(8,128)(2,1)}), bf16[8,2,64,896]{3,2,1,0:T(8,128)(2,1)S(1)}, u32[]{:S(2)}, u32[]{:S(2)}) async-start(bf16[8,2,64,896]{3,2,1,0:T(8,128)(2,1)} %broadcast_in_dim.13), calls=%async_computation.1 | async-start | bytes 3670016 | tf_op jit(solution)/shard_map/all_to_all | solution.py:15
  185.4 17.8 %all-to-all-start.9 = ((f32[32,2,1024]{2,1,0:T(2,128)}), f32[32,2,1024]{2,1,0:T(2,128)S(1)}, u32[]{:S(2)}, u32[]{:S(2)}) async-start(f32[32,2,1024]{2,1,0:T(2,128)} %broadcast_in_dim.18), calls=%async_computation.9 | async-start | bytes 524288 | tf_op jit(solution)/shard_map/all_to_all | solution.py:15
  203.2 31.1 %all-to-all-start.3 = ((bf16[8,256,256]{1,2,0:T(8,128)(2,1)}), bf16[8,256,256]{1,2,0:T(8,128)(2,1)S(1)}, u32[]{:S(2)}, u32[]{:S(2)}) async-start(bf16[8,256,256]{1,2,0:T(8,128)(2,1)} %bitcast.10), calls=%async_computation.3 | async-start | bytes 2097152 | tf_op jit(solution)/shard_map/all_to_all | solution.py:15
  234.5 12.0 %collective-permute-start = (bf16[256,2,64]{0,2,1:T(8,128)(2,1)S(1)}, bf16[256,2,64]{0,2,1:T(8,128)(2,1)S(1)}, u32[]{:S(2)}, u32[]{:S(2)}) collective-permute-start(bf16[256,2,64]{0,2,1:T(8,128)(2,1)S(1)} %get-tuple-element.8), channel_id=1, source_target_pairs={{0,1},{1,0},{2,3},{3,2},{4,129},{5,128},{6,131},{7,130},{8,257},{9... | collective-permute-start | bytes 196616 | tf_op jit(solution)/shard_map/ppermute | solution.py:50
  242.3 12.7 %collective-permute-start.1 = (bf16[256,2,64]{0,2,1:T(8,128)(2,1)S(1)}, bf16[256,2,64]{0,2,1:T(8,128)(2,1)S(1)}, u32[]{:S(2)}, u32[]{:S(2)}) collective-permute-start(bf16[256,2,64]{0,2,1:T(8,128)(2,1)S(1)} %get-tuple-element.9), channel_id=1, source_target_pairs={{0,0},{1,1},{2,2},{3,3},{4,128},{5,129},{6,130},{7,131},{8,256},{9... | collective-permute-start | bytes 196616 | tf_op jit(solution)/shard_map/ppermute | solution.py:49
where the time goes:
time: 257 us; the launch traced here: 256 us
  blocking collectives  110 us (43%)
  waiting for transfers between devices  69.7 us (27%)
  starting transfers between devices  37.5 us (15%)
  matrix products  14.1 us (5%)
  other arithmetic  13.2 us (5%)
  local copies, waits for them, and re-layouts  10.8 us (4%)
    all_to_all x5, blocking collectives, swap(): return lax.all_to_all(parts, axis, split_axis=0, concat_axis=0, tiled=True)  110 us
    all_to_all x5, waiting for transfers between devices, swap(): return lax.all_to_all(parts, axis, split_axis=0, concat_axis=0, tiled=True)  60.1 us
    all_to_all x5, starting transfers between devices, swap(): return lax.all_to_all(parts, axis, split_axis=0, concat_axis=0, tiled=True)  27.4 us
    ppermute x1, waiting for transfers between devices, input_gradient(): mine = lax.ppermute(keep, axes, keep_to)  8.47 us
    ppermute x1, starting transfers between devices, input_gradient(): other = lax.ppermute(give, axes, give_to)  7.81 us
    another operation x3, other arithmetic, body(): lower = jnp.linalg.cholesky(gram_matrix)  6.52 us
    another operation x2, other arithmetic, body(): jax.scipy.linalg.solve_triangular(lower, jnp.concatenate([right, left_row...  5.55 us
  transfers between devices with their start and end apart: 7, of which 6 were waited for; matrix products, arithmetic and copies ran while one was open for 10% of the time, Pallas kernels for 0%

commit v1 on v0

--- a/solution.py
+++ b/solution.py
@@ -1,8 +1,13 @@
+import functools
+
 import jax
 import jax.numpy as jnp
 from jax import lax
+from jax.experimental import pallas as pl
+from jax.experimental.pallas import tpu as pltpu
 from jax.sharding import Mesh
 from jax.sharding import PartitionSpec as P
+
 
 DP = ("x", "z")
 TENSOR = ("y", "c")
@@ -19,22 +24,63 @@
     return swap(jnp.broadcast_to(x[None], (lax.axis_size(axis), *x.shape)), axis)
 
 
+def shifted(x, axis, by):
+    length = lax.axis_size(axis)
+    return lax.ppermute(x, axis, [(i, (i + by) % length) for i in range(length)])
+
+
+def block_kernel(n_x, n_z, n_y, where, *refs):
+    grads, weights = refs[:n_x], refs[n_x : n_x + n_z]
+    outs = refs[n_x + n_z : n_x + n_z + n_y]
+    packed, parts = refs[n_x + n_z + n_y :]
+    x, z, y = where[0], where[1], where[2]
+    half, hidden = weights[0].shape[1:]
+    group = n_z // 2
+    for s in range(n_z):
+        packed[lax.rem(z - s + n_z, n_z)] = weights[s][...]
+    dims = (((1,), (1,)), ((), ()))
+    for h in range(2):
+        rows = packed[h * group : (h + 1) * group]
+        first = rows[:, 0].reshape(group * half, hidden)
+        second = rows[:, 1].reshape(group * half, hidden)
+        for s in range(n_x):
+            total = lax.dot_general(grads[s][0], first, dims, preferred_element_type=jnp.float32)
+            total += lax.dot_general(grads[s][1], second, dims, preferred_element_type=jnp.float32)
+            parts[2 * lax.rem(x - s + n_x, n_x) + h] = total.astype(jnp.bfloat16)
+    for s in range(n_y):
+        outs[s][...] = parts[lax.rem(y + s, n_y)]
+
+
 def input_gradient(grad_output, weight):
     n_x, n_z, n_y = (lax.axis_size(a) for a in ("x", "z", "y"))
     rows, hidden = weight.shape
     tokens = grad_output.shape[0]
     half = rows // 2
-    halves = swap(weight.reshape(2, half, hidden), "c")
-    weights = share(halves, "z")
-    grads = share(grad_output, ("x", "c")).reshape(n_x, 2, tokens, hidden)
-    weights = weights.reshape(2, n_z // 2, 2, half, hidden)
-    partial = jnp.einsum("xkth,gzkrh->xgtzr", grads, weights, preferred_element_type=jnp.float32)
-    parts = partial.astype(jnp.bfloat16).reshape(n_y, tokens, n_z // 2 * half)
-    arrived = swap(parts, "y")
-    summed = arrived.astype(jnp.float32).sum(axis=0).astype(jnp.bfloat16)
-    pair = summed.reshape(tokens, 2, n_z // 4, half)
     core = lax.axis_index("c")
     flip = core == 1
+    keep = jnp.where(flip, weight[half:], weight[:half])
+    give = jnp.where(flip, weight[:half], weight[half:])
+    weights = jnp.stack([keep, shifted(give, "c", 1)])
+    grads = jnp.stack([grad_output, shifted(grad_output, "c", 1)])
+    weights = [weights] + [shifted(weights, "z", s) for s in range(1, n_z)]
+    grads = [grads] + [shifted(grads, "x", s) for s in range(1, n_x)]
+    where = jnp.stack([lax.axis_index(a) for a in ("x", "z", "y")]).astype(jnp.int32)
+    width = n_z // 2 * half
+    vmem = pl.BlockSpec(memory_space=pltpu.VMEM)
+    parts = pl.pallas_call(
+        functools.partial(block_kernel, n_x, n_z, n_y),
+        out_shape=[jax.ShapeDtypeStruct((tokens, width), jnp.bfloat16)] * n_y,
+        in_specs=[pl.BlockSpec(memory_space=pltpu.SMEM)] + [vmem] * (n_x + n_z),
+        out_specs=[vmem] * n_y,
+        scratch_shapes=[
+            pltpu.VMEM((n_z, 2, half, hidden), jnp.bfloat16),
+            pltpu.VMEM((n_y, tokens, width), jnp.bfloat16),
+        ],
+        name="blocks",
+    )(where, *grads, *weights)
+    arrived = [parts[0]] + [shifted(parts[s], "y", s) for s in range(1, n_y)]
+    summed = sum(a.astype(jnp.float32) for a in arrived).astype(jnp.bfloat16)
+    pair = summed.reshape(tokens, 2, n_z // 4, half)
     keep = jnp.where(flip, pair[:, 1], pair[:, 0])
     give = jnp.where(flip, pair[:, 0], pair[:, 1])
     keep_to, give_to = [], []
@@ -53,7 +99,7 @@
     return jnp.stack([first, second], axis=2).reshape(tokens, -1)
 
 
-def body(activations, grad_output, weight, start_basis):
+def step(activations, grad_output, weight, start_basis):
     n_d, n_t = lax.axis_size(DP), lax.axis_size(TENSOR)
     tokens, features = activations.shape
     hidden = grad_output.shape[1]
@@ -64,10 +110,12 @@
     input_grad = input_gradient(grad_output, weight)
     a32, g32 = activations.astype(f32), grad_output.astype(f32)
     mixed = lax.dot_general(start_basis, g32, (((0,), (1,)), ((), ())), precision=HIGH)
-    mixed = swap(mixed.reshape(n_t, few, tokens), TENSOR).sum(axis=0)
+    mixed = swap(mixed.reshape(n_t, few, tokens), TENSOR)
+    mixed = mixed.sum(axis=0)
     left_part = jnp.dot(mixed, a32, precision=HIGH)
     left_part = jnp.swapaxes(left_part.reshape(few, n_d, rows), 0, 1)
-    left_mine = swap(left_part, DP).sum(axis=0)
+    left_mine = swap(left_part, DP)
+    left_mine = left_mine.sum(axis=0)
     left_few = jnp.swapaxes(share(left_mine, DP), 0, 1).reshape(few, features)
     seen = lax.dot_general(left_few, a32, (((1,), (1,)), ((), ())), precision=HIGH)
     both = share(jnp.concatenate([seen, left_mine], axis=1), TENSOR).reshape(rank, tokens + rows)
@@ -93,4 +141,4 @@
     finer = Mesh(mesh.devices.reshape(4, 8, 8, 2), ("x", "z", "y", "c"))
     in_specs = (P(DP, None), P(DP, TENSOR), P(DP, TENSOR), P(TENSOR, None))
     out_specs = (P(DP, TENSOR), P(TENSOR, None), P(DP, TENSOR))
-    return jax.shard_map(body, mesh=finer, in_specs=in_specs, out_specs=out_specs, check_vma=False)
+    return jax.shard_map(step, mesh=finer, in_specs=in_specs, out_specs=out_specs, check_vma=False)

time: 257 us -> 220 us (0.86)
  the two profiles are of different devices: /device:TPU:96 before, /device:TPU:5 now
where the time goes in v1:
time: 220 us; the launch traced here: 218 us
  starting transfers between devices  138 us (63%)
  waiting for transfers between devices  37.3 us (17%)
  other arithmetic  16 us (7%)
  local copies, waits for them, and re-layouts  10.5 us (5%)
  matrix products  9.5 us (4%)
  Pallas kernels  6.1 us (3%)
    ppermute x19, starting transfers between devices, shifted(): lax.ppermute(x, axis, [(i, (i + by) % length) for i in range(length)])  75.1 us
    all_to_all x6, starting transfers between devices, swap(): return lax.all_to_all(parts, axis, split_axis=0, concat_axis=0, tiled=True)  48.6 us
    ppermute x19, waiting for transfers between devices, shifted(): lax.ppermute(x, axis, [(i, (i + by) % length) for i in range(length)])  21.1 us
    ppermute x1, starting transfers between devices, input_gradient(): other = lax.ppermute(give, axes, give_to)  9.35 us
    all_to_all x6, waiting for transfers between devices, swap(): return lax.all_to_all(parts, axis, split_axis=0, concat_axis=0, tiled=True)  8.48 us
    ppermute x1, waiting for transfers between devices, input_gradient(): mine = lax.ppermute(keep, axes, keep_to)  7.69 us
    another operation x3, other arithmetic, step(): lower = jnp.linalg.cholesky(gram_matrix)  6.52 us
    pallas_call x1, Pallas kernels, input_gradient(): pl.pallas_call(functools.partial(block_kernel, n_x, n_z, n_y), out_shape=...  6.1 us
  transfers between devices with their start and end apart: 27, of which 9 were waited for; matrix products, arithmetic and copies ran while one was open for 6% of the time, Pallas kernels for 3%

profile of v1, /device:TPU:5, one launch (start us, length us, event | category | flops | bytes accessed | tf_op | source)
XLA Modules:
  0.0 218.2 jit_solution(14264093912686177282)
XLA Ops:
  0.6 0.9 copy-done
  1.6 1.5 fusion.18
  3.1 0.7 reshape.48
  3.8 7.8 %all-to-all-start = ((f32[16,4,256]{2,1,0:T(4,128)}), f32[16,4,256]{2,1,0:T(4,128)S(1)}, u32[]{:S(2)}, u32[]{:S(2)}) async-start(f32[16,4,256]{2,1,0:T(4,128)} %reshape.48), calls=%async_computation | async-start | bytes 131072 | tf_op jit(solution)/shard_map/all_to_all | solution.py:20
  11.6 4.1 %copy.21 = bf16[4096,256]{1,0:T(8,128)(2,1)} copy(bf16[4096,256]{0,1:T(8,128)(2,1)} %bitcast.46) | data formatting | bytes 4194304 | tf_op jit(solution)/shard_map/dot_general | solution.py:115
  15.7 3.6 %all-to-all-done = f32[16,4,256]{2,1,0:T(4,128)S(1)} async-done(((f32[16,4,256]{2,1,0:T(4,128)}), f32[16,4,256]{2,1,0:T(4,128)S(1)}, u32[]{:S(2)}, u32[]{:S(2)}) %all-to-all-start) | async-done | bytes 65568 | tf_op jit(solution)/shard_map/all_to_all | solution.py:20
  19.4 4.0 %convolution_bitcast_fusion = f32[32,4,128]{2,1,0:T(4,128)} fusion(bf16[32,128,256]{2,1,0:T(8,128)(2,1)} %bitcast.47, f32[4,256]{1,0:T(4,128)S(1)} %reduce_sum.27), kind=kOutput, calls=%fused_computation.2 | convolution fusion | flops 50331648 | bytes 2166784 | tf_op jit(solution)/shard_map/dot_general | solution.py:115
  23.3 12.9 %all-to-all-start.1 = ((f32[32,4,128]{2,1,0:T(4,128)}), f32[32,4,128]{2,1,0:T(4,128)S(1)}, u32[]{:S(2)}, u32[]{:S(2)}) async-start(f32[32,4,128]{2,1,0:T(4,128)} %convolution_bitcast_fusion), calls=%async_computation.1 | async-start | bytes 131072 | tf_op jit(solution)/shard_map/all_to_all | solution.py:20
  36.2 2.6 %collective-permute-start.4 = (bf16[64,896]{1,0:T(8,128)(2,1)S(1)}, bf16[64,896]{1,0:T(8,128)(2,1)S(1)}, u32[]{:S(2)}, u32[]{:S(2)}) collective-permute-start(bf16[64,896]{1,0:T(8,128)(2,1)S(1)} %get-tuple-element.23), channel_id=1, source_target_pairs={{0,1},{1,0},{2,3},{3,2},{4,5},{5,4},{6,7},{7,6},{8,9},{9,8},{10,11... | collective-permute-start | bytes 344072 | tf_op jit(solution)/shard_map/ppermute | solution.py:29
  38.8 4.8 %all-to-all-done.1 = f32[32,4,128]{2,1,0:T(4,128)S(1)} async-done(((f32[32,4,128]{2,1,0:T(4,128)}), f32[32,4,128]{2,1,0:T(4,128)S(1)}, u32[]{:S(2)}, u32[]{:S(2)}) %all-to-all-start.1) | async-done | bytes 65568 | tf_op jit(solution)/shard_map/all_to_all | solution.py:20
  43.7 0.6 broadcast_in_dim.9
  44.4 5.2 %all-to-all-start.2 = ((f32[32,4,128]{2,1,0:T(4,128)}), f32[32,4,128]{2,1,0:T(4,128)S(1)}, u32[]{:S(2)}, u32[]{:S(2)}) async-start(f32[32,4,128]{2,1,0:T(4,128)} %broadcast_in_dim.9), calls=%async_computation.2 | async-start | bytes 131072 | tf_op jit(solution)/shard_map/all_to_all | solution.py:20
  49.6 3.7 %collective-permute-start = (bf16[256,896]{1,0:T(8,128)(2,1)S(1)}, bf16[256,896]{1,0:T(8,128)(2,1)}, u32[]{:S(2)}, u32[]{:S(2)}) collective-permute-start(bf16[256,896]{1,0:T(8,128)(2,1)S(1)} %copy-done.2), channel_id=1, source_target_pairs={{0,1},{1,0},{2,3},{3,2},{4,5},{5,4},{6,7},{7,6},{8,9},{9,8},{10,11... | collective-permute-start | bytes 1376264 | tf_op jit(solution)/shard_map/ppermute | solution.py:29
  53.4 5.2 %collective-permute-start.10 = (bf16[2,64,896]{2,1,0:T(8,128)(2,1)S(1)}, bf16[2,64,896]{2,1,0:T(8,128)(2,1)}, u32[]{:S(2)}, u32[]{:S(2)}) collective-permute-start(bf16[2,64,896]{2,1,0:T(8,128)(2,1)S(1)} %pad_maximum_fusion.2.refs_4_), channel_id=1, source_target_pairs={{0,96},{16,112},{32,0},{48,16},{64,32},{80,48},{96,64},{112,80},{1... | collective-permute-start | bytes 688136 | tf_op jit(solution)/shard_map/ppermute | solution.py:29
  58.7 1.7 fusion.8
  60.4 0.7 broadcast_in_dim.10
  61.1 4.4 %all-to-all-start.3 = ((f32[16,4,384]{2,1,0:T(4,128)}), f32[16,4,384]{2,1,0:T(4,128)S(1)}, u32[]{:S(2)}, u32[]{:S(2)}) async-start(f32[16,4,384]{2,1,0:T(4,128)} %broadcast_in_dim.10), calls=%async_computation.3 | async-start | bytes 196608 | tf_op jit(solution)/shard_map/all_to_all | solution.py:20
  65.5 1.1 pad_maximum_fusion.refs_0_
  66.6 2.9 %collective-permute-start.1 = (bf16[2,256,896]{2,1,0:T(8,128)(2,1)S(1)}, bf16[2,256,896]{2,1,0:T(8,128)(2,1)}, u32[]{:S(2)}, u32[]{:S(2)}) collective-permute-start(bf16[2,256,896]{2,1,0:T(8,128)(2,1)S(1)} %pad_maximum_fusion.refs_0_), channel_id=1, source_target_pairs={{0,128},{128,256},{256,384},{384,0},{1,129},{129,257},{257,385},{3... | collective-permute-start | bytes 2752520 | tf_op jit(solution)/shard_map/ppermute | solution.py:29
  69.6 3.2 %collective-permute-start.2 = (bf16[2,256,896]{2,1,0:T(8,128)(2,1)S(1)}, bf16[2,256,896]{2,1,0:T(8,128)(2,1)}, u32[]{:S(2)}, u32[]{:S(2)}) collective-permute-start(bf16[2,256,896]{2,1,0:T(8,128)(2,1)S(1)} %pad_maximum_fusion.refs_0_), channel_id=1, source_target_pairs={{0,256},{128,384},{256,0},{384,128},{1,257},{129,385},{257,1},{385... | collective-permute-start | bytes 2752520 | tf_op jit(solution)/shard_map/ppermute | solution.py:29
  72.8 3.6 %collective-permute-start.3 = (bf16[2,256,896]{2,1,0:T(8,128)(2,1)S(1)}, bf16[2,256,896]{2,1,0:T(8,128)(2,1)}, u32[]{:S(2)}, u32[]{:S(2)}) collective-permute-start(bf16[2,256,896]{2,1,0:T(8,128)(2,1)S(1)} %pad_maximum_fusion.refs_0_), channel_id=1, source_target_pairs={{0,384},{128,0},{256,128},{384,256},{1,385},{129,1},{257,129},{385... | collective-permute-start | bytes 2752520 | tf_op jit(solution)/shard_map/ppermute | solution.py:29
  76.4 2.2 collective-permute-start.11
  78.7 3.1 %collective-permute-start.5 = (bf16[2,64,896]{2,1,0:T(8,128)(2,1)S(1)}, bf16[2,64,896]{2,1,0:T(8,128)(2,1)S(1)}, u32[]{:S(2)}, u32[]{:S(2)}) collective-permute-start(bf16[2,64,896]{2,1,0:T(8,128)(2,1)S(1)} %pad_maximum_fusion.2.refs_4_), channel_id=1, source_target_pairs={{0,16},{16,32},{32,48},{48,64},{64,80},{80,96},{96,112},{112,0},{1... | collective-permute-start | bytes 688136 | tf_op jit(solution)/shard_map/ppermute | solution.py:29
  81.8 0.3 fusion.6
  82.1 2.5 %collective-permute-done.11.refs_11_ = bf16[2,64,896]{2,1,0:T(8,128)(2,1)S(1)} collective-permute-done((bf16[2,64,896]{2,1,0:T(8,128)(2,1)S(1)}, bf16[2,64,896]{2,1,0:T(8,128)(2,1)S(1)}, u32[]{:S(2)}, u32[]{:S(2)}) %collective-permute-start.11) | collective-permute-done | bytes 229408 | tf_op jit(solution)/shard_map/ppermute | solution.py:29
  84.6 2.6 %collective-permute-start.6 = (bf16[2,64,896]{2,1,0:T(8,128)(2,1)S(1)}, bf16[2,64,896]{2,1,0:T(8,128)(2,1)S(1)}, u32[]{:S(2)}, u32[]{:S(2)}) collective-permute-start(bf16[2,64,896]{2,1,0:T(8,128)(2,1)S(1)} %pad_maximum_fusion.2.refs_4_), channel_id=1, source_target_pairs={{0,32},{16,48},{32,64},{48,80},{64,96},{80,112},{96,0},{112,16},{1... | collective-permute-start | bytes 688136 | tf_op jit(solution)/shard_map/ppermute | solution.py:29
  87.2 0.5 collective-permute-done.5.refs_5_
  87.7 2.5 %collective-permute-start.7 = (bf16[2,64,896]{2,1,0:T(8,128)(2,1)S(1)}, bf16[2,64,896]{2,1,0:T(8,128)(2,1)S(1)}, u32[]{:S(2)}, u32[]{:S(2)}) collective-permute-start(bf16[2,64,896]{2,1,0:T(8,128)(2,1)S(1)} %pad_maximum_fusion.2.refs_4_), channel_id=1, source_target_pairs={{0,48},{16,64},{32,80},{48,96},{64,112},{80,0},{96,16},{112,32},{1... | collective-permute-start | bytes 688136 | tf_op jit(solution)/shard_map/ppermute | solution.py:29
  90.2 0.2 fusion.16
  90.5 0.9 reshape.51
  91.3 8.4 %all-to-all-start.4 = ((f32[32,2,1024]{2,1,0:T(2,128)}), f32[32,2,1024]{2,1,0:T(2,128)S(1)}, u32[]{:S(2)}, u32[]{:S(2)}) async-start(f32[32,2,1024]{2,1,0:T(2,128)} %reshape.51), calls=%async_computation.4 | async-start | bytes 524288 | tf_op jit(solution)/shard_map/all_to_all | solution.py:20
  99.7 7.0 %collective-permute-start.8 = (bf16[2,64,896]{2,1,0:T(8,128)(2,1)S(1)}, bf16[2,64,896]{2,1,0:T(8,128)(2,1)S(1)}, u32[]{:S(2)}, u32[]{:S(2)}) collective-permute-start(bf16[2,64,896]{2,1,0:T(8,128)(2,1)S(1)} %pad_maximum_fusion.2.refs_4_), channel_id=1, source_target_pairs={{0,64},{16,80},{32,96},{48,112},{64,0},{80,16},{96,32},{112,48},{1... | collective-permute-start | bytes 688136 | tf_op jit(solution)/shard_map/ppermute | solution.py:29
  106.7 7.1 %collective-permute-done.7.refs_7_ = bf16[2,64,896]{2,1,0:T(8,128)(2,1)S(1)} collective-permute-done((bf16[2,64,896]{2,1,0:T(8,128)(2,1)S(1)}, bf16[2,64,896]{2,1,0:T(8,128)(2,1)S(1)}, u32[]{:S(2)}, u32[]{:S(2)}) %collective-permute-start.7) | collective-permute-done | bytes 229408 | tf_op jit(solution)/shard_map/ppermute | solution.py:29
  113.8 1.9 collective-permute-start.9
  115.7 0.7 pad_add_fusion.where
  116.4 9.5 %collective-permute-done.8.refs_8_ = bf16[2,64,896]{2,1,0:T(8,128)(2,1)S(1)} collective-permute-done((bf16[2,64,896]{2,1,0:T(8,128)(2,1)S(1)}, bf16[2,64,896]{2,1,0:T(8,128)(2,1)S(1)}, u32[]{:S(2)}, u32[]{:S(2)}) %collective-permute-start.8) | collective-permute-done | bytes 229408 | tf_op jit(solution)/shard_map/ppermute | solution.py:29
  125.9 0.1 collective-permute-done.9.refs_9_
  126.1 0.5 copy-done.11
  126.6 0.1 copy-done.12
  126.7 6.1 %blocks.1 = (bf16[256,256]{1,0:T(8,128)(2,1)}, bf16[256,256]{1,0:T(8,128)(2,1)}, bf16[256,256]{1,0:T(8,128)(2,1)}, bf16[256,256]{1,0:T(8,128)(2,1)}, bf16[256,25...) custom-call(s32[3]{0:T(128)} %pad_add_fusion.where, ...), custom_call_target="tpu_custom_call" | custom-call | tf_op jit(solution)/shard_map/blocks/pallas_call | solution.py:70
  132.8 9.6 %collective-permute-start.12 = (bf16[256,256]{1,0:T(8,128)(2,1)}, bf16[256,256]{1,0:T(8,128)(2,1)S(1)}, u32[]{:S(2)}, u32[]{:S(2)}) collective-permute-start(bf16[256,256]{1,0:T(8,128)(2,1)} %get-tuple-element.12), channel_id=1, source_target_pairs={{0,2},{2,4},{4,6},{6,8},{8,10},{10,12},{12,14},{14,0},{1,3},{3,5},... | collective-permute-start | bytes 393224 | tf_op jit(solution)/shard_map/ppermute | solution.py:29
  142.5 4.0 %collective-permute-start.13 = (bf16[256,256]{1,0:T(8,128)(2,1)}, bf16[256,256]{1,0:T(8,128)(2,1)S(1)}, u32[]{:S(2)}, u32[]{:S(2)}) collective-permute-start(bf16[256,256]{1,0:T(8,128)(2,1)} %get-tuple-element.13), channel_id=1, source_target_pairs={{0,4},{2,6},{4,8},{6,10},{8,12},{10,14},{12,0},{14,2},{1,5},{3,7},... | collective-permute-start | bytes 393224 | tf_op jit(solution)/shard_map/ppermute | solution.py:29
  146.5 4.3 %collective-permute-start.14 = (bf16[256,256]{1,0:T(8,128)(2,1)}, bf16[256,256]{1,0:T(8,128)(2,1)S(1)}, u32[]{:S(2)}, u32[]{:S(2)}) collective-permute-start(bf16[256,256]{1,0:T(8,128)(2,1)} %get-tuple-element.14), channel_id=1, source_target_pairs={{0,6},{2,8},{4,10},{6,12},{8,14},{10,0},{12,2},{14,4},{1,7},{3,9},... | collective-permute-start | bytes 393224 | tf_op jit(solution)/shard_map/ppermute | solution.py:29
  150.8 4.0 %collective-permute-start.15 = (bf16[256,256]{1,0:T(8,128)(2,1)}, bf16[256,256]{1,0:T(8,128)(2,1)S(1)}, u32[]{:S(2)}, u32[]{:S(2)}) collective-permute-start(bf16[256,256]{1,0:T(8,128)(2,1)} %get-tuple-element.15), channel_id=1, source_target_pairs={{0,8},{2,10},{4,12},{6,14},{8,0},{10,2},{12,4},{14,6},{1,9},{3,11}... | collective-permute-start | bytes 393224 | tf_op jit(solution)/shard_map/ppermute | solution.py:29
  154.8 4.3 %collective-permute-start.16 = (bf16[256,256]{1,0:T(8,128)(2,1)}, bf16[256,256]{1,0:T(8,128)(2,1)S(1)}, u32[]{:S(2)}, u32[]{:S(2)}) collective-permute-start(bf16[256,256]{1,0:T(8,128)(2,1)} %get-tuple-element.16), channel_id=1, source_target_pairs={{0,10},{2,12},{4,14},{6,0},{8,2},{10,4},{12,6},{14,8},{1,11},{3,13... | collective-permute-start | bytes 393224 | tf_op jit(solution)/shard_map/ppermute | solution.py:29
  159.1 5.2 %collective-permute-start.17 = (bf16[256,256]{1,0:T(8,128)(2,1)}, bf16[256,256]{1,0:T(8,128)(2,1)S(1)}, u32[]{:S(2)}, u32[]{:S(2)}) collective-permute-start(bf16[256,256]{1,0:T(8,128)(2,1)} %get-tuple-element.17), channel_id=1, source_target_pairs={{0,12},{2,14},{4,0},{6,2},{8,4},{10,6},{12,8},{14,10},{1,13},{3,15... | collective-permute-start | bytes 393224 | tf_op jit(solution)/shard_map/ppermute | solution.py:29
  164.3 3.1 %collective-permute-start.18 = (bf16[256,256]{1,0:T(8,128)(2,1)}, bf16[256,256]{1,0:T(8,128)(2,1)S(1)}, u32[]{:S(2)}, u32[]{:S(2)}) collective-permute-start(bf16[256,256]{1,0:T(8,128)(2,1)} %get-tuple-element.18), channel_id=1, source_target_pairs={{0,14},{2,0},{4,2},{6,4},{8,6},{10,8},{12,10},{14,12},{1,15},{3,1}... | collective-permute-start | bytes 393224 | tf_op jit(solution)/shard_map/ppermute | solution.py:29
  167.5 0.8 broadcast_in_dim.12
  168.3 9.9 %all-to-all-start.5 = ((f32[32,2,1024]{2,1,0:T(2,128)}), f32[32,2,1024]{2,1,0:T(2,128)S(1)}, u32[]{:S(2)}, u32[]{:S(2)}) async-start(f32[32,2,1024]{2,1,0:T(2,128)} %broadcast_in_dim.12), calls=%async_computation.5 | async-start | bytes 524288 | tf_op jit(solution)/shard_map/all_to_all | solution.py:20
  178.3 1.4 collective-permute-done.18
  179.7 1.0 add_convert_fusion
  180.7 0.1 copy.15
  180.8 9.4 %collective-permute-start.19 = (bf16[256,2,64]{0,2,1:T(8,128)(2,1)S(1)}, bf16[256,2,64]{0,2,1:T(8,128)(2,1)S(1)}, u32[]{:S(2)}, u32[]{:S(2)}) collective-permute-start(bf16[256,2,64]{0,2,1:T(8,128)(2,1)S(1)} %get-tuple-element.26), channel_id=1, source_target_pairs={{0,1},{1,0},{2,3},{3,2},{4,129},{5,128},{6,131},{7,130},{8,257},{9... | collective-permute-start | bytes 196616 | tf_op jit(solution)/shard_map/ppermute | solution.py:96
  190.2 4.6 %collective-permute-start.20 = (bf16[256,2,64]{0,2,1:T(8,128)(2,1)S(1)}, bf16[256,2,64]{0,2,1:T(8,128)(2,1)S(1)}, u32[]{:S(2)}, u32[]{:S(2)}) collective-permute-start(bf16[256,2,64]{0,2,1:T(8,128)(2,1)S(1)} %get-tuple-element.27), channel_id=1, source_target_pairs={{0,0},{1,1},{2,2},{3,3},{4,128},{5,129},{6,130},{7,131},{8,256},{9... | collective-permute-start | bytes 196616 | tf_op jit(solution)/shard_map/ppermute | solution.py:95
  194.8 7.7 %collective-permute-done.20 = bf16[256,2,64]{0,2,1:T(8,128)(2,1)S(1)} collective-permute-done((bf16[256,2,64]{0,2,1:T(8,128)(2,1)S(1)}, bf16[256,2,64]{0,2,1:T(8,128)(2,1)S(1)}, u32[]{:S(2)}, u32[]{:S(2)}) %collective-permute-start.20) | collective-permute-done | bytes 65568 | tf_op jit(solution)/shard_map/ppermute | solution.py:95
  202.5 0.8 copy.20
  203.3 0.2 reshape.52
  203.6 5.8 %cholesky.15 = f32[64,64]{1,0:T(8,128)S(1)} custom-call(f32[64,64]{1,0:T(8,128)S(1)} %fusion.13), custom_call_target="Cholesky" | custom-call | tf_op jit(solution)/shard_map/jit(cholesky)/cholesky | solution.py:129
  209.5 0.6 compare_reduce_fusion
  210.2 0.7 fusion.10
  210.8 4.9 %custom-call.7 = f32[1,64,64]{1,2,0:T(8,128)S(1)} custom-call(f32[1,64,64]{2,1,0:T(8,128)S(1)} %fusion.10), custom_call_target="InvertDiagBlocksLowerTriangular" | custom-call | tf_op jit(solution)/shard_map/jit(_solve_triangular)/triangular_solve | solution.py:130
  215.7 0.4 fusion.1
  216.2 1.4 fusion
  217.5 0.7 multiply_bitcast_fusion
  (61 shorter events, 0.7 us)
Async XLA Ops:
  0.6 0.9 copy-start
  3.8 15.6 %all-to-all-start = ((f32[16,4,256]{2,1,0:T(4,128)}), f32[16,4,256]{2,1,0:T(4,128)S(1)}, u32[]{:S(2)}, u32[]{:S(2)}) async-start(f32[16,4,256]{2,1,0:T(4,128)} %reshape.48), calls=%async_computation | async-start | bytes 131072 | tf_op jit(solution)/shard_map/all_to_all | solution.py:20
  11.6 24.6 %copy-start.5 = (bf16[128,896]{1,0:T(8,128)(2,1)S(1)}, bf16[128,896]{1,0:T(8,128)(2,1)}, u32[]{:S(2)}) copy-start(bf16[128,896]{1,0:T(8,128)(2,1)} %param.6) | copy-start | bytes 688132
  15.7 33.9 %copy-start.2 = (bf16[256,896]{1,0:T(8,128)(2,1)S(1)}, bf16[256,896]{1,0:T(8,128)(2,1)}, u32[]{:S(2)}) copy-start(bf16[256,896]{1,0:T(8,128)(2,1)} %param.5) | copy-start | bytes 1376260
  15.7 43.0 %copy-start.1 = (bf16[256,4096]{1,0:T(8,128)(2,1)S(1)}, bf16[256,4096]{1,0:T(8,128)(2,1)}, u32[]{:S(2)}) copy-start(bf16[256,4096]{1,0:T(8,128)(2,1)} %param.4) | copy-start | bytes 6291460
  23.3 20.4 %all-to-all-start.1 = ((f32[32,4,128]{2,1,0:T(4,128)}), f32[32,4,128]{2,1,0:T(4,128)S(1)}, u32[]{:S(2)}, u32[]{:S(2)}) async-start(f32[32,4,128]{2,1,0:T(4,128)} %convolution_bitcast_fusion), calls=%async_computation.1 | async-start | bytes 131072 | tf_op jit(solution)/shard_map/all_to_all | solution.py:20
  36.2 17.1 %collective-permute-start.4 = (bf16[64,896]{1,0:T(8,128)(2,1)S(1)}, bf16[64,896]{1,0:T(8,128)(2,1)S(1)}, u32[]{:S(2)}, u32[]{:S(2)}) collective-permute-start(bf16[64,896]{1,0:T(8,128)(2,1)S(1)} %get-tuple-element.23), channel_id=1, source_target_pairs={{0,1},{1,0},{2,3},{3,2},{4,5},{5,4},{6,7},{7,6},{8,9},{9,8},{10,11... | collective-permute-start | bytes 344072 | tf_op jit(solution)/shard_map/ppermute | solution.py:29
  44.4 14.3 %all-to-all-start.2 = ((f32[32,4,128]{2,1,0:T(4,128)}), f32[32,4,128]{2,1,0:T(4,128)S(1)}, u32[]{:S(2)}, u32[]{:S(2)}) async-start(f32[32,4,128]{2,1,0:T(4,128)} %broadcast_in_dim.9), calls=%async_computation.2 | async-start | bytes 131072 | tf_op jit(solution)/shard_map/all_to_all | solution.py:20
  49.6 15.9 %collective-permute-start = (bf16[256,896]{1,0:T(8,128)(2,1)S(1)}, bf16[256,896]{1,0:T(8,128)(2,1)}, u32[]{:S(2)}, u32[]{:S(2)}) collective-permute-start(bf16[256,896]{1,0:T(8,128)(2,1)S(1)} %copy-done.2), channel_id=1, source_target_pairs={{0,1},{1,0},{2,3},{3,2},{4,5},{5,4},{6,7},{7,6},{8,9},{9,8},{10,11... | collective-permute-start | bytes 1376264 | tf_op jit(solution)/shard_map/ppermute | solution.py:29
  53.4 60.4 %copy-start.4 = (bf16[2,64,896]{2,1,0:T(8,128)(2,1)}, bf16[2,64,896]{2,1,0:T(8,128)(2,1)S(1)}, u32[]{:S(2)}) copy-start(bf16[2,64,896]{2,1,0:T(8,128)(2,1)S(1)} %pad_maximum_fusion.2.refs_4_) | copy-start | bytes 688132
  53.4 25.2 %collective-permute-start.10 = (bf16[2,64,896]{2,1,0:T(8,128)(2,1)S(1)}, bf16[2,64,896]{2,1,0:T(8,128)(2,1)}, u32[]{:S(2)}, u32[]{:S(2)}) collective-permute-start(bf16[2,64,896]{2,1,0:T(8,128)(2,1)S(1)} %pad_maximum_fusion.2.refs_4_), channel_id=1, source_target_pairs={{0,96},{16,112},{32,0},{48,16},{64,32},{80,48},{96,64},{112,80},{1... | collective-permute-start | bytes 688136 | tf_op jit(solution)/shard_map/ppermute | solution.py:29
  61.1 17.5 %all-to-all-start.3 = ((f32[16,4,384]{2,1,0:T(4,128)}), f32[16,4,384]{2,1,0:T(4,128)S(1)}, u32[]{:S(2)}, u32[]{:S(2)}) async-start(f32[16,4,384]{2,1,0:T(4,128)} %broadcast_in_dim.10), calls=%async_computation.3 | async-start | bytes 196608 | tf_op jit(solution)/shard_map/all_to_all | solution.py:20
  66.6 59.5 %copy-start.3 = (bf16[2,256,896]{2,1,0:T(8,128)(2,1)}, bf16[2,256,896]{2,1,0:T(8,128)(2,1)S(1)}, u32[]{:S(2)}) copy-start(bf16[2,256,896]{2,1,0:T(8,128)(2,1)S(1)} %pad_maximum_fusion.refs_0_) | copy-start | bytes 2752516
  66.6 59.4 %collective-permute-start.1 = (bf16[2,256,896]{2,1,0:T(8,128)(2,1)S(1)}, bf16[2,256,896]{2,1,0:T(8,128)(2,1)}, u32[]{:S(2)}, u32[]{:S(2)}) collective-permute-start(bf16[2,256,896]{2,1,0:T(8,128)(2,1)S(1)} %pad_maximum_fusion.refs_0_), channel_id=1, source_target_pairs={{0,128},{128,256},{256,384},{384,0},{1,129},{129,257},{257,385},{3... | collective-permute-start | bytes 2752520 | tf_op jit(solution)/shard_map/ppermute | solution.py:29
  69.6 56.5 %collective-permute-start.2 = (bf16[2,256,896]{2,1,0:T(8,128)(2,1)S(1)}, bf16[2,256,896]{2,1,0:T(8,128)(2,1)}, u32[]{:S(2)}, u32[]{:S(2)}) collective-permute-start(bf16[2,256,896]{2,1,0:T(8,128)(2,1)S(1)} %pad_maximum_fusion.refs_0_), channel_id=1, source_target_pairs={{0,256},{128,384},{256,0},{384,128},{1,257},{129,385},{257,1},{385... | collective-permute-start | bytes 2752520 | tf_op jit(solution)/shard_map/ppermute | solution.py:29
  72.8 53.3 %collective-permute-start.3 = (bf16[2,256,896]{2,1,0:T(8,128)(2,1)S(1)}, bf16[2,256,896]{2,1,0:T(8,128)(2,1)}, u32[]{:S(2)}, u32[]{:S(2)}) collective-permute-start(bf16[2,256,896]{2,1,0:T(8,128)(2,1)S(1)} %pad_maximum_fusion.refs_0_), channel_id=1, source_target_pairs={{0,384},{128,0},{256,128},{384,256},{1,385},{129,1},{257,129},{385... | collective-permute-start | bytes 2752520 | tf_op jit(solution)/shard_map/ppermute | solution.py:29
  76.4 8.2 %collective-permute-start.11 = (bf16[2,64,896]{2,1,0:T(8,128)(2,1)S(1)}, bf16[2,64,896]{2,1,0:T(8,128)(2,1)S(1)}, u32[]{:S(2)}, u32[]{:S(2)}) collective-permute-start(bf16[2,64,896]{2,1,0:T(8,128)(2,1)S(1)} %pad_maximum_fusion.2.refs_4_), channel_id=1, source_target_pairs={{0,112},{16,0},{32,16},{48,32},{64,48},{80,64},{96,80},{112,96},{1... | collective-permute-start | bytes 688136 | tf_op jit(solution)/shard_map/ppermute | solution.py:29
  78.6 116.1 %copy-start.6 = (f32[64,384]{1,0:T(8,128)}, f32[64,384]{1,0:T(8,128)S(1)}, u32[]{:S(2)}) copy-start(f32[64,384]{1,0:T(8,128)S(1)} %reshape.50) | copy-start | bytes 294916
  78.7 9.0 %collective-permute-start.5 = (bf16[2,64,896]{2,1,0:T(8,128)(2,1)S(1)}, bf16[2,64,896]{2,1,0:T(8,128)(2,1)S(1)}, u32[]{:S(2)}, u32[]{:S(2)}) collective-permute-start(bf16[2,64,896]{2,1,0:T(8,128)(2,1)S(1)} %pad_maximum_fusion.2.refs_4_), channel_id=1, source_target_pairs={{0,16},{16,32},{32,48},{48,64},{64,80},{80,96},{96,112},{112,0},{1... | collective-permute-start | bytes 688136 | tf_op jit(solution)/shard_map/ppermute | solution.py:29
  84.6 41.5 %copy-start.7 = (bf16[2,64,896]{2,1,0:T(8,128)(2,1)}, bf16[2,64,896]{2,1,0:T(8,128)(2,1)S(1)}, u32[]{:S(2)}) copy-start(bf16[2,64,896]{2,1,0:T(8,128)(2,1)S(1)} %collective-permute-done.11.refs_11_) | copy-start | bytes 688132
  84.6 15.0 %collective-permute-start.6 = (bf16[2,64,896]{2,1,0:T(8,128)(2,1)S(1)}, bf16[2,64,896]{2,1,0:T(8,128)(2,1)S(1)}, u32[]{:S(2)}, u32[]{:S(2)}) collective-permute-start(bf16[2,64,896]{2,1,0:T(8,128)(2,1)S(1)} %pad_maximum_fusion.2.refs_4_), channel_id=1, source_target_pairs={{0,32},{16,48},{32,64},{48,80},{64,96},{80,112},{96,0},{112,16},{1... | collective-permute-start | bytes 688136 | tf_op jit(solution)/shard_map/ppermute | solution.py:29
  87.7 38.4 %copy-start.8 = (bf16[2,64,896]{2,1,0:T(8,128)(2,1)}, bf16[2,64,896]{2,1,0:T(8,128)(2,1)S(1)}, u32[]{:S(2)}) copy-start(bf16[2,64,896]{2,1,0:T(8,128)(2,1)S(1)} %collective-permute-done.5.refs_5_) | copy-start | bytes 688132
  87.7 26.1 %collective-permute-start.7 = (bf16[2,64,896]{2,1,0:T(8,128)(2,1)S(1)}, bf16[2,64,896]{2,1,0:T(8,128)(2,1)S(1)}, u32[]{:S(2)}, u32[]{:S(2)}) collective-permute-start(bf16[2,64,896]{2,1,0:T(8,128)(2,1)S(1)} %pad_maximum_fusion.2.refs_4_), channel_id=1, source_target_pairs={{0,48},{16,64},{32,80},{48,96},{64,112},{80,0},{96,16},{112,32},{1... | collective-permute-start | bytes 688136 | tf_op jit(solution)/shard_map/ppermute | solution.py:29
  91.3 76.1 %all-to-all-start.4 = ((f32[32,2,1024]{2,1,0:T(2,128)}), f32[32,2,1024]{2,1,0:T(2,128)S(1)}, u32[]{:S(2)}, u32[]{:S(2)}) async-start(f32[32,2,1024]{2,1,0:T(2,128)} %reshape.51), calls=%async_computation.4 | async-start | bytes 524288 | tf_op jit(solution)/shard_map/all_to_all | solution.py:20
  99.7 26.4 %copy-start.9 = (bf16[2,64,896]{2,1,0:T(8,128)(2,1)}, bf16[2,64,896]{2,1,0:T(8,128)(2,1)S(1)}, u32[]{:S(2)}) copy-start(bf16[2,64,896]{2,1,0:T(8,128)(2,1)S(1)} %collective-permute-done.6.refs_6_) | copy-start | bytes 688132
  99.7 26.2 %collective-permute-start.8 = (bf16[2,64,896]{2,1,0:T(8,128)(2,1)S(1)}, bf16[2,64,896]{2,1,0:T(8,128)(2,1)S(1)}, u32[]{:S(2)}, u32[]{:S(2)}) collective-permute-start(bf16[2,64,896]{2,1,0:T(8,128)(2,1)S(1)} %pad_maximum_fusion.2.refs_4_), channel_id=1, source_target_pairs={{0,64},{16,80},{32,96},{48,112},{64,0},{80,16},{96,32},{112,48},{1... | collective-permute-start | bytes 688136 | tf_op jit(solution)/shard_map/ppermute | solution.py:29
  113.8 12.3 %copy-start.10 = (bf16[2,64,896]{2,1,0:T(8,128)(2,1)}, bf16[2,64,896]{2,1,0:T(8,128)(2,1)S(1)}, u32[]{:S(2)}) copy-start(bf16[2,64,896]{2,1,0:T(8,128)(2,1)S(1)} %collective-permute-done.7.refs_7_) | copy-start | bytes 688132
  113.8 12.2 %collective-permute-start.9 = (bf16[2,64,896]{2,1,0:T(8,128)(2,1)S(1)}, bf16[2,64,896]{2,1,0:T(8,128)(2,1)S(1)}, u32[]{:S(2)}, u32[]{:S(2)}) collective-permute-start(bf16[2,64,896]{2,1,0:T(8,128)(2,1)S(1)} %pad_maximum_fusion.2.refs_4_), channel_id=1, source_target_pairs={{0,80},{16,96},{32,112},{48,0},{64,16},{80,32},{96,48},{112,64},{1... | collective-permute-start | bytes 688136 | tf_op jit(solution)/shard_map/ppermute | solution.py:29
  125.9 0.7 copy-start.11
  126.1 0.7 copy-start.12
  132.8 26.3 %collective-permute-start.12 = (bf16[256,256]{1,0:T(8,128)(2,1)}, bf16[256,256]{1,0:T(8,128)(2,1)S(1)}, u32[]{:S(2)}, u32[]{:S(2)}) collective-permute-start(bf16[256,256]{1,0:T(8,128)(2,1)} %get-tuple-element.12), channel_id=1, source_target_pairs={{0,2},{2,4},{4,6},{6,8},{8,10},{10,12},{12,14},{14,0},{1,3},{3,5},... | collective-permute-start | bytes 393224 | tf_op jit(solution)/shard_map/ppermute | solution.py:29
  142.5 21.8 %collective-permute-start.13 = (bf16[256,256]{1,0:T(8,128)(2,1)}, bf16[256,256]{1,0:T(8,128)(2,1)S(1)}, u32[]{:S(2)}, u32[]{:S(2)}) collective-permute-start(bf16[256,256]{1,0:T(8,128)(2,1)} %get-tuple-element.13), channel_id=1, source_target_pairs={{0,4},{2,6},{4,8},{6,10},{8,12},{10,14},{12,0},{14,2},{1,5},{3,7},... | collective-permute-start | bytes 393224 | tf_op jit(solution)/shard_map/ppermute | solution.py:29
  146.5 31.8 %collective-permute-start.14 = (bf16[256,256]{1,0:T(8,128)(2,1)}, bf16[256,256]{1,0:T(8,128)(2,1)S(1)}, u32[]{:S(2)}, u32[]{:S(2)}) collective-permute-start(bf16[256,256]{1,0:T(8,128)(2,1)} %get-tuple-element.14), channel_id=1, source_target_pairs={{0,6},{2,8},{4,10},{6,12},{8,14},{10,0},{12,2},{14,4},{1,7},{3,9},... | collective-permute-start | bytes 393224 | tf_op jit(solution)/shard_map/ppermute | solution.py:29
  150.8 27.5 %collective-permute-start.15 = (bf16[256,256]{1,0:T(8,128)(2,1)}, bf16[256,256]{1,0:T(8,128)(2,1)S(1)}, u32[]{:S(2)}, u32[]{:S(2)}) collective-permute-start(bf16[256,256]{1,0:T(8,128)(2,1)} %get-tuple-element.15), channel_id=1, source_target_pairs={{0,8},{2,10},{4,12},{6,14},{8,0},{10,2},{12,4},{14,6},{1,9},{3,11}... | collective-permute-start | bytes 393224 | tf_op jit(solution)/shard_map/ppermute | solution.py:29
  154.8 23.5 %collective-permute-start.16 = (bf16[256,256]{1,0:T(8,128)(2,1)}, bf16[256,256]{1,0:T(8,128)(2,1)S(1)}, u32[]{:S(2)}, u32[]{:S(2)}) collective-permute-start(bf16[256,256]{1,0:T(8,128)(2,1)} %get-tuple-element.16), channel_id=1, source_target_pairs={{0,10},{2,12},{4,14},{6,0},{8,2},{10,4},{12,6},{14,8},{1,11},{3,13... | collective-permute-start | bytes 393224 | tf_op jit(solution)/shard_map/ppermute | solution.py:29
  159.1 19.2 %collective-permute-start.17 = (bf16[256,256]{1,0:T(8,128)(2,1)}, bf16[256,256]{1,0:T(8,128)(2,1)S(1)}, u32[]{:S(2)}, u32[]{:S(2)}) collective-permute-start(bf16[256,256]{1,0:T(8,128)(2,1)} %get-tuple-element.17), channel_id=1, source_target_pairs={{0,12},{2,14},{4,0},{6,2},{8,4},{10,6},{12,8},{14,10},{1,13},{3,15... | collective-permute-start | bytes 393224 | tf_op jit(solution)/shard_map/ppermute | solution.py:29
  164.3 15.3 %collective-permute-start.18 = (bf16[256,256]{1,0:T(8,128)(2,1)}, bf16[256,256]{1,0:T(8,128)(2,1)S(1)}, u32[]{:S(2)}, u32[]{:S(2)}) collective-permute-start(bf16[256,256]{1,0:T(8,128)(2,1)} %get-tuple-element.18), channel_id=1, source_target_pairs={{0,14},{2,0},{4,2},{6,4},{8,6},{10,8},{12,10},{14,12},{1,15},{3,1}... | collective-permute-start | bytes 393224 | tf_op jit(solution)/shard_map/ppermute | solution.py:29
  168.3 35.0 %all-to-all-start.5 = ((f32[32,2,1024]{2,1,0:T(2,128)}), f32[32,2,1024]{2,1,0:T(2,128)S(1)}, u32[]{:S(2)}, u32[]{:S(2)}) async-start(f32[32,2,1024]{2,1,0:T(2,128)} %broadcast_in_dim.12), calls=%async_computation.5 | async-start | bytes 524288 | tf_op jit(solution)/shard_map/all_to_all | solution.py:20
  180.8 14.0 %collective-permute-start.19 = (bf16[256,2,64]{0,2,1:T(8,128)(2,1)S(1)}, bf16[256,2,64]{0,2,1:T(8,128)(2,1)S(1)}, u32[]{:S(2)}, u32[]{:S(2)}) collective-permute-start(bf16[256,2,64]{0,2,1:T(8,128)(2,1)S(1)} %get-tuple-element.26), channel_id=1, source_target_pairs={{0,1},{1,0},{2,3},{3,2},{4,129},{5,128},{6,131},{7,130},{8,257},{9... | collective-permute-start | bytes 196616 | tf_op jit(solution)/shard_map/ppermute | solution.py:96
  190.2 12.3 %collective-permute-start.20 = (bf16[256,2,64]{0,2,1:T(8,128)(2,1)S(1)}, bf16[256,2,64]{0,2,1:T(8,128)(2,1)S(1)}, u32[]{:S(2)}, u32[]{:S(2)}) collective-permute-start(bf16[256,2,64]{0,2,1:T(8,128)(2,1)S(1)} %get-tuple-element.27), channel_id=1, source_target_pairs={{0,0},{1,1},{2,2},{3,3},{4,128},{5,129},{6,130},{7,131},{8,256},{9... | collective-permute-start | bytes 196616 | tf_op jit(solution)/shard_map/ppermute | solution.py:95
  194.8 21.0 %slice-start = ((f32[64,384]{1,0:T(8,128)}), f32[64,128]{1,0:T(8,128)S(1)}, s32[]{:S(2)}) async-start(f32[64,384]{1,0:T(8,128)} %copy-done.6), calls=%async_computation.6 | async-start | bytes 65536 | tf_op jit(solution)/shard_map/slice | solution.py:122

commit v2 on v0

v2 whole, which is shorter than its diff:
```python
import functools

import jax
import jax.numpy as jnp
from jax import lax
from jax.experimental import pallas as pl
from jax.experimental.pallas import tpu as pltpu
from jax.sharding import Mesh
from jax.sharding import PartitionSpec as P


DP = ("x", "z")
TENSOR = ("y", "c")
HIGH = lax.Precision.HIGHEST

learn_rate = 0.001


def swap(parts, axis):
    return lax.all_to_all(parts, axis, split_axis=0, concat_axis=0, tiled=True)


def share(x, axis):
    return swap(jnp.broadcast_to(x[None], (lax.axis_size(axis), *x.shape)), axis)


def shifted(x, axis, by):
    length = lax.axis_size(axis)
    return lax.ppermute(x, axis, [(i, (i + by) % length) for i in range(length)])


def block_kernel(n_x, where, *refs):
    grads, weights = refs[:n_x], refs[n_x]
    earlier, parts = refs[n_x + 1 : -1], refs[-1]
    x, side = where[0], where[1]
    _, rows, hidden = weights.shape
    dims = (((1,), (1,)), ((), ()))
    for h in range(2):
        block = weights[pl.ds(4 * h + 2 * side, 2)].reshape(2 * rows, hidden)
        for s in range(n_x):
            total = lax.dot_general(grads[s][...], block, dims, preferred_element_type=jnp.float32)
            place = 2 * lax.rem(x - s + n_x, n_x) + h
            if earlier:
                total += earlier[0][place].astype(jnp.float32)
            parts[place] = total.astype(jnp.bfloat16)


def block_products(side, grads, weights, earlier=()):
    n_x, n_y = lax.axis_size("x"), lax.axis_size("y")
    tokens, rows = grads[0].shape[0], weights.shape[1]
    vmem = pl.BlockSpec(memory_space=pltpu.VMEM)
    where = jnp.stack([lax.axis_index("x"), side]).astype(jnp.int32)
    return pl.pallas_call(
        functools.partial(block_kernel, n_x),
        out_shape=jax.ShapeDtypeStruct((n_y, tokens, 2 * rows), jnp.bfloat16),
        in_specs=[pl.BlockSpec(memory_space=pltpu.SMEM)] + [vmem] * (n_x + 1 + len(earlier)),
        out_specs=vmem,
        name="blocks",
    )(where, *grads, weights, *earlier)


def input_gradient(grad_output, weight):
    n_x, n_y = lax.axis_size("x"), lax.axis_size("y")
    core = lax.axis_index("c")
    weights = lax.all_gather(weight, "z", axis=0)
    grads = [grad_output] + [shifted(grad_output, "x", s) for s in range(1, n_x)]
    give = block_products(1 - core, grads, weights)
    arrived = shifted(give, "c", 1)
    parts = block_products(core, grads, weights, (arrived,))
    summed = lax.psum_scatter(parts, "y", scatter_dimension=0)
    to = []
    for x in range(n_x):
        for y in range(n_y):
            for c in range(2):
                to.append(((x * n_y + y) * 2 + c, ((y // 2) * n_y + 2 * x + y % 2) * 2 + c))
    return lax.ppermute(summed, ("x", "y", "c"), to)


def step(activations, grad_output, weight, start_basis):
    n_d, n_t = lax.axis_size(DP), lax.axis_size(TENSOR)
    tokens, features = activations.shape
    hidden = grad_output.shape[1]
    rows = weight.shape[0]
    rank = start_basis.shape[1]
    few = rank // n_t
    f32 = jnp.float32
    input_grad = input_gradient(grad_output, weight)
    a32, g32 = activations.astype(f32), grad_output.astype(f32)
    mixed = lax.dot_general(start_basis, g32, (((0,), (1,)), ((), ())), precision=HIGH)
    mixed = swap(mixed.reshape(n_t, few, tokens), TENSOR)
    mixed = mixed.sum(axis=0)
    left_part = jnp.dot(mixed, a32, precision=HIGH)
    left_part = jnp.swapaxes(left_part.reshape(few, n_d, rows), 0, 1)
    left_mine = swap(left_part, DP)
    left_mine = left_mine.sum(axis=0)
    left_few = jnp.swapaxes(share(left_mine, DP), 0, 1).reshape(few, features)
    seen = lax.dot_general(left_few, a32, (((1,), (1,)), ((), ())), precision=HIGH)
    both = share(jnp.concatenate([seen, left_mine], axis=1), TENSOR).reshape(rank, tokens + rows)
    seen, left_rows = both[:, :tokens], both[:, tokens:]
    right_part = jnp.dot(seen, g32, precision=HIGH)
    gram_part = lax.dot_general(left_rows, left_rows, (((1,), (1,)), ((), ())), precision=HIGH)
    pad = jnp.zeros((rank, 128 - rank), f32)
    packed = jnp.concatenate([right_part, gram_part, pad], axis=1).reshape(n_d, rank // n_d, -1)
    packed = share(swap(packed, DP).sum(axis=0), DP).reshape(rank, -1)
    right, gram_matrix = packed[:, :hidden], packed[:, hidden : hidden + rank]
    lower = jnp.linalg.cholesky(gram_matrix)
    solved = jax.scipy.linalg.solve_triangular(
        lower, jnp.concatenate([right, left_rows], axis=1), lower=True
    )
    right, basis_rows = solved[:, :hidden], solved[:, hidden:]
    right_basis = right.T / jnp.sqrt(f32(tokens * n_d))
    update = lax.dot_general(basis_rows, right, (((0,), (0,)), ((), ())), precision=HIGH)
    new_weight = weight.astype(f32) - learn_rate * update
    return (input_grad, right_basis, new_weight)


def solution(mesh):
    finer = Mesh(mesh.devices.reshape(4, 8, 8, 2), ("x", "z", "y", "c"))
    in_specs = (P(DP, None), P(DP, TENSOR), P(DP, TENSOR), P(TENSOR, None))
    out_specs = (P(DP, TENSOR), P(TENSOR, None), P(DP, TENSOR))
    return jax.shard_map(step, mesh=finer, in_specs=in_specs, out_specs=out_specs, check_vma=False)
```

time: 257 us -> 163 us (0.63)
  the two profiles are of different devices: /device:TPU:96 before, /device:TPU:78 now
where the time goes in v2:
time: 163 us; the launch traced here: 162 us
  starting transfers between devices  45.5 us (28%)
  blocking collectives  34.3 us (21%)
  waiting for transfers between devices  29.3 us (18%)
  between operations  14.3 us (9%)
  other arithmetic  14.2 us (9%)
  Pallas kernels  9.08 us (6%)
  local copies, waits for them, and re-layouts  8.29 us (5%)
  matrix products  7.28 us (4%)
    all_to_all x2, blocking collectives, swap(): return lax.all_to_all(parts, axis, split_axis=0, concat_axis=0, tiled=True)  34.3 us
    all_to_all x4, starting transfers between devices, swap(): return lax.all_to_all(parts, axis, split_axis=0, concat_axis=0, tiled=True)  30.9 us
    all_to_all x4, waiting for transfers between devices, swap(): return lax.all_to_all(parts, axis, split_axis=0, concat_axis=0, tiled=True)  16.6 us
    ppermute x1, waiting for transfers between devices, input_gradient(): return lax.ppermute(summed, ('x', 'y', 'c'), to)  10.8 us
    ppermute x4, starting transfers between devices, shifted(): lax.ppermute(x, axis, [(i, (i + by) % length) for i in range(length)])  10.7 us
    pallas_call x2, Pallas kernels, block_products(): pl.pallas_call(functools.partial(block_kernel, n_x), out_shape=jax.ShapeD...  9.08 us
    another operation x3, other arithmetic, step(): lower = jnp.linalg.cholesky(gram_matrix)  6.52 us
    another operation x2, other arithmetic, step(): jax.scipy.linalg.solve_triangular(lower, jnp.concatenate([right, left_row...  5.55 us
  transfers between devices with their start and end apart: 11, of which 4 were waited for; matrix products, arithmetic and copies ran while one was open for 17% of the time, Pallas kernels for 6%

profile of v2, /device:TPU:78, one launch (start us, length us, event | category | flops | bytes accessed | tf_op | source)
XLA Modules:
  0.0 162.3 jit_solution(9218764390575942844)
XLA Ops:
  7.2 0.0 copy-start
  7.2 0.0 all-gather.3.cloned.1.call-start
  7.2 0.7 all-gather.3.cloned.1.call-update
  7.9 0.2 copy-done
  8.1 1.5 fusion.18
  9.7 0.7 reshape.36
  10.3 7.6 %all-to-all-start = ((f32[16,4,256]{2,1,0:T(4,128)}), f32[16,4,256]{2,1,0:T(4,128)S(1)}, u32[]{:S(2)}, u32[]{:S(2)}) async-start(f32[16,4,256]{2,1,0:T(4,128)} %reshape.36), calls=%async_computation.1 | async-start | bytes 131072 | tf_op jit(solution)/shard_map/all_to_all | solution.py:20
  17.9 2.4 %collective-permute-start = (bf16[256,896]{1,0:T(8,128)(2,1)}, bf16[256,896]{1,0:T(8,128)(2,1)S(1)}, u32[]{:S(2)}, u32[]{:S(2)}) collective-permute-start(bf16[256,896]{1,0:T(8,128)(2,1)} %refs_0_.3), channel_id=1, source_target_pairs={{0,128},{128,256},{256,384},{384,0},{1,129},{129,257},{257,385},{3... | collective-permute-start | bytes 1376264 | tf_op jit(solution)/shard_map/ppermute | solution.py:29
  20.3 4.3 %collective-permute-start.1 = (bf16[256,896]{1,0:T(8,128)(2,1)}, bf16[256,896]{1,0:T(8,128)(2,1)S(1)}, u32[]{:S(2)}, u32[]{:S(2)}) collective-permute-start(bf16[256,896]{1,0:T(8,128)(2,1)} %refs_0_.3), channel_id=1, source_target_pairs={{0,256},{128,384},{256,0},{384,128},{1,257},{129,385},{257,1},{385... | collective-permute-start | bytes 1376264 | tf_op jit(solution)/shard_map/ppermute | solution.py:29
  24.6 1.9 %collective-permute-start.2 = (bf16[256,896]{1,0:T(8,128)(2,1)}, bf16[256,896]{1,0:T(8,128)(2,1)}, u32[]{:S(2)}, u32[]{:S(2)}) collective-permute-start(bf16[256,896]{1,0:T(8,128)(2,1)} %refs_0_.3), channel_id=1, source_target_pairs={{0,384},{128,0},{256,128},{384,256},{1,385},{129,1},{257,129},{385... | collective-permute-start | bytes 1376264 | tf_op jit(solution)/shard_map/ppermute | solution.py:29
  26.5 3.3 %copy.13 = bf16[4096,256]{1,0:T(8,128)(2,1)S(1)} copy(bf16[4096,256]{0,1:T(8,128)(2,1)} %bitcast.33) | data formatting | bytes 4194304 | tf_op jit(solution)/shard_map/dot_general | solution.py:92
  29.8 0.0 all-to-all-done
  29.8 1.7 %convolution_bitcast_fusion = f32[32,4,128]{2,1,0:T(4,128)S(1)} fusion(bf16[32,128,256]{2,1,0:T(8,128)(2,1)S(1)} %bitcast.34, f32[4,256]{1,0:T(4,128)S(1)} %reduce_sum.27), kind=kOutput, calls=%fused_computation.2 | convolution fusion | flops 50331648 | bytes 2166784 | tf_op jit(solution)/shard_map/dot_general | solution.py:92
  31.6 20.4 %all_to_all.30 = f32[32,4,128]{2,1,0:T(4,128)S(1)} all-to-all(f32[32,4,128]{2,1,0:T(4,128)S(1)} %convolution_bitcast_fusion), channel_id=1, replica_groups=mesh['x'=4,'z'=8,'y'=8,'c'=2] {'x','z'}, dimensions={0} | all-to-all | bytes 131072 | tf_op jit(solution)/shard_map/all_to_all | solution.py:20
  52.0 0.6 broadcast_in_dim.9
  52.7 7.4 %all-to-all-start.2 = ((f32[32,4,128]{2,1,0:T(4,128)}), f32[32,4,128]{2,1,0:T(4,128)S(1)}, u32[]{:S(2)}, u32[]{:S(2)}) async-start(f32[32,4,128]{2,1,0:T(4,128)} %broadcast_in_dim.9), calls=%async_computation.3 | async-start | bytes 131072 | tf_op jit(solution)/shard_map/all_to_all | solution.py:20
  60.1 0.6 pad_add_fusion.1.where
  60.7 0.0 collective-permute-done.refs_1_
  60.7 0.0 copy-start.3
  60.7 0.0 collective-permute-done.1.refs_2_
  60.7 0.0 copy-start.4
  60.7 0.0 collective-permute-done.2.refs_3_
  60.7 0.0 all-gather.3.cloned.1.call-done
  60.8 0.7 copy-done.3
  61.5 0.2 copy-done.4
  61.6 0.0 copy-start.1
  61.6 4.5 %blocks.2 = bf16[8,256,256]{2,1,0:T(8,128)(2,1)} custom-call(s32[2]{0:T(128)} %pad_add_fusion.1.where, bf16[256,896]{1,0:T(8,128)(2,1)} %refs_0_.3, bf16[256,896]{1,0:T(8,128)(2,1)} %copy-done.3, bf16[256,896]{1,0:T(8,128)(2,1)} %copy-done.4, bf16[256,896]{1,0:T(8,128)(2,1)} %collective-permute-done.2.refs_3_, bf16[8,128,896]{2,1,0:T(8,128)(2,1)} %bitcast.35), custom_call_target="tpu_custom_call" | custom-call | tf_op jit(solution)/shard_map/blocks/pallas_call | solution.py:53
  66.1 0.0 copy-start.2
  66.1 2.0 %collective-permute-start.3 = (bf16[8,256,256]{2,1,0:T(8,128)(2,1)}, bf16[8,256,256]{2,1,0:T(8,128)(2,1)}, u32[]{:S(2)}, u32[]{:S(2)}) collective-permute-start(bf16[8,256,256]{2,1,0:T(8,128)(2,1)} %blocks.2), channel_id=1, source_target_pairs={{0,1},{1,0},{2,3},{3,2},{4,5},{5,4},{6,7},{7,6},{8,9},{9,8},{10,11... | collective-permute-start | bytes 3145736 | tf_op jit(solution)/shard_map/ppermute | solution.py:29
  68.1 0.0 all-to-all-done.2
  68.2 0.0 copy-done.1
  68.2 1.7 %fusion.8 = f32[4,256]{1,0:T(4,128)S(1)} fusion(bf16[256,4096]{1,0:T(8,128)(2,1)S(1)} %copy-done.1, f32[32,4,128]{2,1,0:T(4,128)S(1)} %all-to-all-done.2), kind=kOutput, calls=%fused_computation.12 | convolution fusion | flops 50331648 | bytes 2166784 | tf_op jit(solution)/shard_map/dot_general | solution.py:97
  69.9 13.9 %all_to_all.31 = f32[16,4,384]{2,1,0:T(4,128)S(1)} all-to-all(f32[16,4,384]{2,1,0:T(4,128)S(1)} %broadcast_in_dim.10), channel_id=1, replica_groups=mesh['x'=4,'z'=8,'y'=8,'c'=2] {'y','c'}, dimensions={0} | all-to-all | bytes 196608 | tf_op jit(solution)/shard_map/all_to_all | solution.py:20
  83.9 0.2 fusion.16
  84.0 0.0 copy-done.2
  84.1 0.3 fusion.6
  84.4 0.1 pad_maximum_fusion
  84.5 0.9 reshape.39
  85.4 9.8 %all-to-all-start.4 = ((f32[32,2,1024]{2,1,0:T(2,128)}), f32[32,2,1024]{2,1,0:T(2,128)S(1)}, u32[]{:S(2)}, u32[]{:S(2)}) async-start(f32[32,2,1024]{2,1,0:T(2,128)} %reshape.39), calls=%async_computation.5 | async-start | bytes 524288 | tf_op jit(solution)/shard_map/all_to_all | solution.py:20
  95.2 0.0 reduce-scatter.2.cloned.1.call-start
  95.2 0.6 pad_add_fusion.where
  95.8 0.0 collective-permute-done.3.refs_5_
  95.8 4.6 %blocks.3 = bf16[8,256,256]{2,1,0:T(8,128)(2,1)} custom-call(s32[2]{0:T(128)} %pad_add_fusion.where, bf16[256,896]{1,0:T(8,128)(2,1)} %refs_0_.3, bf16[256,896]{1,0:T(8,128)(2,1)} %copy-done.3, bf16[256,896]{1,0:T(8,128)(2,1)} %copy-done.4, bf16[256,896]{1,0:T(8,128)(2,1)} %collective-permute-done.2.refs_3_, bf16[8,128,896]{2,1,0:T(8,128)(2,1)} %bitcast.36, ...), custom_call_target="tpu_custom_call" | custom-call | tf_op jit(solution)/shard_map/blocks/pallas_call | solution.py:53
  100.4 0.0 copy-start.5
  100.4 0.0 reduce-scatter.2.cloned.1.call-update
  100.4 6.1 %all-to-all-done.4 = f32[32,2,1024]{2,1,0:T(2,128)S(1)} async-done(((f32[32,2,1024]{2,1,0:T(2,128)}), f32[32,2,1024]{2,1,0:T(2,128)S(1)}, u32[]{:S(2)}, u32[]{:S(2)}) %all-to-all-start.4) | async-done | bytes 262176 | tf_op jit(solution)/shard_map/all_to_all | solution.py:20
  106.5 0.1 reduce_sum.29
  106.6 0.8 broadcast_in_dim.12
  107.4 6.1 %all-to-all-start.5 = ((f32[32,2,1024]{2,1,0:T(2,128)}), f32[32,2,1024]{2,1,0:T(2,128)S(1)}, u32[]{:S(2)}, u32[]{:S(2)}) async-start(f32[32,2,1024]{2,1,0:T(2,128)} %broadcast_in_dim.12), calls=%async_computation.6 | async-start | bytes 524288 | tf_op jit(solution)/shard_map/all_to_all | solution.py:20
  113.6 10.5 %all-to-all-done.5 = f32[32,2,1024]{2,1,0:T(2,128)S(1)} async-done(((f32[32,2,1024]{2,1,0:T(2,128)}), f32[32,2,1024]{2,1,0:T(2,128)S(1)}, u32[]{:S(2)}, u32[]{:S(2)}) %all-to-all-start.5) | async-done | bytes 262176 | tf_op jit(solution)/shard_map/all_to_all | solution.py:20
  124.1 0.2 reshape.40
  124.3 0.1 copy.14
  124.4 5.8 %cholesky.15 = f32[64,64]{1,0:T(8,128)S(1)} custom-call(f32[64,64]{1,0:T(8,128)S(1)} %fusion.13), custom_call_target="Cholesky" | custom-call | tf_op jit(solution)/shard_map/jit(cholesky)/cholesky | solution.py:106
  130.3 0.6 compare_reduce_fusion
  130.9 0.7 fusion.10
  131.6 4.9 %custom-call.7 = f32[1,64,64]{1,2,0:T(8,128)S(1)} custom-call(f32[1,64,64]{2,1,0:T(8,128)S(1)} %fusion.10), custom_call_target="InvertDiagBlocksLowerTriangular" | custom-call | tf_op jit(solution)/shard_map/jit(_solve_triangular)/triangular_solve | solution.py:107
  136.5 0.4 fusion.1
  136.9 0.0 copy-done.5
  136.9 1.4 fusion
  138.3 1.1 reduce-scatter.2.cloned.1.call-done
  139.4 3.9 %collective-permute-start.4 = (bf16[256,256]{1,0:T(8,128)(2,1)}, bf16[256,256]{1,0:T(8,128)(2,1)S(1)}, u32[]{:S(2)}, u32[]{:S(2)}) collective-permute-start(bf16[256,256]{1,0:T(8,128)(2,1)} %bitcast.37), channel_id=1, source_target_pairs={{0,0},{1,1},{2,2},{3,3},{4,128},{5,129},{6,130},{7,131},{8,256},{9... | collective-permute-start | bytes 393224 | tf_op jit(solution)/shard_map/ppermute | solution.py:76
  143.2 0.7 multiply_bitcast_fusion
  143.9 10.8 %collective-permute-done.4 = bf16[256,256]{1,0:T(8,128)(2,1)S(1)} collective-permute-done((bf16[256,256]{1,0:T(8,128)(2,1)}, bf16[256,256]{1,0:T(8,128)(2,1)S(1)}, u32[]{:S(2)}, u32[]{:S(2)}) %collective-permute-start.4) | collective-permute-done | bytes 131104 | tf_op jit(solution)/shard_map/ppermute | solution.py:76
  154.8 0.7 copy.16
  (11 shorter events, 0.2 us)
Async XLA Ops:
  7.2 0.9 copy-start
  7.2 53.6 %all-gather.3.cloned.1.call-start = ((), (), s32[]{:S(2)}) async-start(), calls=%async_computation.8 | async-start | bytes 2064384 | tf_op jit(solution)/shard_map/all_gather | solution.py:65
  10.3 19.5 %all-to-all-start = ((f32[16,4,256]{2,1,0:T(4,128)}), f32[16,4,256]{2,1,0:T(4,128)S(1)}, u32[]{:S(2)}, u32[]{:S(2)}) async-start(f32[16,4,256]{2,1,0:T(4,128)} %reshape.36), calls=%async_computation.1 | async-start | bytes 131072 | tf_op jit(solution)/shard_map/all_to_all | solution.py:20
  17.9 42.8 %collective-permute-start = (bf16[256,896]{1,0:T(8,128)(2,1)}, bf16[256,896]{1,0:T(8,128)(2,1)S(1)}, u32[]{:S(2)}, u32[]{:S(2)}) collective-permute-start(bf16[256,896]{1,0:T(8,128)(2,1)} %refs_0_.3), channel_id=1, source_target_pairs={{0,128},{128,256},{256,384},{384,0},{1,129},{129,257},{257,385},{3... | collective-permute-start | bytes 1376264 | tf_op jit(solution)/shard_map/ppermute | solution.py:29
  20.3 40.4 %collective-permute-start.1 = (bf16[256,896]{1,0:T(8,128)(2,1)}, bf16[256,896]{1,0:T(8,128)(2,1)S(1)}, u32[]{:S(2)}, u32[]{:S(2)}) collective-permute-start(bf16[256,896]{1,0:T(8,128)(2,1)} %refs_0_.3), channel_id=1, source_target_pairs={{0,256},{128,384},{256,0},{384,128},{1,257},{129,385},{257,1},{385... | collective-permute-start | bytes 1376264 | tf_op jit(solution)/shard_map/ppermute | solution.py:29
  24.6 36.1 %collective-permute-start.2 = (bf16[256,896]{1,0:T(8,128)(2,1)}, bf16[256,896]{1,0:T(8,128)(2,1)}, u32[]{:S(2)}, u32[]{:S(2)}) collective-permute-start(bf16[256,896]{1,0:T(8,128)(2,1)} %refs_0_.3), channel_id=1, source_target_pairs={{0,384},{128,0},{256,128},{384,256},{1,385},{129,1},{257,129},{385... | collective-permute-start | bytes 1376264 | tf_op jit(solution)/shard_map/ppermute | solution.py:29
  52.7 15.5 %all-to-all-start.2 = ((f32[32,4,128]{2,1,0:T(4,128)}), f32[32,4,128]{2,1,0:T(4,128)S(1)}, u32[]{:S(2)}, u32[]{:S(2)}) async-start(f32[32,4,128]{2,1,0:T(4,128)} %broadcast_in_dim.9), calls=%async_computation.3 | async-start | bytes 131072 | tf_op jit(solution)/shard_map/all_to_all | solution.py:20
  60.7 0.8 copy-start.3
  60.7 0.9 copy-start.4
  61.6 6.5 %copy-start.1 = (bf16[256,4096]{1,0:T(8,128)(2,1)S(1)}, bf16[256,4096]{1,0:T(8,128)(2,1)}, u32[]{:S(2)}) copy-start(bf16[256,4096]{1,0:T(8,128)(2,1)} %param.4) | copy-start | bytes 6291460
  66.1 18.0 %copy-start.2 = (bf16[256,896]{1,0:T(8,128)(2,1)S(1)}, bf16[256,896]{1,0:T(8,128)(2,1)}, u32[]{:S(2)}) copy-start(bf16[256,896]{1,0:T(8,128)(2,1)} %refs_0_.3) | copy-start | bytes 1376260
  66.1 29.7 %collective-permute-start.3 = (bf16[8,256,256]{2,1,0:T(8,128)(2,1)}, bf16[8,256,256]{2,1,0:T(8,128)(2,1)}, u32[]{:S(2)}, u32[]{:S(2)}) collective-permute-start(bf16[8,256,256]{2,1,0:T(8,128)(2,1)} %blocks.2), channel_id=1, source_target_pairs={{0,1},{1,0},{2,3},{3,2},{4,5},{5,4},{6,7},{7,6},{8,9},{9,8},{10,11... | collective-permute-start | bytes 3145736 | tf_op jit(solution)/shard_map/ppermute | solution.py:29
  85.4 21.2 %all-to-all-start.4 = ((f32[32,2,1024]{2,1,0:T(2,128)}), f32[32,2,1024]{2,1,0:T(2,128)S(1)}, u32[]{:S(2)}, u32[]{:S(2)}) async-start(f32[32,2,1024]{2,1,0:T(2,128)} %reshape.39), calls=%async_computation.5 | async-start | bytes 524288 | tf_op jit(solution)/shard_map/all_to_all | solution.py:20
  95.2 44.2 %reduce-scatter.2.cloned.1.call-start = ((), (), s32[]{:S(2)}) async-start(), calls=%async_computation.7 | async-start | bytes 1179648 | tf_op jit(solution)/shard_map/reduce_scatter | solution.py:70
  100.4 36.5 %copy-start.5 = (bf16[128,896]{1,0:T(8,128)(2,1)S(1)}, bf16[128,896]{1,0:T(8,128)(2,1)}, u32[]{:S(2)}) copy-start(bf16[128,896]{1,0:T(8,128)(2,1)} %param.6) | copy-start | bytes 688132
  107.4 16.7 %all-to-all-start.5 = ((f32[32,2,1024]{2,1,0:T(2,128)}), f32[32,2,1024]{2,1,0:T(2,128)S(1)}, u32[]{:S(2)}, u32[]{:S(2)}) async-start(f32[32,2,1024]{2,1,0:T(2,128)} %broadcast_in_dim.12), calls=%async_computation.6 | async-start | bytes 524288 | tf_op jit(solution)/shard_map/all_to_all | solution.py:20
  139.4 15.4 %collective-permute-start.4 = (bf16[256,256]{1,0:T(8,128)(2,1)}, bf16[256,256]{1,0:T(8,128)(2,1)S(1)}, u32[]{:S(2)}, u32[]{:S(2)}) collective-permute-start(bf16[256,256]{1,0:T(8,128)(2,1)} %bitcast.37), channel_id=1, source_target_pairs={{0,0},{1,1},{2,2},{3,3},{4,128},{5,129},{6,130},{7,131},{8,256},{9... | collective-permute-start | bytes 393224 | tf_op jit(solution)/shard_map/ppermute | solution.py:76
Sparse Core Ops, SparseCore 0:
  10.1 47.6 all-gather.2
  100.6 38.7 reduce-scatter.1

commit v3 on v2

--- a/solution.py
+++ b/solution.py
@@ -76,42 +76,127 @@
     return lax.ppermute(summed, ("x", "y", "c"), to)
 
 
+def thirds(value):
+    first = value.astype(jnp.bfloat16)
+    rest = value - first.astype(jnp.float32)
+    second = rest.astype(jnp.bfloat16)
+    third = (rest - second.astype(jnp.float32)).astype(jnp.bfloat16)
+    return first, second, third
+
+
+def exact_dot(value, other, dims):
+    dot = functools.partial(lax.dot_general, dimension_numbers=(dims, ((), ())), preferred_element_type=jnp.float32)
+    count = value.shape[0]
+    parts = dot(jnp.concatenate(thirds(value), axis=0), other)
+    return (parts[2 * count :] + parts[count : 2 * count]) + parts[:count]
+
+
+def mixed_kernel(basis, grads, out):
+    mixed = exact_dot(basis[...], grads[...], ((1,), (1,)))
+    few = out.shape[1]
+    for t in range(out.shape[0]):
+        out[t] = mixed[t * few : (t + 1) * few]
+
+
+def left_kernel(arrived, activations, out, lines):
+    few = arrived.shape[1]
+    mixed = arrived[0]
+    for t in range(1, arrived.shape[0]):
+        mixed += arrived[t]
+    for i, part in enumerate(thirds(mixed)):
+        lines[i * few : (i + 1) * few] = part.astype(jnp.float32)
+    dot = jnp.dot(lines[: 3 * few].astype(jnp.bfloat16), activations[...], preferred_element_type=jnp.float32)
+    total = (dot[2 * few :] + dot[few : 2 * few]) + dot[:few]
+    rows = out.shape[2]
+    for d in range(out.shape[0]):
+        out[d] = total[:, d * rows : (d + 1) * rows]
+
+
+def right_kernel(both, grads, out):
+    tokens, hidden = grads.shape
+    rank = both.shape[0]
+    right = exact_dot(both[:, :tokens], grads[...], ((1,), (0,)))
+    rows = both[:, tokens:]
+    gram = lax.dot_general(rows, rows, (((1,), (1,)), ((), ())), precision=HIGH, preferred_element_type=jnp.float32)
+    few = out.shape[1]
+    for d in range(out.shape[0]):
+        out[d, :, :hidden] = right[d * few : (d + 1) * few]
+        out[d, :, hidden : hidden + rank] = gram[d * few : (d + 1) * few]
+        out[d, :, hidden + rank :] = jnp.zeros((few, out.shape[2] - hidden - rank), jnp.float32)
+
+
+def last_kernel(token_total, packed, left_rows, weight, right_basis, new_weight):
+    rank = packed.shape[0]
+    hidden = weight.shape[1]
+    row = lax.broadcasted_iota(jnp.int32, (8, 2 * rank), 0)
+    lane = lax.broadcasted_iota(jnp.int32, (8, 2 * rank), 1)
+    blocks = []
+    for j in range(rank // 8):
+        gram = packed[8 * j : 8 * j + 8, hidden : hidden + 2 * rank]
+        blocks.append(jnp.where(lane < rank, gram, jnp.where(lane - rank == row + 8 * j, 1.0, 0.0)))
+    for k in range(rank):
+        b, i = divmod(k, 8)
+        pivot = blocks[b][i : i + 1]
+        scaled = pivot / pivot[:, k : k + 1]
+        for j in range(b, rank // 8):
+            factor = blocks[j][:, k : k + 1]
+            if j == b:
+                factor = jnp.where(row[:, :1] > i, factor, 0.0)
+            blocks[j] = blocks[j] - factor * scaled
+    inverse = []
+    for j, block in enumerate(blocks):
+        pivots = jnp.sum(jnp.where(lane == row + 8 * j, block, 0.0), axis=1, keepdims=True)
+        inverse.append(block / jnp.sqrt(pivots))
+    inverse = jnp.concatenate(inverse, axis=0)[:, rank:]
+    dot = functools.partial(jnp.dot, precision=HIGH, preferred_element_type=jnp.float32)
+    right = dot(inverse, packed[:, :hidden])
+    basis = dot(inverse, left_rows[...])
+    right_basis[...] = right / jnp.sqrt(jnp.float32(token_total))
+    new_weight[...] = weight[...].astype(jnp.float32) - learn_rate * dot(basis.T, right)
+
+
+def run(kernel, shapes, *args, scratch=()):
+    vmem = pl.BlockSpec(memory_space=pltpu.VMEM)
+    several = isinstance(shapes[0], tuple)
+    outs = [jax.ShapeDtypeStruct(s, jnp.float32) for s in (shapes if several else (shapes,))]
+    return pl.pallas_call(
+        kernel,
+        out_shape=outs if several else outs[0],
+        in_specs=[vmem] * len(args),
+        out_specs=[vmem] * len(outs) if several else vmem,
+        scratch_shapes=scratch,
+    )(*args)
+
+
 def step(activations, grad_output, weight, start_basis):
     n_d, n_t = lax.axis_size(DP), lax.axis_size(TENSOR)
     tokens, features = activations.shape
-    hidden = grad_output.shape[1]
-    rows = weight.shape[0]
+    rows, hidden = weight.shape
     rank = start_basis.shape[1]
     few = rank // n_t
     f32 = jnp.float32
     input_grad = input_gradient(grad_output, weight)
-    a32, g32 = activations.astype(f32), grad_output.astype(f32)
-    mixed = lax.dot_general(start_basis, g32, (((0,), (1,)), ((), ())), precision=HIGH)
-    mixed = swap(mixed.reshape(n_t, few, tokens), TENSOR)
-    mixed = mixed.sum(axis=0)
-    left_part = jnp.dot(mixed, a32, precision=HIGH)
-    left_part = jnp.swapaxes(left_part.reshape(few, n_d, rows), 0, 1)
+    mixed = run(mixed_kernel, (n_t, few, tokens), start_basis.T, grad_output)
+    mixed = swap(mixed, TENSOR)
+    left_part = run(left_kernel, (n_d, few, rows), mixed, activations, scratch=[pltpu.VMEM((16, tokens), f32)])
     left_mine = swap(left_part, DP)
     left_mine = left_mine.sum(axis=0)
-    left_few = jnp.swapaxes(share(left_mine, DP), 0, 1).reshape(few, features)
+    left_few = share(left_mine, DP)
+    left_few = jnp.swapaxes(left_few, 0, 1).reshape(few, features)
+    a32 = activations.astype(f32)
     seen = lax.dot_general(left_few, a32, (((1,), (1,)), ((), ())), precision=HIGH)
-    both = share(jnp.concatenate([seen, left_mine], axis=1), TENSOR).reshape(rank, tokens + rows)
-    seen, left_rows = both[:, :tokens], both[:, tokens:]
-    right_part = jnp.dot(seen, g32, precision=HIGH)
-    gram_part = lax.dot_general(left_rows, left_rows, (((1,), (1,)), ((), ())), precision=HIGH)
-    pad = jnp.zeros((rank, 128 - rank), f32)
-    packed = jnp.concatenate([right_part, gram_part, pad], axis=1).reshape(n_d, rank // n_d, -1)
-    packed = share(swap(packed, DP).sum(axis=0), DP).reshape(rank, -1)
-    right, gram_matrix = packed[:, :hidden], packed[:, hidden : hidden + rank]
-    lower = jnp.linalg.cholesky(gram_matrix)
-    solved = jax.scipy.linalg.solve_triangular(
-        lower, jnp.concatenate([right, left_rows], axis=1), lower=True
+    both = share(jnp.concatenate([seen, left_mine], axis=1), TENSOR)
+    both = both.reshape(rank, tokens + rows)
+    width = hidden + 128
+    packed = run(right_kernel, (n_d, rank // n_d, width), both, grad_output)
+    packed = swap(packed, DP)
+    packed = packed.sum(axis=0)
+    packed = share(packed, DP)
+    packed = packed.reshape(rank, width)
+    right_basis, new_weight = run(
+        functools.partial(last_kernel, tokens * n_d), ((rank, hidden), (rows, hidden)), packed, both[:, tokens:], weight
     )
-    right, basis_rows = solved[:, :hidden], solved[:, hidden:]
-    right_basis = right.T / jnp.sqrt(f32(tokens * n_d))
-    update = lax.dot_general(basis_rows, right, (((0,), (0,)), ((), ())), precision=HIGH)
-    new_weight = weight.astype(f32) - learn_rate * update
-    return (input_grad, right_basis, new_weight)
+    return (input_grad, right_basis.T, new_weight)
 
 
 def solution(mesh):

time: 163 us -> 190 us (1.17)
  the two profiles are of different devices: /device:TPU:78 before, /device:TPU:64 now
where the time goes in v3:
time: 190 us; the launch traced here: 189 us
  blocking collectives  73.3 us (39%)
  waiting for transfers between devices  49.6 us (26%)
  Pallas kernels  24.2 us (13%)
  starting transfers between devices  19.7 us (10%)
  between operations  14.1 us (7%)
  local copies, waits for them, and re-layouts  5.39 us (3%)
    all_to_all x5, blocking collectives, swap(): return lax.all_to_all(parts, axis, split_axis=0, concat_axis=0, tiled=True)  73.3 us
    all_gather x1, waiting for transfers between devices, input_gradient(): weights = lax.all_gather(weight, 'z', axis=0)  21.4 us
    ppermute x4, waiting for transfers between devices, shifted(): lax.ppermute(x, axis, [(i, (i + by) % length) for i in range(length)])  18.1 us
    pallas_call x4, Pallas kernels, run(): pl.pallas_call(kernel, out_shape=outs if several else outs[0], in_specs=[...  15.2 us
    ppermute x4, starting transfers between devices, shifted(): lax.ppermute(x, axis, [(i, (i + by) % length) for i in range(length)])  13.3 us
    all_to_all x1, waiting for transfers between devices, swap(): return lax.all_to_all(parts, axis, split_axis=0, concat_axis=0, tiled=True)  9.34 us
    pallas_call x2, Pallas kernels, block_products(): pl.pallas_call(functools.partial(block_kernel, n_x), out_shape=jax.ShapeD...  8.95 us
    all_to_all x1, starting transfers between devices, swap(): return lax.all_to_all(parts, axis, split_axis=0, concat_axis=0, tiled=True)  4.72 us
  transfers between devices with their start and end apart: 8, of which 6 were waited for; matrix products, arithmetic and copies ran while one was open for 4% of the time, Pallas kernels for 8%

profile of v3, /device:TPU:64, one launch (start us, length us, event | category | flops | bytes accessed | tf_op | source)
XLA Modules:
  0.0 189.3 jit_solution(15394427796993549341)
XLA Ops:
  7.2 0.0 all-gather.3.cloned.1.call-start
  7.2 0.7 all-gather.3.cloned.1.call-update
  7.9 0.0 reduce-scatter.2.cloned.1.call-start
  7.9 3.4 %collective-permute-start = (bf16[256,896]{1,0:T(8,128)(2,1)}, bf16[256,896]{1,0:T(8,128)(2,1)S(1)}, u32[]{:S(2)}, u32[]{:S(2)}) collective-permute-start(bf16[256,896]{1,0:T(8,128)(2,1)} %grads.3), channel_id=1, source_target_pairs={{0,128},{128,256},{256,384},{384,0},{1,129},{129,257},{257,385},{3... | collective-permute-start | bytes 1376264 | tf_op jit(solution)/shard_map/ppermute | solution.py:29
  11.4 4.6 %collective-permute-start.1 = (bf16[256,896]{1,0:T(8,128)(2,1)}, bf16[256,896]{1,0:T(8,128)(2,1)S(1)}, u32[]{:S(2)}, u32[]{:S(2)}) collective-permute-start(bf16[256,896]{1,0:T(8,128)(2,1)} %grads.3), channel_id=1, source_target_pairs={{0,256},{128,384},{256,0},{384,128},{1,257},{129,385},{257,1},{385... | collective-permute-start | bytes 1376264 | tf_op jit(solution)/shard_map/ppermute | solution.py:29
  16.0 3.3 %collective-permute-start.2 = (bf16[256,896]{1,0:T(8,128)(2,1)}, bf16[256,896]{1,0:T(8,128)(2,1)S(1)}, u32[]{:S(2)}, u32[]{:S(2)}) collective-permute-start(bf16[256,896]{1,0:T(8,128)(2,1)} %grads.3), channel_id=1, source_target_pairs={{0,384},{128,0},{256,128},{384,256},{1,385},{129,1},{257,129},{385... | collective-permute-start | bytes 1376264 | tf_op jit(solution)/shard_map/ppermute | solution.py:29
  19.4 0.7 pad_add_fusion.1.where
  20.0 3.6 %collective-permute-done.refs_1_ = bf16[256,896]{1,0:T(8,128)(2,1)S(1)} collective-permute-done((bf16[256,896]{1,0:T(8,128)(2,1)}, bf16[256,896]{1,0:T(8,128)(2,1)S(1)}, u32[]{:S(2)}, u32[]{:S(2)}) %collective-permute-start) | collective-permute-done | bytes 458784 | tf_op jit(solution)/shard_map/ppermute | solution.py:29
  23.7 0.0 copy-start.1
  23.7 10.7 %collective-permute-done.1.refs_2_ = bf16[256,896]{1,0:T(8,128)(2,1)S(1)} collective-permute-done((bf16[256,896]{1,0:T(8,128)(2,1)}, bf16[256,896]{1,0:T(8,128)(2,1)S(1)}, u32[]{:S(2)}, u32[]{:S(2)}) %collective-permute-start.1) | collective-permute-done | bytes 458784 | tf_op jit(solution)/shard_map/ppermute | solution.py:29
  34.3 0.0 copy-start.2
  34.3 1.6 collective-permute-done.2.refs_3_
  35.9 0.0 copy-start.3
  35.9 21.4 %all-gather.3.cloned.1.call-done = bf16[1024,896]{1,0:T(8,128)(2,1)} async-done(((bf16[128,896]{1,0:T(8,128)(2,1)}), bf16[1024,896]{1,0:T(8,128)(2,1)}) %all-gather.3.cloned.1.call-update) | async-done | bytes 1835024 | tf_op jit(solution)/shard_map/all_gather | solution.py:65
  57.3 0.0 copy-done.1
  57.3 0.0 copy-done.2
  57.3 0.0 copy-done.3
  57.3 4.3 %blocks.2 = bf16[8,256,256]{2,1,0:T(8,128)(2,1)} custom-call(s32[2]{0:T(128)} %pad_add_fusion.1.where, bf16[256,896]{1,0:T(8,128)(2,1)} %grads.3, bf16[256,896]{1,0:T(8,128)(2,1)} %copy-done.1, bf16[256,896]{1,0:T(8,128)(2,1)} %copy-done.2, bf16[256,896]{1,0:T(8,128)(2,1)} %copy-done.3, bf16[8,128,896]{2,1,0:T(8,128)(2,1)} %bitcast.13), custom_call_target="tpu_custom_call" | custom-call | tf_op jit(solution)/shard_map/blocks/pallas_call | solution.py:53
  61.6 1.9 %collective-permute-start.3 = (bf16[8,256,256]{2,1,0:T(8,128)(2,1)}, bf16[8,256,256]{2,1,0:T(8,128)(2,1)S(1)}, u32[]{:S(2)}, u32[]{:S(2)}) collective-permute-start(bf16[8,256,256]{2,1,0:T(8,128)(2,1)} %blocks.2), channel_id=1, source_target_pairs={{0,1},{1,0},{2,3},{3,2},{4,5},{5,4},{6,7},{7,6},{8,9},{9,8},{10,11... | collective-permute-start | bytes 3145736 | tf_op jit(solution)/shard_map/ppermute | solution.py:29
  63.5 0.6 pad_add_fusion.where
  64.1 2.3 %collective-permute-done.3.refs_5_ = bf16[8,256,256]{2,1,0:T(8,128)(2,1)S(1)} collective-permute-done((bf16[8,256,256]{2,1,0:T(8,128)(2,1)}, bf16[8,256,256]{2,1,0:T(8,128)(2,1)S(1)}, u32[]{:S(2)}, u32[]{:S(2)}) %collective-permute-start.3) | collective-permute-done | bytes 1048608 | tf_op jit(solution)/shard_map/ppermute | solution.py:29
  66.4 0.0 copy-start.4
  66.4 1.0 copy-done.4
  67.4 4.6 %blocks.3 = bf16[8,256,256]{2,1,0:T(8,128)(2,1)} custom-call(s32[2]{0:T(128)} %pad_add_fusion.where, bf16[256,896]{1,0:T(8,128)(2,1)} %grads.3, bf16[256,896]{1,0:T(8,128)(2,1)} %copy-done.1, bf16[256,896]{1,0:T(8,128)(2,1)} %copy-done.2, bf16[256,896]{1,0:T(8,128)(2,1)} %copy-done.3, bf16[8,128,896]{2,1,0:T(8,128)(2,1)} %bitcast.14, ...), custom_call_target="tpu_custom_call" | custom-call | tf_op jit(solution)/shard_map/blocks/pallas_call | solution.py:53
  72.0 0.0 copy-start
  72.0 0.0 reduce-scatter.2.cloned.1.call-update
  72.0 2.2 %shard_map.67 = f32[16,4,256]{2,1,0:T(4,128)} custom-call(f32[64,896]{1,0:T(8,128)} %bitcast.15, bf16[256,896]{1,0:T(8,128)(2,1)} %grads.3), custom_call_target="tpu_custom_call" | custom-call | tf_op jit(solution)/shard_map/pallas_call | solution.py:162
  74.2 14.7 %all_to_all.30.arrived = f32[16,4,256]{2,1,0:T(4,128)} all-to-all(f32[16,4,256]{2,1,0:T(4,128)} %shard_map.67), channel_id=1, replica_groups=mesh['x'=4,'z'=8,'y'=8,'c'=2] {'y','c'}, dimensions={0} | all-to-all | bytes 131072 | tf_op jit(solution)/shard_map/all_to_all | solution.py:20
  89.0 2.7 %shard_map.68 = f32[32,4,128]{2,1,0:T(4,128)} custom-call(f32[16,4,256]{2,1,0:T(4,128)} %all_to_all.30.arrived, bf16[256,4096]{1,0:T(8,128)(2,1)} %activations.1), custom_call_target="tpu_custom_call" | custom-call | tf_op jit(solution)/shard_map/pallas_call | solution.py:162
  91.6 16.8 %all_to_all.31 = f32[32,4,128]{2,1,0:T(4,128)S(1)} all-to-all(f32[32,4,128]{2,1,0:T(4,128)} %shard_map.68), channel_id=1, replica_groups=mesh['x'=4,'z'=8,'y'=8,'c'=2] {'x','z'}, dimensions={0} | all-to-all | bytes 131072 | tf_op jit(solution)/shard_map/all_to_all | solution.py:20
  108.5 13.1 %all_to_all.32 = f32[32,4,128]{2,1,0:T(4,128)S(1)} all-to-all(f32[32,4,128]{2,1,0:T(4,128)S(1)} %broadcast_in_dim.6), channel_id=1, replica_groups=mesh['x'=4,'z'=8,'y'=8,'c'=2] {'x','z'}, dimensions={0} | all-to-all | bytes 131072 | tf_op jit(solution)/shard_map/all_to_all | solution.py:20
  121.5 0.0 copy-done
  121.5 1.7 fusion
  123.3 10.8 %all_to_all.33 = f32[16,4,384]{2,1,0:T(4,128)S(1)} all-to-all(f32[16,4,384]{2,1,0:T(4,128)S(1)} %broadcast_in_dim.7), channel_id=1, replica_groups=mesh['x'=4,'z'=8,'y'=8,'c'=2] {'y','c'}, dimensions={0} | all-to-all | bytes 196608 | tf_op jit(solution)/shard_map/all_to_all | solution.py:20
  134.2 0.7 reshape.19.both
  134.8 2.1 %shard_map.69 = f32[32,2,1024]{2,1,0:T(2,128)} custom-call(f32[64,384]{1,0:T(8,128)} %reshape.19.both, bf16[256,896]{1,0:T(8,128)(2,1)} %grads.3), custom_call_target="tpu_custom_call" | custom-call | tf_op jit(solution)/shard_map/pallas_call | solution.py:162
  136.9 17.9 %all_to_all.34 = f32[32,2,1024]{2,1,0:T(2,128)S(1)} all-to-all(f32[32,2,1024]{2,1,0:T(2,128)} %shard_map.69), channel_id=1, replica_groups=mesh['x'=4,'z'=8,'y'=8,'c'=2] {'x','z'}, dimensions={0} | all-to-all | bytes 524288 | tf_op jit(solution)/shard_map/all_to_all | solution.py:20
  154.9 0.1 reduce_sum.19
  155.0 0.8 broadcast_in_dim.8
  155.7 4.7 %all-to-all-start.5 = ((f32[32,2,1024]{2,1,0:T(2,128)}), f32[32,2,1024]{2,1,0:T(2,128)S(1)}, u32[]{:S(2)}, u32[]{:S(2)}) async-start(f32[32,2,1024]{2,1,0:T(2,128)} %broadcast_in_dim.8), calls=%async_computation.6 | async-start | bytes 524288 | tf_op jit(solution)/shard_map/all_to_all | solution.py:20
  160.5 0.0 reduce-scatter.2.cloned.1.call-done
  160.5 1.6 collective-permute-start.4
  162.1 1.4 slice.4.left_rows
  163.4 9.3 %all-to-all-done.5 = f32[32,2,1024]{2,1,0:T(2,128)S(1)} async-done(((f32[32,2,1024]{2,1,0:T(2,128)}), f32[32,2,1024]{2,1,0:T(2,128)S(1)}, u32[]{:S(2)}, u32[]{:S(2)}) %all-to-all-start.5) | async-done | bytes 262176 | tf_op jit(solution)/shard_map/all_to_all | solution.py:20
  172.8 0.9 reshape.20.packed
  173.7 8.2 %shard_map.70 = (f32[64,896]{1,0:T(8,128)}, f32[128,896]{1,0:T(8,128)}) custom-call(f32[64,1024]{1,0:T(8,128)} %reshape.20.packed, f32[64,128]{1,0:T(8,128)} %slice.4.left_rows, bf16[128,896]{1,0:T(8,128)(2,1)} %weight.1), custom_call_target="tpu_custom_call" | custom-call | tf_op jit(solution)/shard_map/pallas_call | solution.py:162
  181.8 0.0 collective-permute-done.4
  181.9 0.7 copy.8
  (4 shorter events, 0.1 us)
Async XLA Ops:
  7.2 50.1 %all-gather.3.cloned.1.call-start = ((), (), s32[]{:S(2)}) async-start(), calls=%async_computation.8 | async-start | bytes 2064384 | tf_op jit(solution)/shard_map/all_gather | solution.py:65
  7.9 152.6 %reduce-scatter.2.cloned.1.call-start = ((), (), s32[]{:S(2)}) async-start(), calls=%async_computation.7 | async-start | bytes 1179648 | tf_op jit(solution)/shard_map/reduce_scatter | solution.py:70
  7.9 15.7 %collective-permute-start = (bf16[256,896]{1,0:T(8,128)(2,1)}, bf16[256,896]{1,0:T(8,128)(2,1)S(1)}, u32[]{:S(2)}, u32[]{:S(2)}) collective-permute-start(bf16[256,896]{1,0:T(8,128)(2,1)} %grads.3), channel_id=1, source_target_pairs={{0,128},{128,256},{256,384},{384,0},{1,129},{129,257},{257,385},{3... | collective-permute-start | bytes 1376264 | tf_op jit(solution)/shard_map/ppermute | solution.py:29
  11.4 23.0 %collective-permute-start.1 = (bf16[256,896]{1,0:T(8,128)(2,1)}, bf16[256,896]{1,0:T(8,128)(2,1)S(1)}, u32[]{:S(2)}, u32[]{:S(2)}) collective-permute-start(bf16[256,896]{1,0:T(8,128)(2,1)} %grads.3), channel_id=1, source_target_pairs={{0,256},{128,384},{256,0},{384,128},{1,257},{129,385},{257,1},{385... | collective-permute-start | bytes 1376264 | tf_op jit(solution)/shard_map/ppermute | solution.py:29
  16.0 19.9 %collective-permute-start.2 = (bf16[256,896]{1,0:T(8,128)(2,1)}, bf16[256,896]{1,0:T(8,128)(2,1)S(1)}, u32[]{:S(2)}, u32[]{:S(2)}) collective-permute-start(bf16[256,896]{1,0:T(8,128)(2,1)} %grads.3), channel_id=1, source_target_pairs={{0,384},{128,0},{256,128},{384,256},{1,385},{129,1},{257,129},{385... | collective-permute-start | bytes 1376264 | tf_op jit(solution)/shard_map/ppermute | solution.py:29
  23.7 33.6 %copy-start.1 = (bf16[256,896]{1,0:T(8,128)(2,1)}, bf16[256,896]{1,0:T(8,128)(2,1)S(1)}, u32[]{:S(2)}) copy-start(bf16[256,896]{1,0:T(8,128)(2,1)S(1)} %collective-permute-done.refs_1_) | copy-start | bytes 1376260
  34.3 22.9 %copy-start.2 = (bf16[256,896]{1,0:T(8,128)(2,1)}, bf16[256,896]{1,0:T(8,128)(2,1)S(1)}, u32[]{:S(2)}) copy-start(bf16[256,896]{1,0:T(8,128)(2,1)S(1)} %collective-permute-done.1.refs_2_) | copy-start | bytes 1376260
  35.9 21.4 %copy-start.3 = (bf16[256,896]{1,0:T(8,128)(2,1)}, bf16[256,896]{1,0:T(8,128)(2,1)S(1)}, u32[]{:S(2)}) copy-start(bf16[256,896]{1,0:T(8,128)(2,1)S(1)} %collective-permute-done.2.refs_3_) | copy-start | bytes 1376260
  61.6 4.8 %collective-permute-start.3 = (bf16[8,256,256]{2,1,0:T(8,128)(2,1)}, bf16[8,256,256]{2,1,0:T(8,128)(2,1)S(1)}, u32[]{:S(2)}, u32[]{:S(2)}) collective-permute-start(bf16[8,256,256]{2,1,0:T(8,128)(2,1)} %blocks.2), channel_id=1, source_target_pairs={{0,1},{1,0},{2,3},{3,2},{4,5},{5,4},{6,7},{7,6},{8,9},{9,8},{10,11... | collective-permute-start | bytes 3145736 | tf_op jit(solution)/shard_map/ppermute | solution.py:29
  66.4 1.0 copy-start.4
  72.0 49.6 %copy-start = (bf16[256,4096]{1,0:T(8,128)(2,1)S(1)}, bf16[256,4096]{1,0:T(8,128)(2,1)}, u32[]{:S(2)}) copy-start(bf16[256,4096]{1,0:T(8,128)(2,1)} %activations.1) | copy-start | bytes 6291460
  155.7 17.0 %all-to-all-start.5 = ((f32[32,2,1024]{2,1,0:T(2,128)}), f32[32,2,1024]{2,1,0:T(2,128)S(1)}, u32[]{:S(2)}, u32[]{:S(2)}) async-start(f32[32,2,1024]{2,1,0:T(2,128)} %broadcast_in_dim.8), calls=%async_computation.6 | async-start | bytes 524288 | tf_op jit(solution)/shard_map/all_to_all | solution.py:20
  160.5 21.4 %collective-permute-start.4 = (bf16[256,256]{1,0:T(8,128)(2,1)}, bf16[256,256]{1,0:T(8,128)(2,1)S(1)}, u32[]{:S(2)}, u32[]{:S(2)}) collective-permute-start(bf16[256,256]{1,0:T(8,128)(2,1)} %bitcast.17), channel_id=1, source_target_pairs={{0,0},{1,1},{2,2},{3,3},{4,128},{5,129},{6,130},{7,131},{8,256},{9... | collective-permute-start | bytes 393224 | tf_op jit(solution)/shard_map/ppermute | solution.py:76
Sparse Core Ops, SparseCore 0:
  10.0 47.1 all-gather.2
  72.1 40.0 reduce-scatter.1

commit v4 on v3

--- a/solution.py
+++ b/solution.py
@@ -63,7 +63,9 @@
     n_x, n_y = lax.axis_size("x"), lax.axis_size("y")
     core = lax.axis_index("c")
     weights = lax.all_gather(weight, "z", axis=0)
-    grads = [grad_output] + [shifted(grad_output, "x", s) for s in range(1, n_x)]
+    grads = [grad_output]
+    for s in range(1, n_x):
+        grads.append(shifted(grad_output, "x", s))
     give = block_products(1 - core, grads, weights)
     arrived = shifted(give, "c", 1)
     parts = block_products(core, grads, weights, (arrived,))
@@ -112,11 +114,33 @@
         out[d] = total[:, d * rows : (d + 1) * rows]
 
 
-def right_kernel(both, grads, out):
+def seen_kernel(arrived, activations, mine, out, lines):
+    n_d, few, rows = arrived.shape
+    tokens = activations.shape[0]
+    for d in range(n_d):
+        lines[:few, d * rows : (d + 1) * rows] = arrived[d]
+    left = lines[:few]
+    for i, part in enumerate(thirds(left)):
+        lines[i * few : (i + 1) * few] = part.astype(jnp.float32)
+    dims = (((1,), (1,)), ((), ()))
+    dot = lax.dot_general(
+        lines[: 3 * few].astype(jnp.bfloat16), activations[...], dims, preferred_element_type=jnp.float32
+    )
+    seen = (dot[2 * few :] + dot[few : 2 * few]) + dot[:few]
+    for t in range(out.shape[0]):
+        out[t, :, :tokens] = seen
+        out[t, :, tokens:] = mine[...]
+
+
+def right_kernel(both, grads, out, left_rows, lines):
     tokens, hidden = grads.shape
-    rank = both.shape[0]
-    right = exact_dot(both[:, :tokens], grads[...], ((1,), (0,)))
-    rows = both[:, tokens:]
+    n_t, few, _ = both.shape
+    rank = n_t * few
+    for t in range(n_t):
+        lines[t * few : (t + 1) * few] = both[t]
+    right = exact_dot(lines[:, :tokens], grads[...], ((1,), (0,)))
+    rows = lines[:, tokens:]
+    left_rows[...] = rows
     gram = lax.dot_general(rows, rows, (((1,), (1,)), ((), ())), precision=HIGH, preferred_element_type=jnp.float32)
     few = out.shape[1]
     for d in range(out.shape[0]):
@@ -125,7 +149,10 @@
         out[d, :, hidden + rank :] = jnp.zeros((few, out.shape[2] - hidden - rank), jnp.float32)
 
 
-def last_kernel(token_total, packed, left_rows, weight, right_basis, new_weight):
+def last_kernel(token_total, arrived, left_rows, weight, right_basis, new_weight, packed):
+    few = arrived.shape[1]
+    for d in range(arrived.shape[0]):
+        packed[d * few : (d + 1) * few] = arrived[d]
     rank = packed.shape[0]
     hidden = weight.shape[1]
     row = lax.broadcasted_iota(jnp.int32, (8, 2 * rank), 0)
@@ -182,19 +209,33 @@
     left_mine = swap(left_part, DP)
     left_mine = left_mine.sum(axis=0)
     left_few = share(left_mine, DP)
-    left_few = jnp.swapaxes(left_few, 0, 1).reshape(few, features)
-    a32 = activations.astype(f32)
-    seen = lax.dot_general(left_few, a32, (((1,), (1,)), ((), ())), precision=HIGH)
-    both = share(jnp.concatenate([seen, left_mine], axis=1), TENSOR)
-    both = both.reshape(rank, tokens + rows)
+    both = run(
+        seen_kernel,
+        (n_t, few, tokens + rows),
+        left_few,
+        activations,
+        left_mine,
+        scratch=[pltpu.VMEM((16, features), f32)],
+    )
+    both = swap(both, TENSOR)
     width = hidden + 128
-    packed = run(right_kernel, (n_d, rank // n_d, width), both, grad_output)
+    packed, left_rows = run(
+        right_kernel,
+        ((n_d, rank // n_d, width), (rank, rows)),
+        both,
+        grad_output,
+        scratch=[pltpu.VMEM((rank, tokens + rows), f32)],
+    )
     packed = swap(packed, DP)
     packed = packed.sum(axis=0)
     packed = share(packed, DP)
-    packed = packed.reshape(rank, width)
     right_basis, new_weight = run(
-        functools.partial(last_kernel, tokens * n_d), ((rank, hidden), (rows, hidden)), packed, both[:, tokens:], weight
+        functools.partial(last_kernel, tokens * n_d),
+        ((rank, hidden), (rows, hidden)),
+        packed,
+        left_rows,
+        weight,
+        scratch=[pltpu.VMEM((rank, width), f32)],
     )
     return (input_grad, right_basis.T, new_weight)
 

time: 190 us -> 192 us (1.011)
  Pallas kernels: 24.2 us -> 27 us
  local copies, waits for them, and re-layouts: 5.39 us -> 3.13 us
  blocking collectives: 73.3 us -> 75.4 us
    pallas_call x4 -> x5, Pallas kernels: 15.2 us -> 18 us  [run(): pl.pallas_call(kernel, out_shape=outs if several else outs[0], in_specs=[...]
    all_to_all x5, blocking collectives: 73.3 us -> 75.4 us  [swap(): return lax.all_to_all(parts, axis, split_axis=0, concat_axis=0, tiled=True)]
  transfers between devices with their start and end apart: 8 -> 8, of which waited for: 6 -> 6; matrix products, arithmetic and copies ran while one was open for 4% -> 1% of each run, Pallas kernels for 8% -> 9%
where the time goes in v4:
time: 192 us
  blocking collectives  75.4 us (39%)
  waiting for transfers between devices  51 us (27%)
  Pallas kernels  27 us (14%)
  starting transfers between devices  19.7 us (10%)
  between operations  14.1 us (7%)
  local copies, waits for them, and re-layouts  3.13 us (2%)
    all_to_all x5, blocking collectives, swap(): return lax.all_to_all(parts, axis, split_axis=0, concat_axis=0, tiled=True)  75.4 us
    all_gather x1, waiting for transfers between devices, input_gradient(): weights = lax.all_gather(weight, 'z', axis=0)  21.4 us
    ppermute x4, waiting for transfers between devices, shifted(): lax.ppermute(x, axis, [(i, (i + by) % length) for i in range(length)])  18.1 us
    pallas_call x5, Pallas kernels, run(): pl.pallas_call(kernel, out_shape=outs if several else outs[0], in_specs=[...  18 us
    ppermute x4, starting transfers between devices, shifted(): lax.ppermute(x, axis, [(i, (i + by) % length) for i in range(length)])  13.3 us
    all_to_all x1, waiting for transfers between devices, swap(): return lax.all_to_all(parts, axis, split_axis=0, concat_axis=0, tiled=True)  10.7 us
    pallas_call x2, Pallas kernels, block_products(): pl.pallas_call(functools.partial(block_kernel, n_x), out_shape=jax.ShapeD...  8.96 us
    all_to_all x1, starting transfers between devices, swap(): return lax.all_to_all(parts, axis, split_axis=0, concat_axis=0, tiled=True)  4.73 us
  transfers between devices with their start and end apart: 8, of which 6 were waited for; matrix products, arithmetic and copies ran while one was open for 1% of the time, Pallas kernels for 9%

profile of v4, /device:TPU:64, one launch (start us, length us, event | category | flops | bytes accessed | tf_op | source)
XLA Modules:
  0.0 191.6 jit_solution(15454466014165224517)
XLA Ops:
  7.2 0.0 all-gather.3.cloned.1.call-start
  7.2 0.7 all-gather.3.cloned.1.call-update
  7.9 0.0 reduce-scatter.2.cloned.1.call-start
  7.9 3.4 %collective-permute-start = (bf16[256,896]{1,0:T(8,128)(2,1)}, bf16[256,896]{1,0:T(8,128)(2,1)S(1)}, u32[]{:S(2)}, u32[]{:S(2)}) collective-permute-start(bf16[256,896]{1,0:T(8,128)(2,1)} %grads.3), channel_id=1, source_target_pairs={{0,128},{128,256},{256,384},{384,0},{1,129},{129,257},{257,385},{3... | collective-permute-start | bytes 1376264 | tf_op jit(solution)/shard_map/ppermute | solution.py:29
  11.4 4.6 %collective-permute-start.1 = (bf16[256,896]{1,0:T(8,128)(2,1)}, bf16[256,896]{1,0:T(8,128)(2,1)S(1)}, u32[]{:S(2)}, u32[]{:S(2)}) collective-permute-start(bf16[256,896]{1,0:T(8,128)(2,1)} %grads.3), channel_id=1, source_target_pairs={{0,256},{128,384},{256,0},{384,128},{1,257},{129,385},{257,1},{385... | collective-permute-start | bytes 1376264 | tf_op jit(solution)/shard_map/ppermute | solution.py:29
  16.0 3.3 %collective-permute-start.2 = (bf16[256,896]{1,0:T(8,128)(2,1)}, bf16[256,896]{1,0:T(8,128)(2,1)S(1)}, u32[]{:S(2)}, u32[]{:S(2)}) collective-permute-start(bf16[256,896]{1,0:T(8,128)(2,1)} %grads.3), channel_id=1, source_target_pairs={{0,384},{128,0},{256,128},{384,256},{1,385},{129,1},{257,129},{385... | collective-permute-start | bytes 1376264 | tf_op jit(solution)/shard_map/ppermute | solution.py:29
  19.4 0.7 pad_add_fusion.1.where
  20.0 3.6 %collective-permute-done.refs_1_ = bf16[256,896]{1,0:T(8,128)(2,1)S(1)} collective-permute-done((bf16[256,896]{1,0:T(8,128)(2,1)}, bf16[256,896]{1,0:T(8,128)(2,1)S(1)}, u32[]{:S(2)}, u32[]{:S(2)}) %collective-permute-start) | collective-permute-done | bytes 458784 | tf_op jit(solution)/shard_map/ppermute | solution.py:29
  23.7 0.0 copy-start
  23.7 10.7 %collective-permute-done.1.refs_2_ = bf16[256,896]{1,0:T(8,128)(2,1)S(1)} collective-permute-done((bf16[256,896]{1,0:T(8,128)(2,1)}, bf16[256,896]{1,0:T(8,128)(2,1)S(1)}, u32[]{:S(2)}, u32[]{:S(2)}) %collective-permute-start.1) | collective-permute-done | bytes 458784 | tf_op jit(solution)/shard_map/ppermute | solution.py:29
  34.3 0.0 copy-start.1
  34.3 1.6 collective-permute-done.2.refs_3_
  35.9 0.0 copy-start.2
  35.9 21.4 %all-gather.3.cloned.1.call-done = bf16[1024,896]{1,0:T(8,128)(2,1)} async-done(((bf16[128,896]{1,0:T(8,128)(2,1)}), bf16[1024,896]{1,0:T(8,128)(2,1)}) %all-gather.3.cloned.1.call-update) | async-done | bytes 1835024 | tf_op jit(solution)/shard_map/all_gather | solution.py:65
  57.3 0.0 copy-done
  57.3 0.0 copy-done.1
  57.3 0.0 copy-done.2
  57.3 4.3 %blocks.2 = bf16[8,256,256]{2,1,0:T(8,128)(2,1)} custom-call(s32[2]{0:T(128)} %pad_add_fusion.1.where, bf16[256,896]{1,0:T(8,128)(2,1)} %grads.3, bf16[256,896]{1,0:T(8,128)(2,1)} %copy-done, bf16[256,896]{1,0:T(8,128)(2,1)} %copy-done.1, bf16[256,896]{1,0:T(8,128)(2,1)} %copy-done.2, bf16[8,128,896]{2,1,0:T(8,128)(2,1)} %bitcast.7), custom_call_target="tpu_custom_call" | custom-call | tf_op jit(solution)/shard_map/blocks/pallas_call | solution.py:53
  61.6 1.9 collective-permute-start.3
  63.5 0.6 pad_add_fusion.where
  64.1 2.3 %collective-permute-done.3.refs_5_ = bf16[8,256,256]{2,1,0:T(8,128)(2,1)S(1)} collective-permute-done((bf16[8,256,256]{2,1,0:T(8,128)(2,1)}, bf16[8,256,256]{2,1,0:T(8,128)(2,1)S(1)}, u32[]{:S(2)}, u32[]{:S(2)}) %collective-permute-start.3) | collective-permute-done | bytes 1048608 | tf_op jit(solution)/shard_map/ppermute | solution.py:29
  66.4 0.0 copy-start.4
  66.4 1.0 copy-done.4
  67.4 4.6 %blocks.3 = bf16[8,256,256]{2,1,0:T(8,128)(2,1)} custom-call(s32[2]{0:T(128)} %pad_add_fusion.where, bf16[256,896]{1,0:T(8,128)(2,1)} %grads.3, bf16[256,896]{1,0:T(8,128)(2,1)} %copy-done, bf16[256,896]{1,0:T(8,128)(2,1)} %copy-done.1, bf16[256,896]{1,0:T(8,128)(2,1)} %copy-done.2, bf16[8,128,896]{2,1,0:T(8,128)(2,1)} %bitcast.8, bf16[8,256,256]{2,1,0:T(8,128)(2,1)} %copy-done.4), custom_call_target="tpu_custom_call" | custom-call | tf_op jit(solution)/shard_map/blocks/pallas_call | solution.py:53
  72.0 0.0 reduce-scatter.2.cloned.1.call-update
  72.0 2.1 %shard_map.67 = f32[16,4,256]{2,1,0:T(4,128)} custom-call(f32[64,896]{1,0:T(8,128)} %bitcast.9, bf16[256,896]{1,0:T(8,128)(2,1)} %grads.3), custom_call_target="tpu_custom_call" | custom-call | tf_op jit(solution)/shard_map/pallas_call | solution.py:189
  74.1 14.7 %all_to_all.30.arrived = f32[16,4,256]{2,1,0:T(4,128)} all-to-all(f32[16,4,256]{2,1,0:T(4,128)} %shard_map.67), channel_id=1, replica_groups=mesh['x'=4,'z'=8,'y'=8,'c'=2] {'y','c'}, dimensions={0} | all-to-all | bytes 131072 | tf_op jit(solution)/shard_map/all_to_all | solution.py:20
  88.8 2.7 %shard_map.68 = f32[32,4,128]{2,1,0:T(4,128)} custom-call(f32[16,4,256]{2,1,0:T(4,128)} %all_to_all.30.arrived, bf16[256,4096]{1,0:T(8,128)(2,1)} %activations.3), custom_call_target="tpu_custom_call" | custom-call | tf_op jit(solution)/shard_map/pallas_call | solution.py:189
  91.5 16.8 %all_to_all.31 = f32[32,4,128]{2,1,0:T(4,128)S(1)} all-to-all(f32[32,4,128]{2,1,0:T(4,128)} %shard_map.68), channel_id=1, replica_groups=mesh['x'=4,'z'=8,'y'=8,'c'=2] {'x','z'}, dimensions={0} | all-to-all | bytes 131072 | tf_op jit(solution)/shard_map/all_to_all | solution.py:20
  108.4 0.0 copy-start.5
  108.4 13.5 %all_to_all.32.arrived = f32[32,4,128]{2,1,0:T(4,128)} all-to-all(f32[32,4,128]{2,1,0:T(4,128)S(1)} %broadcast_in_dim.4), channel_id=1, replica_groups=mesh['x'=4,'z'=8,'y'=8,'c'=2] {'x','z'}, dimensions={0} | all-to-all | bytes 131072 | tf_op jit(solution)/shard_map/all_to_all | solution.py:20
  121.9 0.0 copy-done.5
  121.9 2.9 %shard_map.69 = f32[16,4,384]{2,1,0:T(4,128)} custom-call(f32[32,4,128]{2,1,0:T(4,128)} %all_to_all.32.arrived, bf16[256,4096]{1,0:T(8,128)(2,1)} %activations.3, f32[4,128]{1,0:T(4,128)} %copy-done.5), custom_call_target="tpu_custom_call" | custom-call | tf_op jit(solution)/shard_map/pallas_call | solution.py:189
  124.9 12.4 %all_to_all.33.both = f32[16,4,384]{2,1,0:T(4,128)} all-to-all(f32[16,4,384]{2,1,0:T(4,128)} %shard_map.69), channel_id=1, replica_groups=mesh['x'=4,'z'=8,'y'=8,'c'=2] {'y','c'}, dimensions={0} | all-to-all | bytes 196608 | tf_op jit(solution)/shard_map/all_to_all | solution.py:20
  137.3 2.1 %shard_map.70 = (f32[32,2,1024]{2,1,0:T(2,128)}, f32[64,128]{1,0:T(8,128)}) custom-call(f32[16,4,384]{2,1,0:T(4,128)} %all_to_all.33.both, bf16[256,896]{1,0:T(8,128)(2,1)} %grads.3), custom_call_target="tpu_custom_call" | custom-call | tf_op jit(solution)/shard_map/pallas_call | solution.py:189
  139.4 17.9 %all_to_all.34 = f32[32,2,1024]{2,1,0:T(2,128)S(1)} all-to-all(f32[32,2,1024]{2,1,0:T(2,128)} %get-tuple-element.7), channel_id=1, replica_groups=mesh['x'=4,'z'=8,'y'=8,'c'=2] {'x','z'}, dimensions={0} | all-to-all | bytes 524288 | tf_op jit(solution)/shard_map/all_to_all | solution.py:20
  157.3 0.1 reduce_sum.19
  157.4 0.8 broadcast_in_dim.5
  158.2 4.7 %all-to-all-start.5 = ((f32[32,2,1024]{2,1,0:T(2,128)}), f32[32,2,1024]{2,1,0:T(2,128)S(1)}, u32[]{:S(2)}, u32[]{:S(2)}) async-start(f32[32,2,1024]{2,1,0:T(2,128)} %broadcast_in_dim.5), calls=%async_computation.6 | async-start | bytes 524288 | tf_op jit(solution)/shard_map/all_to_all | solution.py:20
  162.9 0.0 reduce-scatter.2.cloned.1.call-done
  162.9 1.6 collective-permute-start.4
  164.5 10.7 %all-to-all-done.5.arrived = f32[32,2,1024]{2,1,0:T(2,128)S(1)} async-done(((f32[32,2,1024]{2,1,0:T(2,128)}), f32[32,2,1024]{2,1,0:T(2,128)S(1)}, u32[]{:S(2)}, u32[]{:S(2)}) %all-to-all-start.5) | async-done | bytes 262176 | tf_op jit(solution)/shard_map/all_to_all | solution.py:20
  175.2 0.0 copy-start.3
  175.2 0.7 copy-done.3
  175.9 8.2 %shard_map.71 = (f32[64,896]{1,0:T(8,128)}, f32[128,896]{1,0:T(8,128)}) custom-call(f32[32,2,1024]{2,1,0:T(2,128)} %copy-done.3, f32[64,128]{1,0:T(8,128)} %get-tuple-element.8.left_rows, bf16[128,896]{1,0:T(8,128)(2,1)} %weight.1), custom_call_target="tpu_custom_call" | custom-call | tf_op jit(solution)/shard_map/pallas_call | solution.py:189
  184.1 0.0 collective-permute-done.4
  184.1 0.7 copy.8
  (2 shorter events, 0.1 us)
Async XLA Ops:
  7.2 50.1 %all-gather.3.cloned.1.call-start = ((), (), s32[]{:S(2)}) async-start(), calls=%async_computation.8 | async-start | bytes 2064384 | tf_op jit(solution)/shard_map/all_gather | solution.py:65
  7.9 155.0 %reduce-scatter.2.cloned.1.call-start = ((), (), s32[]{:S(2)}) async-start(), calls=%async_computation.7 | async-start | bytes 1179648 | tf_op jit(solution)/shard_map/reduce_scatter | solution.py:72
  7.9 15.7 %collective-permute-start = (bf16[256,896]{1,0:T(8,128)(2,1)}, bf16[256,896]{1,0:T(8,128)(2,1)S(1)}, u32[]{:S(2)}, u32[]{:S(2)}) collective-permute-start(bf16[256,896]{1,0:T(8,128)(2,1)} %grads.3), channel_id=1, source_target_pairs={{0,128},{128,256},{256,384},{384,0},{1,129},{129,257},{257,385},{3... | collective-permute-start | bytes 1376264 | tf_op jit(solution)/shard_map/ppermute | solution.py:29
  11.4 23.0 %collective-permute-start.1 = (bf16[256,896]{1,0:T(8,128)(2,1)}, bf16[256,896]{1,0:T(8,128)(2,1)S(1)}, u32[]{:S(2)}, u32[]{:S(2)}) collective-permute-start(bf16[256,896]{1,0:T(8,128)(2,1)} %grads.3), channel_id=1, source_target_pairs={{0,256},{128,384},{256,0},{384,128},{1,257},{129,385},{257,1},{385... | collective-permute-start | bytes 1376264 | tf_op jit(solution)/shard_map/ppermute | solution.py:29
  16.0 19.9 %collective-permute-start.2 = (bf16[256,896]{1,0:T(8,128)(2,1)}, bf16[256,896]{1,0:T(8,128)(2,1)S(1)}, u32[]{:S(2)}, u32[]{:S(2)}) collective-permute-start(bf16[256,896]{1,0:T(8,128)(2,1)} %grads.3), channel_id=1, source_target_pairs={{0,384},{128,0},{256,128},{384,256},{1,385},{129,1},{257,129},{385... | collective-permute-start | bytes 1376264 | tf_op jit(solution)/shard_map/ppermute | solution.py:29
  23.7 33.6 %copy-start = (bf16[256,896]{1,0:T(8,128)(2,1)}, bf16[256,896]{1,0:T(8,128)(2,1)S(1)}, u32[]{:S(2)}) copy-start(bf16[256,896]{1,0:T(8,128)(2,1)S(1)} %collective-permute-done.refs_1_) | copy-start | bytes 1376260
  34.3 22.9 %copy-start.1 = (bf16[256,896]{1,0:T(8,128)(2,1)}, bf16[256,896]{1,0:T(8,128)(2,1)S(1)}, u32[]{:S(2)}) copy-start(bf16[256,896]{1,0:T(8,128)(2,1)S(1)} %collective-permute-done.1.refs_2_) | copy-start | bytes 1376260
  35.9 21.4 %copy-start.2 = (bf16[256,896]{1,0:T(8,128)(2,1)}, bf16[256,896]{1,0:T(8,128)(2,1)S(1)}, u32[]{:S(2)}) copy-start(bf16[256,896]{1,0:T(8,128)(2,1)S(1)} %collective-permute-done.2.refs_3_) | copy-start | bytes 1376260
  61.6 4.8 %collective-permute-start.3 = (bf16[8,256,256]{2,1,0:T(8,128)(2,1)}, bf16[8,256,256]{2,1,0:T(8,128)(2,1)S(1)}, u32[]{:S(2)}, u32[]{:S(2)}) collective-permute-start(bf16[8,256,256]{2,1,0:T(8,128)(2,1)} %blocks.2), channel_id=1, source_target_pairs={{0,1},{1,0},{2,3},{3,2},{4,5},{5,4},{6,7},{7,6},{8,9},{9,8},{10,11... | collective-permute-start | bytes 3145736 | tf_op jit(solution)/shard_map/ppermute | solution.py:29
  66.4 1.0 copy-start.4
  108.4 13.6 %copy-start.5 = (f32[4,128]{1,0:T(4,128)}, f32[4,128]{1,0:T(4,128)S(1)}, u32[]{:S(2)}) copy-start(f32[4,128]{1,0:T(4,128)S(1)} %reduce_sum.18.mine) | copy-start | bytes 6148
  158.2 17.0 %all-to-all-start.5 = ((f32[32,2,1024]{2,1,0:T(2,128)}), f32[32,2,1024]{2,1,0:T(2,128)S(1)}, u32[]{:S(2)}, u32[]{:S(2)}) async-start(f32[32,2,1024]{2,1,0:T(2,128)} %broadcast_in_dim.5), calls=%async_computation.6 | async-start | bytes 524288 | tf_op jit(solution)/shard_map/all_to_all | solution.py:20
  162.9 21.2 %collective-permute-start.4 = (bf16[256,256]{1,0:T(8,128)(2,1)}, bf16[256,256]{1,0:T(8,128)(2,1)S(1)}, u32[]{:S(2)}, u32[]{:S(2)}) collective-permute-start(bf16[256,256]{1,0:T(8,128)(2,1)} %bitcast.11), channel_id=1, source_target_pairs={{0,0},{1,1},{2,2},{3,3},{4,128},{5,129},{6,130},{7,131},{8,256},{9... | collective-permute-start | bytes 393224 | tf_op jit(solution)/shard_map/ppermute | solution.py:78
  175.2 0.7 copy-start.3
Sparse Core Ops, SparseCore 0:
  10.0 47.1 all-gather.2
  72.1 40.0 reduce-scatter.1

commit v5 on v4

--- a/solution.py
+++ b/solution.py
@@ -50,13 +50,15 @@
     tokens, rows = grads[0].shape[0], weights.shape[1]
     vmem = pl.BlockSpec(memory_space=pltpu.VMEM)
     where = jnp.stack([lax.axis_index("x"), side]).astype(jnp.int32)
+    held = [pltpu.with_memory_space_constraint(a, pltpu.VMEM) for a in (*grads, *earlier)]
     return pl.pallas_call(
         functools.partial(block_kernel, n_x),
         out_shape=jax.ShapeDtypeStruct((n_y, tokens, 2 * rows), jnp.bfloat16),
         in_specs=[pl.BlockSpec(memory_space=pltpu.SMEM)] + [vmem] * (n_x + 1 + len(earlier)),
         out_specs=vmem,
+        compiler_params=pltpu.CompilerParams(vmem_limit_bytes=16 << 20),
         name="blocks",
-    )(where, *grads, weights, *earlier)
+    )(where, *held[:n_x], weights, *held[n_x:])
 
 
 def input_gradient(grad_output, weight):
@@ -184,6 +186,7 @@
 
 def run(kernel, shapes, *args, scratch=()):
     vmem = pl.BlockSpec(memory_space=pltpu.VMEM)
+    args = [pltpu.with_memory_space_constraint(a, pltpu.VMEM) for a in args]
     several = isinstance(shapes[0], tuple)
     outs = [jax.ShapeDtypeStruct(s, jnp.float32) for s in (shapes if several else (shapes,))]
     return pl.pallas_call(
@@ -192,6 +195,7 @@
         in_specs=[vmem] * len(args),
         out_specs=[vmem] * len(outs) if several else vmem,
         scratch_shapes=scratch,
+        compiler_params=pltpu.CompilerParams(vmem_limit_bytes=12 << 20),
     )(*args)
 
 

time: 192 us -> 178 us (0.927)
  Pallas kernels: 27 us -> 12.6 us
  local copies, waits for them, and re-layouts: 3.13 us -> 6.9 us
  blocking collectives: 75.4 us -> 72 us
    pallas_call x5, Pallas kernels: 18 us -> 8.91 us  [run(): pl.pallas_call(kernel, out_shape=outs if several else outs[0], in_specs=[...]
    pallas_call x2, Pallas kernels: 8.96 us -> 3.66 us  [block_products(): pl.pallas_call(functools.partial(block_kernel, n_x), out_shape=jax.ShapeD...]
    unnamed x13 -> x21, local copies, waits for them, and re-layouts: 2.35 us -> 6.11 us
    all_to_all x5, blocking collectives: 75.4 us -> 72 us  [swap(): return lax.all_to_all(parts, axis, split_axis=0, concat_axis=0, tiled=True)]
  transfers between devices with their start and end apart: 8 -> 8, of which waited for: 6 -> 6; matrix products, arithmetic and copies ran while one was open for 1% -> 1% of each run, Pallas kernels for 9% -> 5%
where the time goes in v5:
time: 178 us; the launch traced here: 177 us
  blocking collectives  72 us (40%)
  waiting for transfers between devices  51.8 us (29%)
  starting transfers between devices  19.7 us (11%)
  between operations  14.2 us (8%)
  Pallas kernels  12.6 us (7%)
  local copies, waits for them, and re-layouts  6.9 us (4%)
    all_to_all x5, blocking collectives, swap(): return lax.all_to_all(parts, axis, split_axis=0, concat_axis=0, tiled=True)  72 us
    all_gather x1, waiting for transfers between devices, input_gradient(): weights = lax.all_gather(weight, 'z', axis=0)  21.4 us
    ppermute x4, waiting for transfers between devices, shifted(): lax.ppermute(x, axis, [(i, (i + by) % length) for i in range(length)])  19 us
    ppermute x4, starting transfers between devices, shifted(): lax.ppermute(x, axis, [(i, (i + by) % length) for i in range(length)])  13.3 us
    all_to_all x1, waiting for transfers between devices, swap(): return lax.all_to_all(parts, axis, split_axis=0, concat_axis=0, tiled=True)  10.7 us
    pallas_call x5, Pallas kernels, run(): pl.pallas_call(kernel, out_shape=outs if several else outs[0], in_specs=[...  8.91 us
    unnamed x21, local copies, waits for them, and re-layouts  6.11 us
    all_to_all x1, starting transfers between devices, swap(): return lax.all_to_all(parts, axis, split_axis=0, concat_axis=0, tiled=True)  4.72 us
  transfers between devices with their start and end apart: 8, of which 6 were waited for; matrix products, arithmetic and copies ran while one was open for 1% of the time, Pallas kernels for 5%

profile of v5, /device:TPU:64, one launch (start us, length us, event | category | flops | bytes accessed | tf_op | source)
XLA Modules:
  0.0 177.4 jit_solution(13398557298236694652)
XLA Ops:
  7.2 0.0 all-gather.3.cloned.1.call-start
  7.2 0.7 all-gather.3.cloned.1.call-update
  7.9 0.0 reduce-scatter.2.cloned.1.call-start
  7.9 3.4 %collective-permute-start = (bf16[256,896]{1,0:T(8,128)(2,1)}, bf16[256,896]{1,0:T(8,128)(2,1)S(1)}, u32[]{:S(2)}, u32[]{:S(2)}) collective-permute-start(bf16[256,896]{1,0:T(8,128)(2,1)} %grads.3), channel_id=1, source_target_pairs={{0,128},{128,256},{256,384},{384,0},{1,129},{129,257},{257,385},{3... | collective-permute-start | bytes 1376264 | tf_op jit(solution)/shard_map/ppermute | solution.py:29
  11.4 4.6 %collective-permute-start.1 = (bf16[256,896]{1,0:T(8,128)(2,1)}, bf16[256,896]{1,0:T(8,128)(2,1)S(1)}, u32[]{:S(2)}, u32[]{:S(2)}) collective-permute-start(bf16[256,896]{1,0:T(8,128)(2,1)} %grads.3), channel_id=1, source_target_pairs={{0,256},{128,384},{256,0},{384,128},{1,257},{129,385},{257,1},{385... | collective-permute-start | bytes 1376264 | tf_op jit(solution)/shard_map/ppermute | solution.py:29
  16.0 3.3 %collective-permute-start.2 = (bf16[256,896]{1,0:T(8,128)(2,1)}, bf16[256,896]{1,0:T(8,128)(2,1)S(1)}, u32[]{:S(2)}, u32[]{:S(2)}) collective-permute-start(bf16[256,896]{1,0:T(8,128)(2,1)} %grads.3), channel_id=1, source_target_pairs={{0,384},{128,0},{256,128},{384,256},{1,385},{129,1},{257,129},{385... | collective-permute-start | bytes 1376264 | tf_op jit(solution)/shard_map/ppermute | solution.py:29
  19.4 0.1 pad_add_fusion.1.where
  19.4 4.2 %collective-permute-done.refs_1_ = bf16[256,896]{1,0:T(8,128)(2,1)S(1)} collective-permute-done((bf16[256,896]{1,0:T(8,128)(2,1)}, bf16[256,896]{1,0:T(8,128)(2,1)S(1)}, u32[]{:S(2)}, u32[]{:S(2)}) %collective-permute-start) | collective-permute-done | bytes 458784 | tf_op jit(solution)/shard_map/ppermute | solution.py:29
  23.7 10.7 %collective-permute-done.1.refs_2_ = bf16[256,896]{1,0:T(8,128)(2,1)S(1)} collective-permute-done((bf16[256,896]{1,0:T(8,128)(2,1)}, bf16[256,896]{1,0:T(8,128)(2,1)S(1)}, u32[]{:S(2)}, u32[]{:S(2)}) %collective-permute-start.1) | collective-permute-done | bytes 458784 | tf_op jit(solution)/shard_map/ppermute | solution.py:29
  34.3 1.6 collective-permute-done.2.refs_3_
  35.9 0.0 copy-start.6
  35.9 21.4 %all-gather.3.cloned.1.call-done = bf16[1024,896]{1,0:T(8,128)(2,1)} async-done(((bf16[128,896]{1,0:T(8,128)(2,1)}), bf16[1024,896]{1,0:T(8,128)(2,1)}) %all-gather.3.cloned.1.call-update) | async-done | bytes 1835024 | tf_op jit(solution)/shard_map/all_gather | solution.py:67
  57.3 0.0 copy-start.1
  57.3 1.0 copy-done.1
  58.3 0.0 copy-start.3
  58.3 1.5 copy-done.3
  59.8 0.0 copy-start.2
  59.8 0.0 copy-start.4
  59.8 1.8 %blocks.2 = bf16[8,256,256]{2,1,0:T(8,128)(2,1)S(1)} custom-call(s32[2]{0:T(128)S(1)} %pad_add_fusion.1.where, bf16[256,896]{1,0:T(8,128)(2,1)S(1)} %copy-done.1, bf16[256,896]{1,0:T(8,128)(2,1)S(1)} %collective-permute-done.refs_1_, bf16[256,896]{1,0:T(8,128)(2,1)S(1)} %collective-permute-done.1.refs_2_, ...), custom_call_target="tpu_custom_call" | custom-call | tf_op jit(solution)/shard_map/blocks/pallas_call | solution.py:54
  61.6 0.0 copy-done.6
  61.6 1.9 %collective-permute-start.3 = (bf16[8,256,256]{2,1,0:T(8,128)(2,1)S(1)}, bf16[8,256,256]{2,1,0:T(8,128)(2,1)S(1)}, u32[]{:S(2)}, u32[]{:S(2)}) collective-permute-start(bf16[8,256,256]{2,1,0:T(8,128)(2,1)S(1)} %blocks.2), channel_id=1, source_target_pairs={{0,1},{1,0},{2,3},{3,2},{4,5},{5,4},{6,7},{7,6},{8,9},{9,8},{10,11... | collective-permute-start | bytes 3145736 | tf_op jit(solution)/shard_map/ppermute | solution.py:29
  63.6 0.1 pad_add_fusion.where
  63.6 2.5 %collective-permute-done.3.refs_5_ = bf16[8,256,256]{2,1,0:T(8,128)(2,1)S(1)} collective-permute-done((bf16[8,256,256]{2,1,0:T(8,128)(2,1)S(1)}, bf16[8,256,256]{2,1,0:T(8,128)(2,1)S(1)}, u32[]{:S(2)}, u32[]{:S(2)}) %collective-permute-start.3) | collective-permute-done | bytes 1048608 | tf_op jit(solution)/shard_map/ppermute | solution.py:29
  66.2 0.0 copy-done.2
  66.2 0.0 copy-done.4
  66.2 0.0 copy-start.7
  66.2 1.0 copy-done.7
  67.2 0.0 copy-start
  67.2 1.8 %blocks.3 = bf16[8,256,256]{2,1,0:T(8,128)(2,1)S(1)} custom-call(s32[2]{0:T(128)S(1)} %pad_add_fusion.where, bf16[256,896]{1,0:T(8,128)(2,1)S(1)} %copy-done.2, bf16[256,896]{1,0:T(8,128)(2,1)S(1)} %collective-permute-done.refs_1_, bf16[256,896]{1,0:T(8,128)(2,1)S(1)} %collective-permute-done.1.refs_2_, bf16[256,896]{1,0:T(8,128)(2,1)S(1)} %copy-done.7, ...), custom_call_target="tpu_custom_call" | custom-call | tf_op jit(solution)/shard_map/blocks/pallas_call | solution.py:54
  69.1 0.0 copy-start.5
  69.1 1.0 copy-done.5
  70.0 0.0 reduce-scatter.2.cloned.1.call-update
  70.1 0.0 copy-start.9
  70.1 0.9 copy-done.9
  71.0 0.3 shard_map.67
  71.3 14.4 %all_to_all.30.arrived = f32[16,4,256]{2,1,0:T(4,128)S(1)} all-to-all(f32[16,4,256]{2,1,0:T(4,128)S(1)} %shard_map.67), channel_id=1, replica_groups=mesh['x'=4,'z'=8,'y'=8,'c'=2] {'y','c'}, dimensions={0} | all-to-all | bytes 131072 | tf_op jit(solution)/shard_map/all_to_all | solution.py:20
  85.8 0.0 copy-done
  85.8 0.4 shard_map.68
  86.1 16.6 %all_to_all.31 = f32[32,4,128]{2,1,0:T(4,128)S(1)} all-to-all(f32[32,4,128]{2,1,0:T(4,128)S(1)} %shard_map.68), channel_id=1, replica_groups=mesh['x'=4,'z'=8,'y'=8,'c'=2] {'x','z'}, dimensions={0} | all-to-all | bytes 131072 | tf_op jit(solution)/shard_map/all_to_all | solution.py:20
  102.8 13.1 %all_to_all.32.arrived = f32[32,4,128]{2,1,0:T(4,128)S(1)} all-to-all(f32[32,4,128]{2,1,0:T(4,128)S(1)} %broadcast_in_dim.4), channel_id=1, replica_groups=mesh['x'=4,'z'=8,'y'=8,'c'=2] {'x','z'}, dimensions={0} | all-to-all | bytes 131072 | tf_op jit(solution)/shard_map/all_to_all | solution.py:20
  115.9 0.0 copy-start.8
  115.9 0.7 shard_map.69
  116.6 10.8 %all_to_all.33.both = f32[16,4,384]{2,1,0:T(4,128)S(1)} all-to-all(f32[16,4,384]{2,1,0:T(4,128)S(1)} %shard_map.69), channel_id=1, replica_groups=mesh['x'=4,'z'=8,'y'=8,'c'=2] {'y','c'}, dimensions={0} | all-to-all | bytes 196608 | tf_op jit(solution)/shard_map/all_to_all | solution.py:20
  127.4 0.3 shard_map.70
  127.8 17.0 %all_to_all.34 = f32[32,2,1024]{2,1,0:T(2,128)S(1)} all-to-all(f32[32,2,1024]{2,1,0:T(2,128)S(1)} %get-tuple-element.7), channel_id=1, replica_groups=mesh['x'=4,'z'=8,'y'=8,'c'=2] {'x','z'}, dimensions={0} | all-to-all | bytes 524288 | tf_op jit(solution)/shard_map/all_to_all | solution.py:20
  144.8 0.1 reduce_sum.19
  144.9 0.8 broadcast_in_dim.5
  145.7 4.7 %all-to-all-start.5 = ((f32[32,2,1024]{2,1,0:T(2,128)}), f32[32,2,1024]{2,1,0:T(2,128)S(1)}, u32[]{:S(2)}, u32[]{:S(2)}) async-start(f32[32,2,1024]{2,1,0:T(2,128)} %broadcast_in_dim.5), calls=%async_computation.6 | async-start | bytes 524288 | tf_op jit(solution)/shard_map/all_to_all | solution.py:20
  150.4 0.0 reduce-scatter.2.cloned.1.call-done
  150.5 1.6 collective-permute-start.4
  152.0 10.7 %all-to-all-done.5.arrived = f32[32,2,1024]{2,1,0:T(2,128)S(1)} async-done(((f32[32,2,1024]{2,1,0:T(2,128)}), f32[32,2,1024]{2,1,0:T(2,128)S(1)}, u32[]{:S(2)}, u32[]{:S(2)}) %all-to-all-start.5) | async-done | bytes 262176 | tf_op jit(solution)/shard_map/all_to_all | solution.py:20
  162.7 0.0 copy-done.8
  162.7 7.2 %shard_map.71 = (f32[64,896]{1,0:T(8,128)}, f32[128,896]{1,0:T(8,128)}) custom-call(f32[32,2,1024]{2,1,0:T(2,128)S(1)} %all-to-all-done.5.arrived, f32[64,128]{1,0:T(8,128)S(1)} %get-tuple-element.8.left_rows, bf16[128,896]{1,0:T(8,128)(2,1)S(1)} %copy-done.8), custom_call_target="tpu_custom_call" | custom-call | tf_op jit(solution)/shard_map/pallas_call | solution.py:192
  169.9 0.0 collective-permute-done.4
  169.9 0.7 copy.8
  (2 shorter events, 0.1 us)
Async XLA Ops:
  7.2 50.1 %all-gather.3.cloned.1.call-start = ((), (), s32[]{:S(2)}) async-start(), calls=%async_computation.8 | async-start | bytes 2064384 | tf_op jit(solution)/shard_map/all_gather | solution.py:67
  7.9 142.6 %reduce-scatter.2.cloned.1.call-start = ((), (), s32[]{:S(2)}) async-start(), calls=%async_computation.7 | async-start | bytes 1179648 | tf_op jit(solution)/shard_map/reduce_scatter | solution.py:74
  7.9 15.7 %collective-permute-start = (bf16[256,896]{1,0:T(8,128)(2,1)}, bf16[256,896]{1,0:T(8,128)(2,1)S(1)}, u32[]{:S(2)}, u32[]{:S(2)}) collective-permute-start(bf16[256,896]{1,0:T(8,128)(2,1)} %grads.3), channel_id=1, source_target_pairs={{0,128},{128,256},{256,384},{384,0},{1,129},{129,257},{257,385},{3... | collective-permute-start | bytes 1376264 | tf_op jit(solution)/shard_map/ppermute | solution.py:29
  11.4 23.0 %collective-permute-start.1 = (bf16[256,896]{1,0:T(8,128)(2,1)}, bf16[256,896]{1,0:T(8,128)(2,1)S(1)}, u32[]{:S(2)}, u32[]{:S(2)}) collective-permute-start(bf16[256,896]{1,0:T(8,128)(2,1)} %grads.3), channel_id=1, source_target_pairs={{0,256},{128,384},{256,0},{384,128},{1,257},{129,385},{257,1},{385... | collective-permute-start | bytes 1376264 | tf_op jit(solution)/shard_map/ppermute | solution.py:29
  16.0 19.9 %collective-permute-start.2 = (bf16[256,896]{1,0:T(8,128)(2,1)}, bf16[256,896]{1,0:T(8,128)(2,1)S(1)}, u32[]{:S(2)}, u32[]{:S(2)}) collective-permute-start(bf16[256,896]{1,0:T(8,128)(2,1)} %grads.3), channel_id=1, source_target_pairs={{0,384},{128,0},{256,128},{384,256},{1,385},{129,1},{257,129},{385... | collective-permute-start | bytes 1376264 | tf_op jit(solution)/shard_map/ppermute | solution.py:29
  35.9 25.7 %copy-start.6 = (bf16[256,896]{1,0:T(8,128)(2,1)}, bf16[256,896]{1,0:T(8,128)(2,1)S(1)}, u32[]{:S(2)}) copy-start(bf16[256,896]{1,0:T(8,128)(2,1)S(1)} %collective-permute-done.2.refs_3_) | copy-start | bytes 1376260
  57.3 1.0 copy-start.1
  58.3 1.5 copy-start.3
  59.8 6.4 %copy-start.2 = (bf16[256,896]{1,0:T(8,128)(2,1)S(1)}, bf16[256,896]{1,0:T(8,128)(2,1)}, u32[]{:S(2)}) copy-start(bf16[256,896]{1,0:T(8,128)(2,1)} %grads.3) | copy-start | bytes 1376260
  59.8 6.4 %copy-start.4 = (bf16[1024,896]{1,0:T(8,128)(2,1)S(1)}, bf16[1024,896]{1,0:T(8,128)(2,1)}, u32[]{:S(2)}) copy-start(bf16[1024,896]{1,0:T(8,128)(2,1)} %all-gather.3.cloned.1.call-done) | copy-start | bytes 5505028
  61.6 4.6 %collective-permute-start.3 = (bf16[8,256,256]{2,1,0:T(8,128)(2,1)S(1)}, bf16[8,256,256]{2,1,0:T(8,128)(2,1)S(1)}, u32[]{:S(2)}, u32[]{:S(2)}) collective-permute-start(bf16[8,256,256]{2,1,0:T(8,128)(2,1)S(1)} %blocks.2), channel_id=1, source_target_pairs={{0,1},{1,0},{2,3},{3,2},{4,5},{5,4},{6,7},{7,6},{8,9},{9,8},{10,11... | collective-permute-start | bytes 3145736 | tf_op jit(solution)/shard_map/ppermute | solution.py:29
  66.2 1.0 copy-start.7
  67.2 18.5 %copy-start = (bf16[256,4096]{1,0:T(8,128)(2,1)S(1)}, bf16[256,4096]{1,0:T(8,128)(2,1)}, u32[]{:S(2)}) copy-start(bf16[256,4096]{1,0:T(8,128)(2,1)} %activations.3) | copy-start | bytes 6291460
  69.1 1.0 copy-start.5
  70.1 0.9 copy-start.9
  115.9 46.8 %copy-start.8 = (bf16[128,896]{1,0:T(8,128)(2,1)S(1)}, bf16[128,896]{1,0:T(8,128)(2,1)}, u32[]{:S(2)}) copy-start(bf16[128,896]{1,0:T(8,128)(2,1)} %weight.1) | copy-start | bytes 688132
  145.7 17.0 %all-to-all-start.5 = ((f32[32,2,1024]{2,1,0:T(2,128)}), f32[32,2,1024]{2,1,0:T(2,128)S(1)}, u32[]{:S(2)}, u32[]{:S(2)}) async-start(f32[32,2,1024]{2,1,0:T(2,128)} %broadcast_in_dim.5), calls=%async_computation.6 | async-start | bytes 524288 | tf_op jit(solution)/shard_map/all_to_all | solution.py:20
  150.5 19.4 %collective-permute-start.4 = (bf16[256,256]{1,0:T(8,128)(2,1)}, bf16[256,256]{1,0:T(8,128)(2,1)S(1)}, u32[]{:S(2)}, u32[]{:S(2)}) collective-permute-start(bf16[256,256]{1,0:T(8,128)(2,1)} %bitcast.11), channel_id=1, source_target_pairs={{0,0},{1,1},{2,2},{3,3},{4,128},{5,129},{6,130},{7,131},{8,256},{9... | collective-permute-start | bytes 393224 | tf_op jit(solution)/shard_map/ppermute | solution.py:80
Sparse Core Ops, SparseCore 0:
  10.0 47.1 all-gather.2
  70.2 39.9 reduce-scatter.1

commit v6 on v5

--- a/solution.py
+++ b/solution.py
@@ -31,46 +31,42 @@
 
 def block_kernel(n_x, where, *refs):
     grads, weights = refs[:n_x], refs[n_x]
-    earlier, parts = refs[n_x + 1 : -1], refs[-1]
-    x, side = where[0], where[1]
+    x, core = where[0], where[1]
     _, rows, hidden = weights.shape
     dims = (((1,), (1,)), ((), ()))
-    for h in range(2):
-        block = weights[pl.ds(4 * h + 2 * side, 2)].reshape(2 * rows, hidden)
-        for s in range(n_x):
-            total = lax.dot_general(grads[s][...], block, dims, preferred_element_type=jnp.float32)
-            place = 2 * lax.rem(x - s + n_x, n_x) + h
-            if earlier:
-                total += earlier[0][place].astype(jnp.float32)
-            parts[place] = total.astype(jnp.bfloat16)
-
-
-def block_products(side, grads, weights, earlier=()):
+    for side, parts in ((1 - core, refs[n_x + 1]), (core, refs[n_x + 2])):
+        for h in range(2):
+            block = weights[pl.ds(4 * h + 2 * side, 2)].reshape(2 * rows, hidden)
+            for s in range(n_x):
+                total = lax.dot_general(grads[s][...], block, dims, preferred_element_type=jnp.float32)
+                parts[2 * lax.rem(x - s + n_x, n_x) + h] = total.astype(jnp.bfloat16)
+
+
+def block_products(grads, weights):
     n_x, n_y = lax.axis_size("x"), lax.axis_size("y")
     tokens, rows = grads[0].shape[0], weights.shape[1]
     vmem = pl.BlockSpec(memory_space=pltpu.VMEM)
-    where = jnp.stack([lax.axis_index("x"), side]).astype(jnp.int32)
-    held = [pltpu.with_memory_space_constraint(a, pltpu.VMEM) for a in (*grads, *earlier)]
+    where = jnp.stack([lax.axis_index("x"), lax.axis_index("c")]).astype(jnp.int32)
+    held = [pltpu.with_memory_space_constraint(a, pltpu.VMEM) for a in grads]
     return pl.pallas_call(
         functools.partial(block_kernel, n_x),
-        out_shape=jax.ShapeDtypeStruct((n_y, tokens, 2 * rows), jnp.bfloat16),
-        in_specs=[pl.BlockSpec(memory_space=pltpu.SMEM)] + [vmem] * (n_x + 1 + len(earlier)),
-        out_specs=vmem,
+        out_shape=[space((n_y, tokens, 2 * rows), jnp.bfloat16) for space in (pltpu.HBM, pltpu.HBM)],
+        in_specs=[pl.BlockSpec(memory_space=pltpu.SMEM)] + [vmem] * (n_x + 1),
+        out_specs=[vmem] * 2,
         compiler_params=pltpu.CompilerParams(vmem_limit_bytes=16 << 20),
         name="blocks",
-    )(where, *held[:n_x], weights, *held[n_x:])
+    )(where, *held, weights)
 
 
 def input_gradient(grad_output, weight):
     n_x, n_y = lax.axis_size("x"), lax.axis_size("y")
-    core = lax.axis_index("c")
     weights = lax.all_gather(weight, "z", axis=0)
     grads = [grad_output]
     for s in range(1, n_x):
         grads.append(shifted(grad_output, "x", s))
-    give = block_products(1 - core, grads, weights)
+    give, keep = block_products(grads, weights)
     arrived = shifted(give, "c", 1)
-    parts = block_products(core, grads, weights, (arrived,))
+    parts = (keep.astype(jnp.float32) + arrived.astype(jnp.float32)).astype(jnp.bfloat16)
     summed = lax.psum_scatter(parts, "y", scatter_dimension=0)
     to = []
     for x in range(n_x):
@@ -184,9 +180,28 @@
     new_weight[...] = weight[...].astype(jnp.float32) - learn_rate * dot(basis.T, right)
 
 
-def run(kernel, shapes, *args, scratch=()):
+def hold_kernel(source, out, done):
+    copy = pltpu.make_async_copy(source, out, done)
+    copy.start()
+    copy.wait()
+
+
+def hold(x):
+    return pl.pallas_call(
+        hold_kernel,
+        out_shape=pltpu.VMEM(x.shape, x.dtype),
+        in_specs=[pl.BlockSpec(memory_space=pl.ANY)],
+        out_specs=pl.BlockSpec(memory_space=pltpu.VMEM),
+        scratch_shapes=[pltpu.SemaphoreType.DMA],
+        compiler_params=pltpu.CompilerParams(vmem_limit_bytes=4 << 20),
+        name="hold",
+    )(pltpu.with_memory_space_constraint(x, pltpu.HBM))
+
+
+def run(kernel, shapes, *args, scratch=(), held=True):
     vmem = pl.BlockSpec(memory_space=pltpu.VMEM)
-    args = [pltpu.with_memory_space_constraint(a, pltpu.VMEM) for a in args]
+    space = pltpu.VMEM if held else pltpu.HBM
+    args = [pltpu.with_memory_space_constraint(a, space) for a in args]
     several = isinstance(shapes[0], tuple)
     outs = [jax.ShapeDtypeStruct(s, jnp.float32) for s in (shapes if several else (shapes,))]
     return pl.pallas_call(
@@ -207,7 +222,8 @@
     few = rank // n_t
     f32 = jnp.float32
     input_grad = input_gradient(grad_output, weight)
-    mixed = run(mixed_kernel, (n_t, few, tokens), start_basis.T, grad_output)
+    mixed = run(mixed_kernel, (n_t, few, tokens), start_basis.T, grad_output, held=False)
+    activations = hold(activations)
     mixed = swap(mixed, TENSOR)
     left_part = run(left_kernel, (n_d, few, rows), mixed, activations, scratch=[pltpu.VMEM((16, tokens), f32)])
     left_mine = swap(left_part, DP)

time: 178 us -> 180 us (1.011)
  blocking collectives: 72 us -> 57.6 us
  starting transfers between devices: 19.7 us -> 26.5 us
  waiting for transfers between devices: 51.8 us -> 58.3 us
  Pallas kernels: 12.6 us -> 16.3 us
  local copies, waits for them, and re-layouts: 6.9 us -> 3.97 us
  other arithmetic: 0.29 us -> 2.74 us
    all_to_all x5 -> x4, blocking collectives: 72 us -> 57.6 us  [swap(): return lax.all_to_all(parts, axis, split_axis=0, concat_axis=0, tiled=True)]
    all_to_all x1 -> x2, starting transfers between devices: 4.72 us -> 11.6 us  [swap(): return lax.all_to_all(parts, axis, split_axis=0, concat_axis=0, tiled=True)]
    all_to_all x1 -> x2, waiting for transfers between devices: 10.7 us -> 16.9 us  [swap(): return lax.all_to_all(parts, axis, split_axis=0, concat_axis=0, tiled=True)]
    unnamed x21 -> x9, local copies, waits for them, and re-layouts: 6.11 us -> 3.18 us
    convert_element_type x0 -> x1, other arithmetic: none -> 2.52 us  [input_gradient(): (keep.astype(jnp.float32) + arrived.astype(jnp.float32)).astype(jnp.bfloa...]
    pallas_call x2, Pallas kernels: 3.66 us -> 5.63 us  [the longest x1 4.02 us: block_products(): pl.pallas_call(functools.partial(block_kernel, n_x), out_shape=[space((n_...]
  transfers between devices with their start and end apart: 8 -> 9, of which waited for: 6 -> 7; matrix products, arithmetic and copies ran while one was open for 1% -> 1% of each run, Pallas kernels for 5% -> 7%
where the time goes in v6:
time: 180 us; the launch traced here: 179 us
  waiting for transfers between devices  58.3 us (32%)
  blocking collectives  57.6 us (32%)
  starting transfers between devices  26.5 us (15%)
  Pallas kernels  16.3 us (9%)
  between operations  14.1 us (8%)
  local copies, waits for them, and re-layouts  3.97 us (2%)
  other arithmetic  2.74 us (2%)
    all_to_all x4, blocking collectives, swap(): return lax.all_to_all(parts, axis, split_axis=0, concat_axis=0, tiled=True)  57.6 us
    all_gather x1, waiting for transfers between devices, input_gradient(): weights = lax.all_gather(weight, 'z', axis=0)  21.4 us
    ppermute x4, waiting for transfers between devices, shifted(): lax.ppermute(x, axis, [(i, (i + by) % length) for i in range(length)])  19.3 us
    all_to_all x2, waiting for transfers between devices, swap(): return lax.all_to_all(parts, axis, split_axis=0, concat_axis=0, tiled=True)  16.9 us
    ppermute x4, starting transfers between devices, shifted(): lax.ppermute(x, axis, [(i, (i + by) % length) for i in range(length)])  13.3 us
    all_to_all x2, starting transfers between devices, swap(): return lax.all_to_all(parts, axis, split_axis=0, concat_axis=0, tiled=True)  11.6 us
    pallas_call x5, Pallas kernels, run(): pl.pallas_call(kernel, out_shape=outs if several else outs[0], in_specs=[...  10.7 us
    pallas_call x1, Pallas kernels, block_products(): pl.pallas_call(functools.partial(block_kernel, n_x), out_shape=[space((n_...  4.02 us
  transfers between devices with their start and end apart: 9, of which 7 were waited for; matrix products, arithmetic and copies ran while one was open for 1% of the time, Pallas kernels for 7%

profile of v6, /device:TPU:64, one launch (start us, length us, event | category | flops | bytes accessed | tf_op | source)
XLA Modules:
  0.0 179.5 jit_solution(12988755503726426818)
XLA Ops:
  7.2 0.0 all-gather.3.cloned.1.call-start
  7.2 0.7 all-gather.3.cloned.1.call-update
  7.9 0.0 reduce-scatter.2.cloned.1.call-start
  7.9 3.4 %collective-permute-start = (bf16[256,896]{1,0:T(8,128)(2,1)}, bf16[256,896]{1,0:T(8,128)(2,1)S(1)}, u32[]{:S(2)}, u32[]{:S(2)}) collective-permute-start(bf16[256,896]{1,0:T(8,128)(2,1)} %grads.3), channel_id=1, source_target_pairs={{0,128},{128,256},{256,384},{384,0},{1,129},{129,257},{257,385},{3... | collective-permute-start | bytes 1376264 | tf_op jit(solution)/shard_map/ppermute | solution.py:29
  11.4 4.6 %collective-permute-start.1 = (bf16[256,896]{1,0:T(8,128)(2,1)}, bf16[256,896]{1,0:T(8,128)(2,1)S(1)}, u32[]{:S(2)}, u32[]{:S(2)}) collective-permute-start(bf16[256,896]{1,0:T(8,128)(2,1)} %grads.3), channel_id=1, source_target_pairs={{0,256},{128,384},{256,0},{384,128},{1,257},{129,385},{257,1},{385... | collective-permute-start | bytes 1376264 | tf_op jit(solution)/shard_map/ppermute | solution.py:29
  16.0 3.3 %collective-permute-start.2 = (bf16[256,896]{1,0:T(8,128)(2,1)}, bf16[256,896]{1,0:T(8,128)(2,1)S(1)}, u32[]{:S(2)}, u32[]{:S(2)}) collective-permute-start(bf16[256,896]{1,0:T(8,128)(2,1)} %grads.3), channel_id=1, source_target_pairs={{0,384},{128,0},{256,128},{384,256},{1,385},{129,1},{257,129},{385... | collective-permute-start | bytes 1376264 | tf_op jit(solution)/shard_map/ppermute | solution.py:29
  19.4 0.1 pad_add_fusion.where
  19.4 4.2 %collective-permute-done.refs_1_ = bf16[256,896]{1,0:T(8,128)(2,1)S(1)} collective-permute-done((bf16[256,896]{1,0:T(8,128)(2,1)}, bf16[256,896]{1,0:T(8,128)(2,1)S(1)}, u32[]{:S(2)}, u32[]{:S(2)}) %collective-permute-start) | collective-permute-done | bytes 458784 | tf_op jit(solution)/shard_map/ppermute | solution.py:29
  23.7 10.7 %collective-permute-done.1.refs_2_ = bf16[256,896]{1,0:T(8,128)(2,1)S(1)} collective-permute-done((bf16[256,896]{1,0:T(8,128)(2,1)}, bf16[256,896]{1,0:T(8,128)(2,1)S(1)}, u32[]{:S(2)}, u32[]{:S(2)}) %collective-permute-start.1) | collective-permute-done | bytes 458784 | tf_op jit(solution)/shard_map/ppermute | solution.py:29
  34.3 1.6 collective-permute-done.2.refs_3_
  35.9 21.4 %all-gather.3.cloned.1.call-done = bf16[1024,896]{1,0:T(8,128)(2,1)} async-done(((bf16[128,896]{1,0:T(8,128)(2,1)}), bf16[1024,896]{1,0:T(8,128)(2,1)}) %all-gather.3.cloned.1.call-update) | async-done | bytes 1835024 | tf_op jit(solution)/shard_map/all_gather | solution.py:63
  57.3 0.0 copy-start
  57.3 1.0 copy-done
  58.3 0.0 copy-start.2
  58.3 1.5 copy-done.2
  59.8 4.0 %blocks.1 = (bf16[8,256,256]{2,1,0:T(8,128)(2,1)}, bf16[8,256,256]{2,1,0:T(8,128)(2,1)}) custom-call(s32[2]{0:T(128)S(1)} %pad_add_fusion.where, bf16[256,896]{1,0:T(8,128)(2,1)S(1)} %copy-done, bf16[256,896]{1,0:T(8,128)(2,1)S(1)} %collective-permute-done.refs_1_, bf16[256,896]{1,0:T(8,128)(2,1)S(1)} %collective-permute-done.1.refs_2_, ...), custom_call_target="tpu_custom_call" | custom-call | tf_op jit(solution)/shard_map/blocks/pallas_call | solution.py:51
  63.8 1.9 %collective-permute-start.3 = (bf16[8,256,256]{2,1,0:T(8,128)(2,1)}, bf16[8,256,256]{2,1,0:T(8,128)(2,1)S(1)}, u32[]{:S(2)}, u32[]{:S(2)}) collective-permute-start(bf16[8,256,256]{2,1,0:T(8,128)(2,1)} %get-tuple-element.10), channel_id=1, source_target_pairs={{0,1},{1,0},{2,3},{3,2},{4,5},{5,4},{6,7},{7,6},{8,9},{9,8},{10,11... | collective-permute-start | bytes 3145736 | tf_op jit(solution)/shard_map/ppermute | solution.py:29
  65.7 2.8 %collective-permute-done.3 = bf16[8,256,256]{2,1,0:T(8,128)(2,1)S(1)} collective-permute-done((bf16[8,256,256]{2,1,0:T(8,128)(2,1)}, bf16[8,256,256]{2,1,0:T(8,128)(2,1)S(1)}, u32[]{:S(2)}, u32[]{:S(2)}) %collective-permute-start.3) | collective-permute-done | bytes 1048608 | tf_op jit(solution)/shard_map/ppermute | solution.py:29
  68.6 2.5 %add_convert_fusion = bf16[8,256,256]{2,1,0:T(8,128)(2,1)} fusion(bf16[8,256,256]{2,1,0:T(8,128)(2,1)S(1)} %collective-permute-done.3, bf16[8,256,256]{2,1,0:T(8,128)(2,1)} %get-tuple-element.9), kind=kLoop, calls=%fused_computation | loop fusion | flops 2097152 | bytes 3145728 | tf_op jit(solution)/shard_map/convert_element_type | solution.py:69
  71.1 0.0 reduce-scatter.2.cloned.1.call-update
  71.1 2.1 %shard_map.67 = f32[16,4,256]{2,1,0:T(4,128)} custom-call(f32[64,896]{1,0:T(8,128)} %bitcast.7, bf16[256,896]{1,0:T(8,128)(2,1)} %grads.3), custom_call_target="tpu_custom_call" | custom-call | tf_op jit(solution)/shard_map/pallas_call | solution.py:207
  73.2 6.8 %all-to-all-start = ((f32[16,4,256]{2,1,0:T(4,128)}), f32[16,4,256]{2,1,0:T(4,128)S(1)}, u32[]{:S(2)}, u32[]{:S(2)}) async-start(f32[16,4,256]{2,1,0:T(4,128)} %shard_map.67), calls=%async_computation.1 | async-start | bytes 131072 | tf_op jit(solution)/shard_map/all_to_all | solution.py:20
  80.1 1.6 hold.1.activations
  81.7 0.0 copy-start.1
  81.7 6.2 %all-to-all-done.arrived = f32[16,4,256]{2,1,0:T(4,128)S(1)} async-done(((f32[16,4,256]{2,1,0:T(4,128)}), f32[16,4,256]{2,1,0:T(4,128)S(1)}, u32[]{:S(2)}, u32[]{:S(2)}) %all-to-all-start) | async-done | bytes 65568 | tf_op jit(solution)/shard_map/all_to_all | solution.py:20
  87.8 0.4 shard_map.68
  88.2 16.6 %all_to_all.30 = f32[32,4,128]{2,1,0:T(4,128)S(1)} all-to-all(f32[32,4,128]{2,1,0:T(4,128)S(1)} %shard_map.68), channel_id=1, replica_groups=mesh['x'=4,'z'=8,'y'=8,'c'=2] {'x','z'}, dimensions={0} | all-to-all | bytes 131072 | tf_op jit(solution)/shard_map/all_to_all | solution.py:20
  104.9 13.1 %all_to_all.31.arrived = f32[32,4,128]{2,1,0:T(4,128)S(1)} all-to-all(f32[32,4,128]{2,1,0:T(4,128)S(1)} %broadcast_in_dim.4), channel_id=1, replica_groups=mesh['x'=4,'z'=8,'y'=8,'c'=2] {'x','z'}, dimensions={0} | all-to-all | bytes 131072 | tf_op jit(solution)/shard_map/all_to_all | solution.py:20
  118.0 0.0 copy-start.3
  118.0 0.7 shard_map.69
  118.7 10.8 %all_to_all.32.both = f32[16,4,384]{2,1,0:T(4,128)S(1)} all-to-all(f32[16,4,384]{2,1,0:T(4,128)S(1)} %shard_map.69), channel_id=1, replica_groups=mesh['x'=4,'z'=8,'y'=8,'c'=2] {'y','c'}, dimensions={0} | all-to-all | bytes 196608 | tf_op jit(solution)/shard_map/all_to_all | solution.py:20
  129.5 0.0 copy-done.1
  129.5 0.3 shard_map.70
  129.9 17.0 %all_to_all.33 = f32[32,2,1024]{2,1,0:T(2,128)S(1)} all-to-all(f32[32,2,1024]{2,1,0:T(2,128)S(1)} %get-tuple-element.11), channel_id=1, replica_groups=mesh['x'=4,'z'=8,'y'=8,'c'=2] {'x','z'}, dimensions={0} | all-to-all | bytes 524288 | tf_op jit(solution)/shard_map/all_to_all | solution.py:20
  146.9 0.1 reduce_sum.19
  147.0 0.8 broadcast_in_dim.5
  147.8 4.7 %all-to-all-start.5 = ((f32[32,2,1024]{2,1,0:T(2,128)}), f32[32,2,1024]{2,1,0:T(2,128)S(1)}, u32[]{:S(2)}, u32[]{:S(2)}) async-start(f32[32,2,1024]{2,1,0:T(2,128)} %broadcast_in_dim.5), calls=%async_computation.6 | async-start | bytes 524288 | tf_op jit(solution)/shard_map/all_to_all | solution.py:20
  152.5 0.0 reduce-scatter.2.cloned.1.call-done
  152.5 1.6 collective-permute-start.4
  154.1 10.7 %all-to-all-done.5.arrived = f32[32,2,1024]{2,1,0:T(2,128)S(1)} async-done(((f32[32,2,1024]{2,1,0:T(2,128)}), f32[32,2,1024]{2,1,0:T(2,128)S(1)}, u32[]{:S(2)}, u32[]{:S(2)}) %all-to-all-start.5) | async-done | bytes 262176 | tf_op jit(solution)/shard_map/all_to_all | solution.py:20
  164.8 0.0 copy-done.3
  164.8 7.2 %shard_map.71 = (f32[64,896]{1,0:T(8,128)}, f32[128,896]{1,0:T(8,128)}) custom-call(f32[32,2,1024]{2,1,0:T(2,128)S(1)} %all-to-all-done.5.arrived, f32[64,128]{1,0:T(8,128)S(1)} %get-tuple-element.12.left_rows, bf16[128,896]{1,0:T(8,128)(2,1)S(1)} %copy-done.3), custom_call_target="tpu_custom_call" | custom-call | tf_op jit(solution)/shard_map/pallas_call | solution.py:207
  172.0 0.0 collective-permute-done.4
  172.0 0.7 copy.8
  (2 shorter events, 0.1 us)
Async XLA Ops:
  7.2 50.1 %all-gather.3.cloned.1.call-start = ((), (), s32[]{:S(2)}) async-start(), calls=%async_computation.8 | async-start | bytes 2064384 | tf_op jit(solution)/shard_map/all_gather | solution.py:63
  7.9 144.6 %reduce-scatter.2.cloned.1.call-start = ((), (), s32[]{:S(2)}) async-start(), calls=%async_computation.7 | async-start | bytes 1179648 | tf_op jit(solution)/shard_map/reduce_scatter | solution.py:70
  7.9 15.7 %collective-permute-start = (bf16[256,896]{1,0:T(8,128)(2,1)}, bf16[256,896]{1,0:T(8,128)(2,1)S(1)}, u32[]{:S(2)}, u32[]{:S(2)}) collective-permute-start(bf16[256,896]{1,0:T(8,128)(2,1)} %grads.3), channel_id=1, source_target_pairs={{0,128},{128,256},{256,384},{384,0},{1,129},{129,257},{257,385},{3... | collective-permute-start | bytes 1376264 | tf_op jit(solution)/shard_map/ppermute | solution.py:29
  11.4 23.0 %collective-permute-start.1 = (bf16[256,896]{1,0:T(8,128)(2,1)}, bf16[256,896]{1,0:T(8,128)(2,1)S(1)}, u32[]{:S(2)}, u32[]{:S(2)}) collective-permute-start(bf16[256,896]{1,0:T(8,128)(2,1)} %grads.3), channel_id=1, source_target_pairs={{0,256},{128,384},{256,0},{384,128},{1,257},{129,385},{257,1},{385... | collective-permute-start | bytes 1376264 | tf_op jit(solution)/shard_map/ppermute | solution.py:29
  16.0 19.9 %collective-permute-start.2 = (bf16[256,896]{1,0:T(8,128)(2,1)}, bf16[256,896]{1,0:T(8,128)(2,1)S(1)}, u32[]{:S(2)}, u32[]{:S(2)}) collective-permute-start(bf16[256,896]{1,0:T(8,128)(2,1)} %grads.3), channel_id=1, source_target_pairs={{0,384},{128,0},{256,128},{384,256},{1,385},{129,1},{257,129},{385... | collective-permute-start | bytes 1376264 | tf_op jit(solution)/shard_map/ppermute | solution.py:29
  57.3 1.0 copy-start
  58.3 1.5 copy-start.2
  63.8 4.8 %collective-permute-start.3 = (bf16[8,256,256]{2,1,0:T(8,128)(2,1)}, bf16[8,256,256]{2,1,0:T(8,128)(2,1)S(1)}, u32[]{:S(2)}, u32[]{:S(2)}) collective-permute-start(bf16[8,256,256]{2,1,0:T(8,128)(2,1)} %get-tuple-element.10), channel_id=1, source_target_pairs={{0,1},{1,0},{2,3},{3,2},{4,5},{5,4},{6,7},{7,6},{8,9},{9,8},{10,11... | collective-permute-start | bytes 3145736 | tf_op jit(solution)/shard_map/ppermute | solution.py:29
  73.2 14.6 %all-to-all-start = ((f32[16,4,256]{2,1,0:T(4,128)}), f32[16,4,256]{2,1,0:T(4,128)S(1)}, u32[]{:S(2)}, u32[]{:S(2)}) async-start(f32[16,4,256]{2,1,0:T(4,128)} %shard_map.67), calls=%async_computation.1 | async-start | bytes 131072 | tf_op jit(solution)/shard_map/all_to_all | solution.py:20
  81.7 47.9 %copy-start.1 = (bf16[256,896]{1,0:T(8,128)(2,1)S(1)}, bf16[256,896]{1,0:T(8,128)(2,1)}, u32[]{:S(2)}) copy-start(bf16[256,896]{1,0:T(8,128)(2,1)} %grads.3) | copy-start | bytes 1376260
  118.0 46.8 %copy-start.3 = (bf16[128,896]{1,0:T(8,128)(2,1)S(1)}, bf16[128,896]{1,0:T(8,128)(2,1)}, u32[]{:S(2)}) copy-start(bf16[128,896]{1,0:T(8,128)(2,1)} %weight.1) | copy-start | bytes 688132
  147.8 17.0 %all-to-all-start.5 = ((f32[32,2,1024]{2,1,0:T(2,128)}), f32[32,2,1024]{2,1,0:T(2,128)S(1)}, u32[]{:S(2)}, u32[]{:S(2)}) async-start(f32[32,2,1024]{2,1,0:T(2,128)} %broadcast_in_dim.5), calls=%async_computation.6 | async-start | bytes 524288 | tf_op jit(solution)/shard_map/all_to_all | solution.py:20
  152.5 19.4 %collective-permute-start.4 = (bf16[256,256]{1,0:T(8,128)(2,1)}, bf16[256,256]{1,0:T(8,128)(2,1)S(1)}, u32[]{:S(2)}, u32[]{:S(2)}) collective-permute-start(bf16[256,256]{1,0:T(8,128)(2,1)} %bitcast.9), channel_id=1, source_target_pairs={{0,0},{1,1},{2,2},{3,3},{4,128},{5,129},{6,130},{7,131},{8,256},{9... | collective-permute-start | bytes 393224 | tf_op jit(solution)/shard_map/ppermute | solution.py:76
Sparse Core Ops, SparseCore 0:
  10.0 47.1 all-gather.2
  71.2 40.0 reduce-scatter.1

commit v7 on v6

--- a/solution.py
+++ b/solution.py
@@ -20,10 +20,6 @@
     return lax.all_to_all(parts, axis, split_axis=0, concat_axis=0, tiled=True)
 
 
-def share(x, axis):
-    return swap(jnp.broadcast_to(x[None], (lax.axis_size(axis), *x.shape)), axis)
-
-
 def shifted(x, axis, by):
     length = lax.axis_size(axis)
     return lax.ppermute(x, axis, [(i, (i + by) % length) for i in range(length)])
@@ -31,31 +27,73 @@
 
 def block_kernel(n_x, where, *refs):
     grads, weights = refs[:n_x], refs[n_x]
+    give, keep, held, sent, arrive, leave = refs[n_x + 1 :]
     x, core = where[0], where[1]
     _, rows, hidden = weights.shape
     dims = (((1,), (1,)), ((), ()))
-    for side, parts in ((1 - core, refs[n_x + 1]), (core, refs[n_x + 2])):
-        for h in range(2):
-            block = weights[pl.ds(4 * h + 2 * side, 2)].reshape(2 * rows, hidden)
-            for s in range(n_x):
-                total = lax.dot_general(grads[s][...], block, dims, preferred_element_type=jnp.float32)
-                parts[2 * lax.rem(x - s + n_x, n_x) + h] = total.astype(jnp.bfloat16)
+    order = [(side, h) for side in range(2) for h in range(2)]
+    coming, going = [], []
+    for i, (side, h) in enumerate(order):
+        first = 4 * h + 2 * (core if side else 1 - core)
+        copy = pltpu.make_async_copy(weights.at[pl.ds(first, 2)], held.at[i], arrive.at[i])
+        copy.start()
+        coming.append(copy)
+    for i, (side, h) in enumerate(order):
+        coming[i].wait()
+        block = held[i].reshape(2 * rows, hidden)
+        for s in range(n_x):
+            total = lax.dot_general(grads[s][...], block, dims, preferred_element_type=jnp.float32)
+            place = 2 * lax.rem(x - s + n_x, n_x) + h
+            k = i * n_x + s
+            sent[k] = total.astype(jnp.bfloat16)
+            copy = pltpu.make_async_copy(sent.at[k], (keep if side else give).at[place], leave.at[k])
+            copy.start()
+            going.append(copy)
+    for copy in going:
+        copy.wait()
+
+
+def add_kernel(mine, other, out):
+    out[...] = (mine[...].astype(jnp.float32) + other[...].astype(jnp.float32)).astype(jnp.bfloat16)
+
+
+def added(mine, other):
+    args = [pltpu.with_memory_space_constraint(a, pltpu.HBM) for a in (mine, other)]
+    block = pl.BlockSpec((2, *mine.shape[1:]), lambda i: (i, 0, 0))
+    return pl.pallas_call(
+        add_kernel,
+        grid=(mine.shape[0] // 2,),
+        out_shape=pltpu.HBM(mine.shape, mine.dtype),
+        in_specs=[block] * 2,
+        out_specs=block,
+        compiler_params=pltpu.CompilerParams(vmem_limit_bytes=8 << 20),
+        name="added",
+    )(*args)
 
 
 def block_products(grads, weights):
     n_x, n_y = lax.axis_size("x"), lax.axis_size("y")
-    tokens, rows = grads[0].shape[0], weights.shape[1]
+    tokens = grads[0].shape[0]
+    _, rows, hidden = weights.shape
     vmem = pl.BlockSpec(memory_space=pltpu.VMEM)
+    anywhere = pl.BlockSpec(memory_space=pl.ANY)
     where = jnp.stack([lax.axis_index("x"), lax.axis_index("c")]).astype(jnp.int32)
     held = [pltpu.with_memory_space_constraint(a, pltpu.VMEM) for a in grads]
+    parts = (n_y, tokens, 2 * rows)
     return pl.pallas_call(
         functools.partial(block_kernel, n_x),
-        out_shape=[space((n_y, tokens, 2 * rows), jnp.bfloat16) for space in (pltpu.HBM, pltpu.HBM)],
-        in_specs=[pl.BlockSpec(memory_space=pltpu.SMEM)] + [vmem] * (n_x + 1),
-        out_specs=[vmem] * 2,
-        compiler_params=pltpu.CompilerParams(vmem_limit_bytes=16 << 20),
+        out_shape=[pltpu.HBM(parts, jnp.bfloat16)] * 2,
+        in_specs=[pl.BlockSpec(memory_space=pltpu.SMEM)] + [vmem] * n_x + [anywhere],
+        out_specs=[anywhere] * 2,
+        scratch_shapes=[
+            pltpu.VMEM((4, 2, rows, hidden), jnp.bfloat16),
+            pltpu.VMEM((2 * n_y, *parts[1:]), jnp.bfloat16),
+            pltpu.SemaphoreType.DMA((4,)),
+            pltpu.SemaphoreType.DMA((2 * n_y,)),
+        ],
+        compiler_params=pltpu.CompilerParams(vmem_limit_bytes=12 << 20),
         name="blocks",
-    )(where, *held, weights)
+    )(where, *held, pltpu.with_memory_space_constraint(weights, pltpu.HBM))
 
 
 def input_gradient(grad_output, weight):
@@ -66,7 +104,7 @@
         grads.append(shifted(grad_output, "x", s))
     give, keep = block_products(grads, weights)
     arrived = shifted(give, "c", 1)
-    parts = (keep.astype(jnp.float32) + arrived.astype(jnp.float32)).astype(jnp.bfloat16)
+    parts = added(keep, arrived)
     summed = lax.psum_scatter(parts, "y", scatter_dimension=0)
     to = []
     for x in range(n_x):
@@ -145,6 +183,15 @@
         out[d, :, :hidden] = right[d * few : (d + 1) * few]
         out[d, :, hidden : hidden + rank] = gram[d * few : (d + 1) * few]
         out[d, :, hidden + rank :] = jnp.zeros((few, out.shape[2] - hidden - rank), jnp.float32)
+
+
+def spread_kernel(arrived, mine, out):
+    total = arrived[0]
+    for d in range(1, arrived.shape[0]):
+        total += arrived[d]
+    mine[...] = total
+    for d in range(out.shape[0]):
+        out[d] = total
 
 
 def last_kernel(token_total, arrived, left_rows, weight, right_basis, new_weight, packed):
@@ -198,12 +245,12 @@
     )(pltpu.with_memory_space_constraint(x, pltpu.HBM))
 
 
-def run(kernel, shapes, *args, scratch=(), held=True):
+def run(kernel, shapes, *args, scratch=(), held=True, out=jax.ShapeDtypeStruct):
     vmem = pl.BlockSpec(memory_space=pltpu.VMEM)
     space = pltpu.VMEM if held else pltpu.HBM
     args = [pltpu.with_memory_space_constraint(a, space) for a in args]
     several = isinstance(shapes[0], tuple)
-    outs = [jax.ShapeDtypeStruct(s, jnp.float32) for s in (shapes if several else (shapes,))]
+    outs = [out(s, jnp.float32) for s in (shapes if several else (shapes,))]
     return pl.pallas_call(
         kernel,
         out_shape=outs if several else outs[0],
@@ -227,8 +274,8 @@
     mixed = swap(mixed, TENSOR)
     left_part = run(left_kernel, (n_d, few, rows), mixed, activations, scratch=[pltpu.VMEM((16, tokens), f32)])
     left_mine = swap(left_part, DP)
-    left_mine = left_mine.sum(axis=0)
-    left_few = share(left_mine, DP)
+    left_mine, left_few = run(spread_kernel, ((few, rows), (n_d, few, rows)), left_mine, out=pltpu.HBM)
+    left_few = swap(left_few, DP)
     both = run(
         seen_kernel,
         (n_t, few, tokens + rows),
@@ -247,8 +294,8 @@
         scratch=[pltpu.VMEM((rank, tokens + rows), f32)],
     )
     packed = swap(packed, DP)
-    packed = packed.sum(axis=0)
-    packed = share(packed, DP)
+    _, packed = run(spread_kernel, ((rank // n_d, width), (n_d, rank // n_d, width)), packed, out=pltpu.HBM)
+    packed = swap(packed, DP)
     right_basis, new_weight = run(
         functools.partial(last_kernel, tokens * n_d),
         ((rank, hidden), (rows, hidden)),

time: 180 us -> 184 us (1.022)
  Pallas kernels: 16.3 us -> 22.8 us
  other arithmetic: 2.74 us -> 0.08 us
    pallas_call x1 -> x2, Pallas kernels: 4.02 us -> 9.04 us  [the longest x1 5.42 us: block_products(): pl.pallas_call(functools.partial(block_kernel, n_x), out_shape=[pltpu.HBM...]
    convert_element_type x1 -> x0, other arithmetic: 2.52 us -> none  [input_gradient(): (keep.astype(jnp.float32) + arrived.astype(jnp.float32)).astype(jnp.bfloa...]
    pallas_call x5 -> x7, Pallas kernels: 10.7 us -> 12.1 us  [run(): pl.pallas_call(kernel, out_shape=outs if several else outs[0], in_specs=[...]
  transfers between devices with their start and end apart: 9 -> 9, of which waited for: 7 -> 7; matrix products, arithmetic and copies ran while one was open for 1% -> 0% of each run, Pallas kernels for 7% -> 7%
where the time goes in v7:
time: 184 us; the launch traced here: 183 us
  waiting for transfers between devices  58.3 us (32%)
  blocking collectives  58.3 us (32%)
  starting transfers between devices  26.5 us (14%)
  Pallas kernels  22.8 us (12%)
  between operations  14.1 us (8%)
  local copies, waits for them, and re-layouts  3.36 us (2%)
    all_to_all x4, blocking collectives, swap(): return lax.all_to_all(parts, axis, split_axis=0, concat_axis=0, tiled=True)  58.3 us
    all_gather x1, waiting for transfers between devices, input_gradient(): weights = lax.all_gather(weight, 'z', axis=0)  21.4 us
    ppermute x4, waiting for transfers between devices, shifted(): lax.ppermute(x, axis, [(i, (i + by) % length) for i in range(length)])  19.3 us
    all_to_all x2, waiting for transfers between devices, swap(): return lax.all_to_all(parts, axis, split_axis=0, concat_axis=0, tiled=True)  16.9 us
    ppermute x4, starting transfers between devices, shifted(): lax.ppermute(x, axis, [(i, (i + by) % length) for i in range(length)])  13.3 us
    pallas_call x7, Pallas kernels, run(): pl.pallas_call(kernel, out_shape=outs if several else outs[0], in_specs=[...  12.1 us
    all_to_all x2, starting transfers between devices, swap(): return lax.all_to_all(parts, axis, split_axis=0, concat_axis=0, tiled=True)  11.6 us
    pallas_call x1, Pallas kernels, block_products(): pl.pallas_call(functools.partial(block_kernel, n_x), out_shape=[pltpu.HBM...  5.42 us
  transfers between devices with their start and end apart: 9, of which 7 were waited for; matrix products, arithmetic and copies ran while one was open for 0% of the time, Pallas kernels for 7%

profile of v7, /device:TPU:64, one launch (start us, length us, event | category | flops | bytes accessed | tf_op | source)
XLA Modules:
  0.0 183.4 jit_solution(6213498831030682888)
XLA Ops:
  7.2 0.0 all-gather.3.cloned.1.call-start
  7.2 0.7 all-gather.3.cloned.1.call-update
  7.9 0.0 reduce-scatter.2.cloned.1.call-start
  7.9 3.4 %collective-permute-start = (bf16[256,896]{1,0:T(8,128)(2,1)}, bf16[256,896]{1,0:T(8,128)(2,1)S(1)}, u32[]{:S(2)}, u32[]{:S(2)}) collective-permute-start(bf16[256,896]{1,0:T(8,128)(2,1)} %grads.3), channel_id=1, source_target_pairs={{0,128},{128,256},{256,384},{384,0},{1,129},{129,257},{257,385},{3... | collective-permute-start | bytes 1376264 | tf_op jit(solution)/shard_map/ppermute | solution.py:25
  11.4 4.6 %collective-permute-start.1 = (bf16[256,896]{1,0:T(8,128)(2,1)}, bf16[256,896]{1,0:T(8,128)(2,1)S(1)}, u32[]{:S(2)}, u32[]{:S(2)}) collective-permute-start(bf16[256,896]{1,0:T(8,128)(2,1)} %grads.3), channel_id=1, source_target_pairs={{0,256},{128,384},{256,0},{384,128},{1,257},{129,385},{257,1},{385... | collective-permute-start | bytes 1376264 | tf_op jit(solution)/shard_map/ppermute | solution.py:25
  16.0 3.3 %collective-permute-start.2 = (bf16[256,896]{1,0:T(8,128)(2,1)}, bf16[256,896]{1,0:T(8,128)(2,1)S(1)}, u32[]{:S(2)}, u32[]{:S(2)}) collective-permute-start(bf16[256,896]{1,0:T(8,128)(2,1)} %grads.3), channel_id=1, source_target_pairs={{0,384},{128,0},{256,128},{384,256},{1,385},{129,1},{257,129},{385... | collective-permute-start | bytes 1376264 | tf_op jit(solution)/shard_map/ppermute | solution.py:25
  19.4 0.1 pad_add_fusion.where
  19.4 4.2 %collective-permute-done.refs_1_ = bf16[256,896]{1,0:T(8,128)(2,1)S(1)} collective-permute-done((bf16[256,896]{1,0:T(8,128)(2,1)}, bf16[256,896]{1,0:T(8,128)(2,1)S(1)}, u32[]{:S(2)}, u32[]{:S(2)}) %collective-permute-start) | collective-permute-done | bytes 458784 | tf_op jit(solution)/shard_map/ppermute | solution.py:25
  23.7 10.7 %collective-permute-done.1.refs_2_ = bf16[256,896]{1,0:T(8,128)(2,1)S(1)} collective-permute-done((bf16[256,896]{1,0:T(8,128)(2,1)}, bf16[256,896]{1,0:T(8,128)(2,1)S(1)}, u32[]{:S(2)}, u32[]{:S(2)}) %collective-permute-start.1) | collective-permute-done | bytes 458784 | tf_op jit(solution)/shard_map/ppermute | solution.py:25
  34.3 1.6 collective-permute-done.2.refs_3_
  35.9 21.4 %all-gather.3.cloned.1.call-done = bf16[1024,896]{1,0:T(8,128)(2,1)} async-done(((bf16[128,896]{1,0:T(8,128)(2,1)}), bf16[1024,896]{1,0:T(8,128)(2,1)}) %all-gather.3.cloned.1.call-update) | async-done | bytes 1835024 | tf_op jit(solution)/shard_map/all_gather | solution.py:101
  57.3 0.0 copy-start
  57.3 1.0 copy-done
  58.3 5.4 %blocks.1 = (bf16[8,256,256]{2,1,0:T(8,128)(2,1)}, bf16[8,256,256]{2,1,0:T(8,128)(2,1)}) custom-call(s32[2]{0:T(128)S(1)} %pad_add_fusion.where, bf16[256,896]{1,0:T(8,128)(2,1)S(1)} %copy-done, bf16[256,896]{1,0:T(8,128)(2,1)S(1)} %collective-permute-done.refs_1_, bf16[256,896]{1,0:T(8,128)(2,1)S(1)} %collective-permute-done.1.refs_2_, ...), custom_call_target="tpu_custom_call" | custom-call | tf_op jit(solution)/shard_map/blocks/pallas_call | solution.py:83
  63.7 1.9 %collective-permute-start.3 = (bf16[8,256,256]{2,1,0:T(8,128)(2,1)}, bf16[8,256,256]{2,1,0:T(8,128)(2,1)S(1)}, u32[]{:S(2)}, u32[]{:S(2)}) collective-permute-start(bf16[8,256,256]{2,1,0:T(8,128)(2,1)} %get-tuple-element.13), channel_id=1, source_target_pairs={{0,1},{1,0},{2,3},{3,2},{4,5},{5,4},{6,7},{7,6},{8,9},{9,8},{10,11... | collective-permute-start | bytes 3145736 | tf_op jit(solution)/shard_map/ppermute | solution.py:25
  65.6 2.8 %collective-permute-done.3.other = bf16[8,256,256]{2,1,0:T(8,128)(2,1)S(1)} collective-permute-done((bf16[8,256,256]{2,1,0:T(8,128)(2,1)}, bf16[8,256,256]{2,1,0:T(8,128)(2,1)S(1)}, u32[]{:S(2)}, u32[]{:S(2)}) %collective-permute-start.3) | collective-permute-done | bytes 1048608 | tf_op jit(solution)/shard_map/ppermute | solution.py:25
  68.5 0.0 copy-start.4
  68.5 1.0 copy-done.4
  69.5 3.6 %added.1 = bf16[8,256,256]{2,1,0:T(8,128)(2,1)} custom-call(bf16[8,256,256]{2,1,0:T(8,128)(2,1)} %get-tuple-element.12.mine, bf16[8,256,256]{2,1,0:T(8,128)(2,1)} %copy-done.4), custom_call_target="tpu_custom_call" | custom-call | tf_op jit(solution)/shard_map/added/pallas_call | solution.py:63
  73.1 0.0 reduce-scatter.2.cloned.1.call-update
  73.1 2.1 %shard_map.67 = f32[16,4,256]{2,1,0:T(4,128)} custom-call(f32[64,896]{1,0:T(8,128)} %bitcast.7, bf16[256,896]{1,0:T(8,128)(2,1)} %grads.3), custom_call_target="tpu_custom_call" | custom-call | tf_op jit(solution)/shard_map/pallas_call | solution.py:254
  75.2 6.8 %all-to-all-start = ((f32[16,4,256]{2,1,0:T(4,128)}), f32[16,4,256]{2,1,0:T(4,128)S(1)}, u32[]{:S(2)}, u32[]{:S(2)}) async-start(f32[16,4,256]{2,1,0:T(4,128)} %shard_map.67), calls=%async_computation.1 | async-start | bytes 131072 | tf_op jit(solution)/shard_map/all_to_all | solution.py:20
  82.1 1.6 hold.1.activations
  83.7 0.0 copy-start.1
  83.7 6.2 %all-to-all-done.arrived = f32[16,4,256]{2,1,0:T(4,128)S(1)} async-done(((f32[16,4,256]{2,1,0:T(4,128)}), f32[16,4,256]{2,1,0:T(4,128)S(1)}, u32[]{:S(2)}, u32[]{:S(2)}) %all-to-all-start) | async-done | bytes 65568 | tf_op jit(solution)/shard_map/all_to_all | solution.py:20
  89.9 0.4 shard_map.68
  90.2 16.6 %all_to_all.30.arrived = f32[32,4,128]{2,1,0:T(4,128)S(1)} all-to-all(f32[32,4,128]{2,1,0:T(4,128)S(1)} %shard_map.68), channel_id=1, replica_groups=mesh['x'=4,'z'=8,'y'=8,'c'=2] {'x','z'}, dimensions={0} | all-to-all | bytes 131072 | tf_op jit(solution)/shard_map/all_to_all | solution.py:20
  106.9 0.7 shard_map.69
  107.6 13.8 %all_to_all.31.arrived = f32[32,4,128]{2,1,0:T(4,128)S(1)} all-to-all(f32[32,4,128]{2,1,0:T(4,128)} %get-tuple-element.14), channel_id=1, replica_groups=mesh['x'=4,'z'=8,'y'=8,'c'=2] {'x','z'}, dimensions={0} | all-to-all | bytes 131072 | tf_op jit(solution)/shard_map/all_to_all | solution.py:20
  121.3 0.0 copy-start.3
  121.3 0.7 copy-done.3
  122.0 0.0 copy-start.2
  122.0 0.7 shard_map.70
  122.7 10.8 %all_to_all.32.both = f32[16,4,384]{2,1,0:T(4,128)S(1)} all-to-all(f32[16,4,384]{2,1,0:T(4,128)S(1)} %shard_map.70), channel_id=1, replica_groups=mesh['x'=4,'z'=8,'y'=8,'c'=2] {'y','c'}, dimensions={0} | all-to-all | bytes 196608 | tf_op jit(solution)/shard_map/all_to_all | solution.py:20
  133.6 0.0 copy-done.1
  133.6 0.3 shard_map.71
  133.9 17.0 %all_to_all.33.arrived = f32[32,2,1024]{2,1,0:T(2,128)S(1)} all-to-all(f32[32,2,1024]{2,1,0:T(2,128)S(1)} %get-tuple-element.16), channel_id=1, replica_groups=mesh['x'=4,'z'=8,'y'=8,'c'=2] {'x','z'}, dimensions={0} | all-to-all | bytes 524288 | tf_op jit(solution)/shard_map/all_to_all | solution.py:20
  150.9 0.8 shard_map.72
  151.7 4.7 %all-to-all-start.5 = ((f32[32,2,1024]{2,1,0:T(2,128)}), f32[32,2,1024]{2,1,0:T(2,128)S(1)}, u32[]{:S(2)}, u32[]{:S(2)}) async-start(f32[32,2,1024]{2,1,0:T(2,128)} %get-tuple-element.17), calls=%async_computation.6 | async-start | bytes 524288 | tf_op jit(solution)/shard_map/all_to_all | solution.py:20
  156.4 0.0 reduce-scatter.2.cloned.1.call-done
  156.5 1.6 collective-permute-start.4
  158.0 10.7 %all-to-all-done.5.arrived = f32[32,2,1024]{2,1,0:T(2,128)S(1)} async-done(((f32[32,2,1024]{2,1,0:T(2,128)}), f32[32,2,1024]{2,1,0:T(2,128)S(1)}, u32[]{:S(2)}, u32[]{:S(2)}) %all-to-all-start.5) | async-done | bytes 262176 | tf_op jit(solution)/shard_map/all_to_all | solution.py:20
  168.7 0.0 copy-done.2
  168.7 7.2 %shard_map.73 = (f32[64,896]{1,0:T(8,128)}, f32[128,896]{1,0:T(8,128)}) custom-call(f32[32,2,1024]{2,1,0:T(2,128)S(1)} %all-to-all-done.5.arrived, f32[64,128]{1,0:T(8,128)S(1)} %get-tuple-element.18.left_rows, bf16[128,896]{1,0:T(8,128)(2,1)S(1)} %copy-done.2), custom_call_target="tpu_custom_call" | custom-call | tf_op jit(solution)/shard_map/pallas_call | solution.py:254
  175.9 0.0 collective-permute-done.4
  175.9 0.7 copy.8
Async XLA Ops:
  7.2 50.1 %all-gather.3.cloned.1.call-start = ((), (), s32[]{:S(2)}) async-start(), calls=%async_computation.8 | async-start | bytes 2064384 | tf_op jit(solution)/shard_map/all_gather | solution.py:101
  7.9 148.6 %reduce-scatter.2.cloned.1.call-start = ((), (), s32[]{:S(2)}) async-start(), calls=%async_computation.7 | async-start | bytes 1179648 | tf_op jit(solution)/shard_map/reduce_scatter | solution.py:108
  7.9 15.7 %collective-permute-start = (bf16[256,896]{1,0:T(8,128)(2,1)}, bf16[256,896]{1,0:T(8,128)(2,1)S(1)}, u32[]{:S(2)}, u32[]{:S(2)}) collective-permute-start(bf16[256,896]{1,0:T(8,128)(2,1)} %grads.3), channel_id=1, source_target_pairs={{0,128},{128,256},{256,384},{384,0},{1,129},{129,257},{257,385},{3... | collective-permute-start | bytes 1376264 | tf_op jit(solution)/shard_map/ppermute | solution.py:25
  11.4 23.0 %collective-permute-start.1 = (bf16[256,896]{1,0:T(8,128)(2,1)}, bf16[256,896]{1,0:T(8,128)(2,1)S(1)}, u32[]{:S(2)}, u32[]{:S(2)}) collective-permute-start(bf16[256,896]{1,0:T(8,128)(2,1)} %grads.3), channel_id=1, source_target_pairs={{0,256},{128,384},{256,0},{384,128},{1,257},{129,385},{257,1},{385... | collective-permute-start | bytes 1376264 | tf_op jit(solution)/shard_map/ppermute | solution.py:25
  16.0 19.9 %collective-permute-start.2 = (bf16[256,896]{1,0:T(8,128)(2,1)}, bf16[256,896]{1,0:T(8,128)(2,1)S(1)}, u32[]{:S(2)}, u32[]{:S(2)}) collective-permute-start(bf16[256,896]{1,0:T(8,128)(2,1)} %grads.3), channel_id=1, source_target_pairs={{0,384},{128,0},{256,128},{384,256},{1,385},{129,1},{257,129},{385... | collective-permute-start | bytes 1376264 | tf_op jit(solution)/shard_map/ppermute | solution.py:25
  57.3 1.0 copy-start
  63.7 4.8 %collective-permute-start.3 = (bf16[8,256,256]{2,1,0:T(8,128)(2,1)}, bf16[8,256,256]{2,1,0:T(8,128)(2,1)S(1)}, u32[]{:S(2)}, u32[]{:S(2)}) collective-permute-start(bf16[8,256,256]{2,1,0:T(8,128)(2,1)} %get-tuple-element.13), channel_id=1, source_target_pairs={{0,1},{1,0},{2,3},{3,2},{4,5},{5,4},{6,7},{7,6},{8,9},{9,8},{10,11... | collective-permute-start | bytes 3145736 | tf_op jit(solution)/shard_map/ppermute | solution.py:25
  68.5 1.0 copy-start.4
  75.2 14.6 %all-to-all-start = ((f32[16,4,256]{2,1,0:T(4,128)}), f32[16,4,256]{2,1,0:T(4,128)S(1)}, u32[]{:S(2)}, u32[]{:S(2)}) async-start(f32[16,4,256]{2,1,0:T(4,128)} %shard_map.67), calls=%async_computation.1 | async-start | bytes 131072 | tf_op jit(solution)/shard_map/all_to_all | solution.py:20
  83.7 49.9 %copy-start.1 = (bf16[256,896]{1,0:T(8,128)(2,1)S(1)}, bf16[256,896]{1,0:T(8,128)(2,1)}, u32[]{:S(2)}) copy-start(bf16[256,896]{1,0:T(8,128)(2,1)} %grads.3) | copy-start | bytes 1376260
  121.3 0.7 copy-start.3
  122.0 46.7 %copy-start.2 = (bf16[128,896]{1,0:T(8,128)(2,1)S(1)}, bf16[128,896]{1,0:T(8,128)(2,1)}, u32[]{:S(2)}) copy-start(bf16[128,896]{1,0:T(8,128)(2,1)} %weight.1) | copy-start | bytes 688132
  151.7 17.0 %all-to-all-start.5 = ((f32[32,2,1024]{2,1,0:T(2,128)}), f32[32,2,1024]{2,1,0:T(2,128)S(1)}, u32[]{:S(2)}, u32[]{:S(2)}) async-start(f32[32,2,1024]{2,1,0:T(2,128)} %get-tuple-element.17), calls=%async_computation.6 | async-start | bytes 524288 | tf_op jit(solution)/shard_map/all_to_all | solution.py:20
  156.5 19.4 %collective-permute-start.4 = (bf16[256,256]{1,0:T(8,128)(2,1)}, bf16[256,256]{1,0:T(8,128)(2,1)S(1)}, u32[]{:S(2)}, u32[]{:S(2)}) collective-permute-start(bf16[256,256]{1,0:T(8,128)(2,1)} %bitcast.9), channel_id=1, source_target_pairs={{0,0},{1,1},{2,2},{3,3},{4,128},{5,129},{6,130},{7,131},{8,256},{9... | collective-permute-start | bytes 393224 | tf_op jit(solution)/shard_map/ppermute | solution.py:114
Sparse Core Ops, SparseCore 0:
  10.0 47.1 all-gather.2
  73.2 40.1 reduce-scatter.1

commit v8 on v7

--- a/solution.py
+++ b/solution.py
@@ -27,73 +27,75 @@
 
 def block_kernel(n_x, where, *refs):
     grads, weights = refs[:n_x], refs[n_x]
-    give, keep, held, sent, arrive, leave = refs[n_x + 1 :]
+    give, keep, lines, held, sent, enter, arrive, leave = refs[n_x + 1 :]
     x, core = where[0], where[1]
     _, rows, hidden = weights.shape
+    tokens = grads[0].shape[0]
     dims = (((1,), (1,)), ((), ()))
     order = [(side, h) for side in range(2) for h in range(2)]
-    coming, going = [], []
-    for i, (side, h) in enumerate(order):
+
+    def bring_weights(i):
+        side, h = order[i]
         first = 4 * h + 2 * (core if side else 1 - core)
         copy = pltpu.make_async_copy(weights.at[pl.ds(first, 2)], held.at[i], arrive.at[i])
         copy.start()
-        coming.append(copy)
+        return copy
+
+    def bring_grads(s):
+        copy = pltpu.make_async_copy(grads[s], lines.at[pl.ds(s * tokens, tokens)], enter.at[s])
+        copy.start()
+        return copy
+
+    first = bring_weights(0)
+    entering = [bring_grads(s) for s in range(n_x)]
+    coming = [first] + [bring_weights(i) for i in range(1, len(order))]
+    going = []
     for i, (side, h) in enumerate(order):
         coming[i].wait()
         block = held[i].reshape(2 * rows, hidden)
-        for s in range(n_x):
-            total = lax.dot_general(grads[s][...], block, dims, preferred_element_type=jnp.float32)
-            place = 2 * lax.rem(x - s + n_x, n_x) + h
-            k = i * n_x + s
-            sent[k] = total.astype(jnp.bfloat16)
-            copy = pltpu.make_async_copy(sent.at[k], (keep if side else give).at[place], leave.at[k])
-            copy.start()
-            going.append(copy)
+        step = 2 if i == 0 else n_x
+        for start in range(0, n_x, step):
+            if i == 0:
+                for s in range(start, start + step):
+                    entering[s].wait()
+            total = lax.dot_general(
+                lines[start * tokens : (start + step) * tokens], block, dims, preferred_element_type=jnp.float32
+            )
+            for s in range(start, start + step):
+                k = i * n_x + s
+                sent[k] = total[(s - start) * tokens : (s - start + 1) * tokens].astype(jnp.bfloat16)
+                place = 2 * lax.rem(x - s + n_x, n_x) + h
+                copy = pltpu.make_async_copy(sent.at[k], (keep if side else give).at[place], leave.at[k])
+                copy.start()
+                going.append(copy)
     for copy in going:
         copy.wait()
-
-
-def add_kernel(mine, other, out):
-    out[...] = (mine[...].astype(jnp.float32) + other[...].astype(jnp.float32)).astype(jnp.bfloat16)
-
-
-def added(mine, other):
-    args = [pltpu.with_memory_space_constraint(a, pltpu.HBM) for a in (mine, other)]
-    block = pl.BlockSpec((2, *mine.shape[1:]), lambda i: (i, 0, 0))
-    return pl.pallas_call(
-        add_kernel,
-        grid=(mine.shape[0] // 2,),
-        out_shape=pltpu.HBM(mine.shape, mine.dtype),
-        in_specs=[block] * 2,
-        out_specs=block,
-        compiler_params=pltpu.CompilerParams(vmem_limit_bytes=8 << 20),
-        name="added",
-    )(*args)
 
 
 def block_products(grads, weights):
     n_x, n_y = lax.axis_size("x"), lax.axis_size("y")
     tokens = grads[0].shape[0]
     _, rows, hidden = weights.shape
-    vmem = pl.BlockSpec(memory_space=pltpu.VMEM)
     anywhere = pl.BlockSpec(memory_space=pl.ANY)
     where = jnp.stack([lax.axis_index("x"), lax.axis_index("c")]).astype(jnp.int32)
-    held = [pltpu.with_memory_space_constraint(a, pltpu.VMEM) for a in grads]
+    args = [pltpu.with_memory_space_constraint(a, pltpu.HBM) for a in (*grads, weights)]
     parts = (n_y, tokens, 2 * rows)
     return pl.pallas_call(
         functools.partial(block_kernel, n_x),
         out_shape=[pltpu.HBM(parts, jnp.bfloat16)] * 2,
-        in_specs=[pl.BlockSpec(memory_space=pltpu.SMEM)] + [vmem] * n_x + [anywhere],
+        in_specs=[pl.BlockSpec(memory_space=pltpu.SMEM)] + [anywhere] * (n_x + 1),
         out_specs=[anywhere] * 2,
         scratch_shapes=[
+            pltpu.VMEM((n_x * tokens, hidden), jnp.bfloat16),
             pltpu.VMEM((4, 2, rows, hidden), jnp.bfloat16),
             pltpu.VMEM((2 * n_y, *parts[1:]), jnp.bfloat16),
+            pltpu.SemaphoreType.DMA((n_x,)),
             pltpu.SemaphoreType.DMA((4,)),
             pltpu.SemaphoreType.DMA((2 * n_y,)),
         ],
-        compiler_params=pltpu.CompilerParams(vmem_limit_bytes=12 << 20),
+        compiler_params=pltpu.CompilerParams(vmem_limit_bytes=20 << 20),
         name="blocks",
-    )(where, *held, pltpu.with_memory_space_constraint(weights, pltpu.HBM))
+    )(where, *args)
 
 
 def input_gradient(grad_output, weight):
@@ -104,7 +106,7 @@
         grads.append(shifted(grad_output, "x", s))
     give, keep = block_products(grads, weights)
     arrived = shifted(give, "c", 1)
-    parts = added(keep, arrived)
+    parts = (keep.astype(jnp.float32) + arrived.astype(jnp.float32)).astype(jnp.bfloat16)
     summed = lax.psum_scatter(parts, "y", scatter_dimension=0)
     to = []
     for x in range(n_x):
@@ -129,11 +131,14 @@
     return (parts[2 * count :] + parts[count : 2 * count]) + parts[:count]
 
 
-def mixed_kernel(basis, grads, out):
+def mixed_kernel(basis, grads, activations, out, held, done):
+    copy = pltpu.make_async_copy(activations, held, done)
+    copy.start()
     mixed = exact_dot(basis[...], grads[...], ((1,), (1,)))
     few = out.shape[1]
     for t in range(out.shape[0]):
         out[t] = mixed[t * few : (t + 1) * few]
+    copy.wait()
 
 
 def left_kernel(arrived, activations, out, lines):
@@ -194,12 +199,11 @@
         out[d] = total
 
 
-def last_kernel(token_total, arrived, left_rows, weight, right_basis, new_weight, packed):
+def factor_kernel(hidden, arrived, packed, out):
     few = arrived.shape[1]
     for d in range(arrived.shape[0]):
         packed[d * few : (d + 1) * few] = arrived[d]
     rank = packed.shape[0]
-    hidden = weight.shape[1]
     row = lax.broadcasted_iota(jnp.int32, (8, 2 * rank), 0)
     lane = lax.broadcasted_iota(jnp.int32, (8, 2 * rank), 1)
     blocks = []
@@ -219,7 +223,13 @@
     for j, block in enumerate(blocks):
         pivots = jnp.sum(jnp.where(lane == row + 8 * j, block, 0.0), axis=1, keepdims=True)
         inverse.append(block / jnp.sqrt(pivots))
-    inverse = jnp.concatenate(inverse, axis=0)[:, rank:]
+    out[...] = jnp.concatenate(inverse, axis=0)
+
+
+def last_kernel(token_total, packed, inverse, left_rows, weight, right_basis, new_weight):
+    rank = packed.shape[0]
+    hidden = weight.shape[1]
+    inverse = inverse[:, rank:]
     dot = functools.partial(jnp.dot, precision=HIGH, preferred_element_type=jnp.float32)
     right = dot(inverse, packed[:, :hidden])
     basis = dot(inverse, left_rows[...])
@@ -227,22 +237,18 @@
     new_weight[...] = weight[...].astype(jnp.float32) - learn_rate * dot(basis.T, right)
 
 
-def hold_kernel(source, out, done):
-    copy = pltpu.make_async_copy(source, out, done)
-    copy.start()
-    copy.wait()
-
-
-def hold(x):
+def mixed_and_held(basis, grads, activations, shape):
+    vmem = pl.BlockSpec(memory_space=pltpu.VMEM)
+    args = [pltpu.with_memory_space_constraint(a, pltpu.HBM) for a in (basis, grads, activations)]
     return pl.pallas_call(
-        hold_kernel,
-        out_shape=pltpu.VMEM(x.shape, x.dtype),
-        in_specs=[pl.BlockSpec(memory_space=pl.ANY)],
-        out_specs=pl.BlockSpec(memory_space=pltpu.VMEM),
+        mixed_kernel,
+        out_shape=[pltpu.HBM(shape, jnp.float32), pltpu.VMEM(activations.shape, activations.dtype)],
+        in_specs=[vmem] * 2 + [pl.BlockSpec(memory_space=pl.ANY)],
+        out_specs=[vmem] * 2,
         scratch_shapes=[pltpu.SemaphoreType.DMA],
-        compiler_params=pltpu.CompilerParams(vmem_limit_bytes=4 << 20),
-        name="hold",
-    )(pltpu.with_memory_space_constraint(x, pltpu.HBM))
+        compiler_params=pltpu.CompilerParams(vmem_limit_bytes=12 << 20),
+        name="mixed",
+    )(*args)
 
 
 def run(kernel, shapes, *args, scratch=(), held=True, out=jax.ShapeDtypeStruct):
@@ -269,8 +275,7 @@
     few = rank // n_t
     f32 = jnp.float32
     input_grad = input_gradient(grad_output, weight)
-    mixed = run(mixed_kernel, (n_t, few, tokens), start_basis.T, grad_output, held=False)
-    activations = hold(activations)
+    mixed, activations = mixed_and_held(start_basis.T, grad_output, activations, (n_t, few, tokens))
     mixed = swap(mixed, TENSOR)
     left_part = run(left_kernel, (n_d, few, rows), mixed, activations, scratch=[pltpu.VMEM((16, tokens), f32)])
     left_mine = swap(left_part, DP)
@@ -296,13 +301,16 @@
     packed = swap(packed, DP)
     _, packed = run(spread_kernel, ((rank // n_d, width), (n_d, rank // n_d, width)), packed, out=pltpu.HBM)
     packed = swap(packed, DP)
+    packed, inverse = run(
+        functools.partial(factor_kernel, hidden), ((rank, width), (rank, 2 * rank)), packed, out=pltpu.VMEM
+    )
     right_basis, new_weight = run(
         functools.partial(last_kernel, tokens * n_d),
         ((rank, hidden), (rows, hidden)),
         packed,
+        inverse,
         left_rows,
         weight,
-        scratch=[pltpu.VMEM((rank, width), f32)],
     )
     return (input_grad, right_basis.T, new_weight)
 

time: 184 us -> 184 us (level)
  blocking collectives: 58.3 us -> 72.9 us
  starting transfers between devices: 26.5 us -> 18.5 us
  waiting for transfers between devices: 58.3 us -> 53.3 us
  other arithmetic: 0.08 us -> 2.59 us
  Pallas kernels: 22.8 us -> 20.8 us
  local copies, waits for them, and re-layouts: 3.36 us -> 1.36 us
    all_to_all x4 -> x5, blocking collectives: 58.3 us -> 72.9 us  [swap(): return lax.all_to_all(parts, axis, split_axis=0, concat_axis=0, tiled=True)]
    all_to_all x2 -> x1, starting transfers between devices: 11.6 us -> 4.72 us  [swap(): return lax.all_to_all(parts, axis, split_axis=0, concat_axis=0, tiled=True)]
    all_to_all x2 -> x1, waiting for transfers between devices: 16.9 us -> 10.7 us  [swap(): return lax.all_to_all(parts, axis, split_axis=0, concat_axis=0, tiled=True)]
    ppermute x4, waiting for transfers between devices: 19.3 us -> 22.6 us  [shifted(): lax.ppermute(x, axis, [(i, (i + by) % length) for i in range(length)])]
    convert_element_type x0 -> x1, other arithmetic: none -> 2.51 us  [input_gradient(): (keep.astype(jnp.float32) + arrived.astype(jnp.float32)).astype(jnp.bfloa...]
    all_gather x1, waiting for transfers between devices: 21.4 us -> 19.2 us  [input_gradient(): weights = lax.all_gather(weight, 'z', axis=0)]
    pallas_call x7, Pallas kernels: 12.1 us -> 10 us  [run(): pl.pallas_call(kernel, out_shape=outs if several else outs[0], in_specs=[...]
    pallas_call x1, Pallas kernels: 5.42 us -> 7.44 us  [block_products(): pl.pallas_call(functools.partial(block_kernel, n_x), out_shape=[pltpu.HBM...]
  transfers between devices with their start and end apart: 9 -> 8, of which waited for: 7 -> 5; matrix products, arithmetic and copies ran while one was open for 0% -> 0% of each run, Pallas kernels for 7% -> 7%
where the time goes in v8:
time: 184 us
  blocking collectives  72.9 us (40%)
  waiting for transfers between devices  53.3 us (29%)
  Pallas kernels  20.8 us (11%)
  starting transfers between devices  18.5 us (10%)
  between operations  14.1 us (8%)
  other arithmetic  2.59 us (1%)
    all_to_all x5, blocking collectives, swap(): return lax.all_to_all(parts, axis, split_axis=0, concat_axis=0, tiled=True)  72.9 us
    ppermute x4, waiting for transfers between devices, shifted(): lax.ppermute(x, axis, [(i, (i + by) % length) for i in range(length)])  22.6 us
    all_gather x1, waiting for transfers between devices, input_gradient(): weights = lax.all_gather(weight, 'z', axis=0)  19.2 us
    ppermute x4, starting transfers between devices, shifted(): lax.ppermute(x, axis, [(i, (i + by) % length) for i in range(length)])  12.1 us
    all_to_all x1, waiting for transfers between devices, swap(): return lax.all_to_all(parts, axis, split_axis=0, concat_axis=0, tiled=True)  10.7 us
    pallas_call x7, Pallas kernels, run(): pl.pallas_call(kernel, out_shape=outs if several else outs[0], in_specs=[...  10 us
    pallas_call x1, Pallas kernels, block_products(): pl.pallas_call(functools.partial(block_kernel, n_x), out_shape=[pltpu.HBM...  7.44 us
    all_to_all x1, starting transfers between devices, swap(): return lax.all_to_all(parts, axis, split_axis=0, concat_axis=0, tiled=True)  4.72 us
  transfers between devices with their start and end apart: 8, of which 5 were waited for; matrix products, arithmetic and copies ran while one was open for 0% of the time, Pallas kernels for 7%

profile of v8, /device:TPU:64, one launch (start us, length us, event | category | flops | bytes accessed | tf_op | source)
XLA Modules:
  0.0 183.6 jit_solution(7159889007898137869)
XLA Ops:
  7.2 0.0 all-gather.3.cloned.1.call-start
  7.2 0.7 all-gather.3.cloned.1.call-update
  7.9 0.0 reduce-scatter.2.cloned.1.call-start
  7.9 4.7 %collective-permute-start.2 = (bf16[256,896]{1,0:T(8,128)(2,1)}, bf16[256,896]{1,0:T(8,128)(2,1)S(1)}, u32[]{:S(2)}, u32[]{:S(2)}) collective-permute-start(bf16[256,896]{1,0:T(8,128)(2,1)} %grads.3), channel_id=1, source_target_pairs={{0,384},{128,0},{256,128},{384,256},{1,385},{129,1},{257,129},{385... | collective-permute-start | bytes 1376264 | tf_op jit(solution)/shard_map/ppermute | solution.py:25
  12.6 2.7 %collective-permute-start.1 = (bf16[256,896]{1,0:T(8,128)(2,1)}, bf16[256,896]{1,0:T(8,128)(2,1)S(1)}, u32[]{:S(2)}, u32[]{:S(2)}) collective-permute-start(bf16[256,896]{1,0:T(8,128)(2,1)} %grads.3), channel_id=1, source_target_pairs={{0,256},{128,384},{256,0},{384,128},{1,257},{129,385},{257,1},{385... | collective-permute-start | bytes 1376264 | tf_op jit(solution)/shard_map/ppermute | solution.py:25
  15.3 2.8 %collective-permute-start = (bf16[256,896]{1,0:T(8,128)(2,1)}, bf16[256,896]{1,0:T(8,128)(2,1)S(1)}, u32[]{:S(2)}, u32[]{:S(2)}) collective-permute-start(bf16[256,896]{1,0:T(8,128)(2,1)} %grads.3), channel_id=1, source_target_pairs={{0,128},{128,256},{256,384},{384,0},{1,129},{129,257},{257,385},{3... | collective-permute-start | bytes 1376264 | tf_op jit(solution)/shard_map/ppermute | solution.py:25
  18.1 0.1 pad_add_fusion.where
  18.2 14.3 %collective-permute-done.2.refs_3_ = bf16[256,896]{1,0:T(8,128)(2,1)S(1)} collective-permute-done((bf16[256,896]{1,0:T(8,128)(2,1)}, bf16[256,896]{1,0:T(8,128)(2,1)S(1)}, u32[]{:S(2)}, u32[]{:S(2)}) %collective-permute-start.2) | collective-permute-done | bytes 458784 | tf_op jit(solution)/shard_map/ppermute | solution.py:25
  32.6 0.0 copy-start.3
  32.6 0.0 collective-permute-done.1.refs_2_
  32.6 0.0 copy-start.4
  32.6 5.5 %collective-permute-done.refs_1_ = bf16[256,896]{1,0:T(8,128)(2,1)S(1)} collective-permute-done((bf16[256,896]{1,0:T(8,128)(2,1)}, bf16[256,896]{1,0:T(8,128)(2,1)S(1)}, u32[]{:S(2)}, u32[]{:S(2)}) %collective-permute-start) | collective-permute-done | bytes 458784 | tf_op jit(solution)/shard_map/ppermute | solution.py:25
  38.0 0.0 copy-start.5
  38.0 19.2 %all-gather.3.cloned.1.call-done = bf16[1024,896]{1,0:T(8,128)(2,1)} async-done(((bf16[128,896]{1,0:T(8,128)(2,1)}), bf16[1024,896]{1,0:T(8,128)(2,1)}) %all-gather.3.cloned.1.call-update) | async-done | bytes 1835024 | tf_op jit(solution)/shard_map/all_gather | solution.py:103
  57.3 0.0 copy-done.3
  57.3 0.0 copy-done.4
  57.3 0.0 copy-done.5
  57.3 7.4 %blocks.1 = (bf16[8,256,256]{2,1,0:T(8,128)(2,1)}, bf16[8,256,256]{2,1,0:T(8,128)(2,1)}) custom-call(s32[2]{0:T(128)S(1)} %pad_add_fusion.where, bf16[256,896]{1,0:T(8,128)(2,1)} %grads.3, bf16[256,896]{1,0:T(8,128)(2,1)} %copy-done.5, bf16[256,896]{1,0:T(8,128)(2,1)} %copy-done.4, bf16[256,896]{1,0:T(8,128)(2,1)} %copy-done.3, bf16[8,128,896]{2,1,0:T(8,128)(2,1)} %bitcast.6), custom_call_target="tpu_custom_call" | custom-call | tf_op jit(solution)/shard_map/blocks/pallas_call | solution.py:83
  64.7 1.9 %collective-permute-start.3 = (bf16[8,256,256]{2,1,0:T(8,128)(2,1)}, bf16[8,256,256]{2,1,0:T(8,128)(2,1)S(1)}, u32[]{:S(2)}, u32[]{:S(2)}) collective-permute-start(bf16[8,256,256]{2,1,0:T(8,128)(2,1)} %get-tuple-element.17), channel_id=1, source_target_pairs={{0,1},{1,0},{2,3},{3,2},{4,5},{5,4},{6,7},{7,6},{8,9},{9,8},{10,11... | collective-permute-start | bytes 3145736 | tf_op jit(solution)/shard_map/ppermute | solution.py:25
  66.7 2.8 %collective-permute-done.3 = bf16[8,256,256]{2,1,0:T(8,128)(2,1)S(1)} collective-permute-done((bf16[8,256,256]{2,1,0:T(8,128)(2,1)}, bf16[8,256,256]{2,1,0:T(8,128)(2,1)S(1)}, u32[]{:S(2)}, u32[]{:S(2)}) %collective-permute-start.3) | collective-permute-done | bytes 1048608 | tf_op jit(solution)/shard_map/ppermute | solution.py:25
  69.5 2.5 %add_convert_fusion = bf16[8,256,256]{2,1,0:T(8,128)(2,1)} fusion(bf16[8,256,256]{2,1,0:T(8,128)(2,1)S(1)} %collective-permute-done.3, bf16[8,256,256]{2,1,0:T(8,128)(2,1)} %get-tuple-element.16), kind=kLoop, calls=%fused_computation | loop fusion | flops 2097152 | bytes 3145728 | tf_op jit(solution)/shard_map/convert_element_type | solution.py:109
  72.0 0.0 reduce-scatter.2.cloned.1.call-update
  72.0 3.4 %mixed.1 = (f32[16,4,256]{2,1,0:T(4,128)}, bf16[256,4096]{1,0:T(8,128)(2,1)S(1)}) custom-call(f32[64,896]{1,0:T(8,128)} %bitcast.7, bf16[256,896]{1,0:T(8,128)(2,1)} %grads.3, bf16[256,4096]{1,0:T(8,128)(2,1)} %activations.1), custom_call_target="tpu_custom_call" | custom-call | tf_op jit(solution)/shard_map/mixed/pallas_call | solution.py:243
  75.4 14.7 %all_to_all.30.arrived = f32[16,4,256]{2,1,0:T(4,128)S(1)} all-to-all(f32[16,4,256]{2,1,0:T(4,128)} %get-tuple-element.18), channel_id=1, replica_groups=mesh['x'=4,'z'=8,'y'=8,'c'=2] {'y','c'}, dimensions={0} | all-to-all | bytes 131072 | tf_op jit(solution)/shard_map/all_to_all | solution.py:20
  90.1 0.0 copy-start
  90.1 0.4 shard_map.67
  90.5 16.6 %all_to_all.31.arrived = f32[32,4,128]{2,1,0:T(4,128)S(1)} all-to-all(f32[32,4,128]{2,1,0:T(4,128)S(1)} %shard_map.67), channel_id=1, replica_groups=mesh['x'=4,'z'=8,'y'=8,'c'=2] {'x','z'}, dimensions={0} | all-to-all | bytes 131072 | tf_op jit(solution)/shard_map/all_to_all | solution.py:20
  107.1 0.7 shard_map.68
  107.8 13.8 %all_to_all.32.arrived = f32[32,4,128]{2,1,0:T(4,128)S(1)} all-to-all(f32[32,4,128]{2,1,0:T(4,128)} %get-tuple-element.20), channel_id=1, replica_groups=mesh['x'=4,'z'=8,'y'=8,'c'=2] {'x','z'}, dimensions={0} | all-to-all | bytes 131072 | tf_op jit(solution)/shard_map/all_to_all | solution.py:20
  121.5 0.0 copy-start.2
  121.5 0.7 copy-done.2
  122.2 0.0 copy-start.1
  122.2 0.7 shard_map.69
  122.9 10.8 %all_to_all.33.both = f32[16,4,384]{2,1,0:T(4,128)S(1)} all-to-all(f32[16,4,384]{2,1,0:T(4,128)S(1)} %shard_map.69), channel_id=1, replica_groups=mesh['x'=4,'z'=8,'y'=8,'c'=2] {'y','c'}, dimensions={0} | all-to-all | bytes 196608 | tf_op jit(solution)/shard_map/all_to_all | solution.py:20
  133.7 0.0 copy-done
  133.8 0.3 shard_map.70
  134.1 17.0 %all_to_all.34.arrived = f32[32,2,1024]{2,1,0:T(2,128)S(1)} all-to-all(f32[32,2,1024]{2,1,0:T(2,128)S(1)} %get-tuple-element.22), channel_id=1, replica_groups=mesh['x'=4,'z'=8,'y'=8,'c'=2] {'x','z'}, dimensions={0} | all-to-all | bytes 524288 | tf_op jit(solution)/shard_map/all_to_all | solution.py:20
  151.1 0.8 shard_map.71
  151.9 4.7 %all-to-all-start.5 = ((f32[32,2,1024]{2,1,0:T(2,128)}), f32[32,2,1024]{2,1,0:T(2,128)S(1)}, u32[]{:S(2)}, u32[]{:S(2)}) async-start(f32[32,2,1024]{2,1,0:T(2,128)} %get-tuple-element.23), calls=%async_computation.6 | async-start | bytes 524288 | tf_op jit(solution)/shard_map/all_to_all | solution.py:20
  156.6 0.0 reduce-scatter.2.cloned.1.call-done
  156.6 1.6 collective-permute-start.4
  158.2 10.7 %all-to-all-done.5.arrived = f32[32,2,1024]{2,1,0:T(2,128)S(1)} async-done(((f32[32,2,1024]{2,1,0:T(2,128)}), f32[32,2,1024]{2,1,0:T(2,128)S(1)}, u32[]{:S(2)}, u32[]{:S(2)}) %all-to-all-start.5) | async-done | bytes 262176 | tf_op jit(solution)/shard_map/all_to_all | solution.py:20
  168.9 5.4 %shard_map.72 = (f32[64,1024]{1,0:T(8,128)S(1)}, f32[64,128]{1,0:T(8,128)S(1)}) custom-call(f32[32,2,1024]{2,1,0:T(2,128)S(1)} %all-to-all-done.5.arrived), custom_call_target="tpu_custom_call" | custom-call | tf_op jit(solution)/shard_map/pallas_call | solution.py:260
  174.3 0.0 copy-done.1
  174.3 1.8 shard_map.73
  176.1 0.0 collective-permute-done.4
  176.1 0.7 copy.8
Async XLA Ops:
  7.2 50.1 %all-gather.3.cloned.1.call-start = ((), (), s32[]{:S(2)}) async-start(), calls=%async_computation.8 | async-start | bytes 2064384 | tf_op jit(solution)/shard_map/all_gather | solution.py:103
  7.9 148.7 %reduce-scatter.2.cloned.1.call-start = ((), (), s32[]{:S(2)}) async-start(), calls=%async_computation.7 | async-start | bytes 1179648 | tf_op jit(solution)/shard_map/reduce_scatter | solution.py:110
  7.9 24.6 %collective-permute-start.2 = (bf16[256,896]{1,0:T(8,128)(2,1)}, bf16[256,896]{1,0:T(8,128)(2,1)S(1)}, u32[]{:S(2)}, u32[]{:S(2)}) collective-permute-start(bf16[256,896]{1,0:T(8,128)(2,1)} %grads.3), channel_id=1, source_target_pairs={{0,384},{128,0},{256,128},{384,256},{1,385},{129,1},{257,129},{385... | collective-permute-start | bytes 1376264 | tf_op jit(solution)/shard_map/ppermute | solution.py:25
  12.6 19.9 %collective-permute-start.1 = (bf16[256,896]{1,0:T(8,128)(2,1)}, bf16[256,896]{1,0:T(8,128)(2,1)S(1)}, u32[]{:S(2)}, u32[]{:S(2)}) collective-permute-start(bf16[256,896]{1,0:T(8,128)(2,1)} %grads.3), channel_id=1, source_target_pairs={{0,256},{128,384},{256,0},{384,128},{1,257},{129,385},{257,1},{385... | collective-permute-start | bytes 1376264 | tf_op jit(solution)/shard_map/ppermute | solution.py:25
  15.3 22.7 %collective-permute-start = (bf16[256,896]{1,0:T(8,128)(2,1)}, bf16[256,896]{1,0:T(8,128)(2,1)S(1)}, u32[]{:S(2)}, u32[]{:S(2)}) collective-permute-start(bf16[256,896]{1,0:T(8,128)(2,1)} %grads.3), channel_id=1, source_target_pairs={{0,128},{128,256},{256,384},{384,0},{1,129},{129,257},{257,385},{3... | collective-permute-start | bytes 1376264 | tf_op jit(solution)/shard_map/ppermute | solution.py:25
  32.6 24.7 %copy-start.3 = (bf16[256,896]{1,0:T(8,128)(2,1)}, bf16[256,896]{1,0:T(8,128)(2,1)S(1)}, u32[]{:S(2)}) copy-start(bf16[256,896]{1,0:T(8,128)(2,1)S(1)} %collective-permute-done.2.refs_3_) | copy-start | bytes 1376260
  32.6 24.7 %copy-start.4 = (bf16[256,896]{1,0:T(8,128)(2,1)}, bf16[256,896]{1,0:T(8,128)(2,1)S(1)}, u32[]{:S(2)}) copy-start(bf16[256,896]{1,0:T(8,128)(2,1)S(1)} %collective-permute-done.1.refs_2_) | copy-start | bytes 1376260
  38.0 19.2 %copy-start.5 = (bf16[256,896]{1,0:T(8,128)(2,1)}, bf16[256,896]{1,0:T(8,128)(2,1)S(1)}, u32[]{:S(2)}) copy-start(bf16[256,896]{1,0:T(8,128)(2,1)S(1)} %collective-permute-done.refs_1_) | copy-start | bytes 1376260
  64.7 4.8 %collective-permute-start.3 = (bf16[8,256,256]{2,1,0:T(8,128)(2,1)}, bf16[8,256,256]{2,1,0:T(8,128)(2,1)S(1)}, u32[]{:S(2)}, u32[]{:S(2)}) collective-permute-start(bf16[8,256,256]{2,1,0:T(8,128)(2,1)} %get-tuple-element.17), channel_id=1, source_target_pairs={{0,1},{1,0},{2,3},{3,2},{4,5},{5,4},{6,7},{7,6},{8,9},{9,8},{10,11... | collective-permute-start | bytes 3145736 | tf_op jit(solution)/shard_map/ppermute | solution.py:25
  90.1 43.7 %copy-start = (bf16[256,896]{1,0:T(8,128)(2,1)S(1)}, bf16[256,896]{1,0:T(8,128)(2,1)}, u32[]{:S(2)}) copy-start(bf16[256,896]{1,0:T(8,128)(2,1)} %grads.3) | copy-start | bytes 1376260
  121.5 0.7 copy-start.2
  122.2 52.1 %copy-start.1 = (bf16[128,896]{1,0:T(8,128)(2,1)S(1)}, bf16[128,896]{1,0:T(8,128)(2,1)}, u32[]{:S(2)}) copy-start(bf16[128,896]{1,0:T(8,128)(2,1)} %weight.1) | copy-start | bytes 688132
  151.9 17.0 %all-to-all-start.5 = ((f32[32,2,1024]{2,1,0:T(2,128)}), f32[32,2,1024]{2,1,0:T(2,128)S(1)}, u32[]{:S(2)}, u32[]{:S(2)}) async-start(f32[32,2,1024]{2,1,0:T(2,128)} %get-tuple-element.23), calls=%async_computation.6 | async-start | bytes 524288 | tf_op jit(solution)/shard_map/all_to_all | solution.py:20
  156.6 19.5 %collective-permute-start.4 = (bf16[256,256]{1,0:T(8,128)(2,1)}, bf16[256,256]{1,0:T(8,128)(2,1)S(1)}, u32[]{:S(2)}, u32[]{:S(2)}) collective-permute-start(bf16[256,256]{1,0:T(8,128)(2,1)} %bitcast.9), channel_id=1, source_target_pairs={{0,0},{1,1},{2,2},{3,3},{4,128},{5,129},{6,130},{7,131},{8,256},{9... | collective-permute-start | bytes 393224 | tf_op jit(solution)/shard_map/ppermute | solution.py:116
Sparse Core Ops, SparseCore 0:
  10.0 47.1 all-gather.2
  72.1 40.3 reduce-scatter.1

commit v9 on v7

--- a/solution.py
+++ b/solution.py
@@ -27,71 +27,51 @@
 
 def block_kernel(n_x, where, *refs):
     grads, weights = refs[:n_x], refs[n_x]
-    give, keep, held, sent, arrive, leave = refs[n_x + 1 :]
-    x, core = where[0], where[1]
+    out, held, sent, arrive, leave = refs[n_x + 1 :]
+    x, side = where[0], where[1]
     _, rows, hidden = weights.shape
     dims = (((1,), (1,)), ((), ()))
-    order = [(side, h) for side in range(2) for h in range(2)]
     coming, going = [], []
-    for i, (side, h) in enumerate(order):
-        first = 4 * h + 2 * (core if side else 1 - core)
-        copy = pltpu.make_async_copy(weights.at[pl.ds(first, 2)], held.at[i], arrive.at[i])
+    for h in range(2):
+        copy = pltpu.make_async_copy(weights.at[pl.ds(4 * h + 2 * side, 2)], held.at[h], arrive.at[h])
         copy.start()
         coming.append(copy)
-    for i, (side, h) in enumerate(order):
-        coming[i].wait()
-        block = held[i].reshape(2 * rows, hidden)
+    for h in range(2):
+        coming[h].wait()
+        block = held[h].reshape(2 * rows, hidden)
         for s in range(n_x):
             total = lax.dot_general(grads[s][...], block, dims, preferred_element_type=jnp.float32)
+            k = h * n_x + s
+            sent[k] = total.astype(jnp.bfloat16)
             place = 2 * lax.rem(x - s + n_x, n_x) + h
-            k = i * n_x + s
-            sent[k] = total.astype(jnp.bfloat16)
-            copy = pltpu.make_async_copy(sent.at[k], (keep if side else give).at[place], leave.at[k])
+            copy = pltpu.make_async_copy(sent.at[k], out.at[place], leave.at[k])
             copy.start()
             going.append(copy)
     for copy in going:
         copy.wait()
 
 
-def add_kernel(mine, other, out):
-    out[...] = (mine[...].astype(jnp.float32) + other[...].astype(jnp.float32)).astype(jnp.bfloat16)
-
-
-def added(mine, other):
-    args = [pltpu.with_memory_space_constraint(a, pltpu.HBM) for a in (mine, other)]
-    block = pl.BlockSpec((2, *mine.shape[1:]), lambda i: (i, 0, 0))
-    return pl.pallas_call(
-        add_kernel,
-        grid=(mine.shape[0] // 2,),
-        out_shape=pltpu.HBM(mine.shape, mine.dtype),
-        in_specs=[block] * 2,
-        out_specs=block,
-        compiler_params=pltpu.CompilerParams(vmem_limit_bytes=8 << 20),
-        name="added",
-    )(*args)
-
-
-def block_products(grads, weights):
+def block_products(side, grads, weights):
     n_x, n_y = lax.axis_size("x"), lax.axis_size("y")
     tokens = grads[0].shape[0]
     _, rows, hidden = weights.shape
     vmem = pl.BlockSpec(memory_space=pltpu.VMEM)
     anywhere = pl.BlockSpec(memory_space=pl.ANY)
-    where = jnp.stack([lax.axis_index("x"), lax.axis_index("c")]).astype(jnp.int32)
+    where = jnp.stack([lax.axis_index("x"), side]).astype(jnp.int32)
     held = [pltpu.with_memory_space_constraint(a, pltpu.VMEM) for a in grads]
     parts = (n_y, tokens, 2 * rows)
     return pl.pallas_call(
         functools.partial(block_kernel, n_x),
-        out_shape=[pltpu.HBM(parts, jnp.bfloat16)] * 2,
+        out_shape=pltpu.HBM(parts, jnp.bfloat16),
         in_specs=[pl.BlockSpec(memory_space=pltpu.SMEM)] + [vmem] * n_x + [anywhere],
-        out_specs=[anywhere] * 2,
+        out_specs=anywhere,
         scratch_shapes=[
-            pltpu.VMEM((4, 2, rows, hidden), jnp.bfloat16),
-            pltpu.VMEM((2 * n_y, *parts[1:]), jnp.bfloat16),
-            pltpu.SemaphoreType.DMA((4,)),
-            pltpu.SemaphoreType.DMA((2 * n_y,)),
+            pltpu.VMEM((2, 2, rows, hidden), jnp.bfloat16),
+            pltpu.VMEM(parts, jnp.bfloat16),
+            pltpu.SemaphoreType.DMA((2,)),
+            pltpu.SemaphoreType.DMA((n_y,)),
         ],
-        compiler_params=pltpu.CompilerParams(vmem_limit_bytes=12 << 20),
+        compiler_params=pltpu.CompilerParams(vmem_limit_bytes=8 << 20),
         name="blocks",
     )(where, *held, pltpu.with_memory_space_constraint(weights, pltpu.HBM))
 
@@ -102,9 +82,11 @@
     grads = [grad_output]
     for s in range(1, n_x):
         grads.append(shifted(grad_output, "x", s))
-    give, keep = block_products(grads, weights)
+    core = lax.axis_index("c")
+    give = block_products(1 - core, grads, weights)
     arrived = shifted(give, "c", 1)
-    parts = added(keep, arrived)
+    keep = block_products(core, grads, weights)
+    parts = (keep.astype(jnp.float32) + arrived.astype(jnp.float32)).astype(jnp.bfloat16)
     summed = lax.psum_scatter(parts, "y", scatter_dimension=0)
     to = []
     for x in range(n_x):

time: 184 us -> 182 us (0.989)
  waiting for transfers between devices: 58.3 us -> 55.4 us
  other arithmetic: 0.08 us -> 2.65 us
    ppermute x4, waiting for transfers between devices: 19.3 us -> 16.5 us  [shifted(): lax.ppermute(x, axis, [(i, (i + by) % length) for i in range(length)])]
    convert_element_type x0 -> x1, other arithmetic: none -> 2.5 us  [input_gradient(): (keep.astype(jnp.float32) + arrived.astype(jnp.float32)).astype(jnp.bfloa...]
  transfers between devices with their start and end apart: 9 -> 9, of which waited for: 7 -> 6; matrix products, arithmetic and copies ran while one was open for 0% -> 0% of each run, Pallas kernels for 7% -> 10%
where the time goes in v9:
time: 182 us; the launch traced here: 181 us
  blocking collectives  58.3 us (32%)
  waiting for transfers between devices  55.4 us (30%)
  starting transfers between devices  26.6 us (15%)
  Pallas kernels  21.4 us (12%)
  between operations  14.2 us (8%)
  other arithmetic  2.65 us (1%)
  local copies, waits for them, and re-layouts  2.37 us (1%)
    all_to_all x4, blocking collectives, swap(): return lax.all_to_all(parts, axis, split_axis=0, concat_axis=0, tiled=True)  58.3 us
    all_gather x1, waiting for transfers between devices, input_gradient(): weights = lax.all_gather(weight, 'z', axis=0)  21.4 us
    all_to_all x2, waiting for transfers between devices, swap(): return lax.all_to_all(parts, axis, split_axis=0, concat_axis=0, tiled=True)  16.9 us
    ppermute x4, waiting for transfers between devices, shifted(): lax.ppermute(x, axis, [(i, (i + by) % length) for i in range(length)])  16.5 us
    ppermute x4, starting transfers between devices, shifted(): lax.ppermute(x, axis, [(i, (i + by) % length) for i in range(length)])  13.3 us
    pallas_call x7, Pallas kernels, run(): pl.pallas_call(kernel, out_shape=outs if several else outs[0], in_specs=[...  12.1 us
    all_to_all x2, starting transfers between devices, swap(): return lax.all_to_all(parts, axis, split_axis=0, concat_axis=0, tiled=True)  11.7 us
    pallas_call x2, Pallas kernels, block_products(): pl.pallas_call(functools.partial(block_kernel, n_x), out_shape=pltpu.HBM(...  7.68 us
  transfers between devices with their start and end apart: 9, of which 6 were waited for; matrix products, arithmetic and copies ran while one was open for 0% of the time, Pallas kernels for 10%

profile of v9, /device:TPU:64, one launch (start us, length us, event | category | flops | bytes accessed | tf_op | source)
XLA Modules:
  0.0 180.9 jit_solution(8808491376043498801)
XLA Ops:
  7.2 0.0 all-gather.3.cloned.1.call-start
  7.2 0.7 all-gather.3.cloned.1.call-update
  7.9 0.0 reduce-scatter.2.cloned.1.call-start
  7.9 3.4 %collective-permute-start = (bf16[256,896]{1,0:T(8,128)(2,1)}, bf16[256,896]{1,0:T(8,128)(2,1)S(1)}, u32[]{:S(2)}, u32[]{:S(2)}) collective-permute-start(bf16[256,896]{1,0:T(8,128)(2,1)} %grads.3), channel_id=1, source_target_pairs={{0,128},{128,256},{256,384},{384,0},{1,129},{129,257},{257,385},{3... | collective-permute-start | bytes 1376264 | tf_op jit(solution)/shard_map/ppermute | solution.py:25
  11.4 4.6 %collective-permute-start.1 = (bf16[256,896]{1,0:T(8,128)(2,1)}, bf16[256,896]{1,0:T(8,128)(2,1)S(1)}, u32[]{:S(2)}, u32[]{:S(2)}) collective-permute-start(bf16[256,896]{1,0:T(8,128)(2,1)} %grads.3), channel_id=1, source_target_pairs={{0,256},{128,384},{256,0},{384,128},{1,257},{129,385},{257,1},{385... | collective-permute-start | bytes 1376264 | tf_op jit(solution)/shard_map/ppermute | solution.py:25
  16.0 3.3 %collective-permute-start.2 = (bf16[256,896]{1,0:T(8,128)(2,1)}, bf16[256,896]{1,0:T(8,128)(2,1)S(1)}, u32[]{:S(2)}, u32[]{:S(2)}) collective-permute-start(bf16[256,896]{1,0:T(8,128)(2,1)} %grads.3), channel_id=1, source_target_pairs={{0,384},{128,0},{256,128},{384,256},{1,385},{129,1},{257,129},{385... | collective-permute-start | bytes 1376264 | tf_op jit(solution)/shard_map/ppermute | solution.py:25
  19.4 0.1 pad_add_fusion.1.where
  19.4 4.2 %collective-permute-done.refs_1_ = bf16[256,896]{1,0:T(8,128)(2,1)S(1)} collective-permute-done((bf16[256,896]{1,0:T(8,128)(2,1)}, bf16[256,896]{1,0:T(8,128)(2,1)S(1)}, u32[]{:S(2)}, u32[]{:S(2)}) %collective-permute-start) | collective-permute-done | bytes 458784 | tf_op jit(solution)/shard_map/ppermute | solution.py:25
  23.7 10.7 %collective-permute-done.1.refs_2_ = bf16[256,896]{1,0:T(8,128)(2,1)S(1)} collective-permute-done((bf16[256,896]{1,0:T(8,128)(2,1)}, bf16[256,896]{1,0:T(8,128)(2,1)S(1)}, u32[]{:S(2)}, u32[]{:S(2)}) %collective-permute-start.1) | collective-permute-done | bytes 458784 | tf_op jit(solution)/shard_map/ppermute | solution.py:25
  34.3 1.6 collective-permute-done.2.refs_3_
  35.9 21.4 %all-gather.3.cloned.1.call-done = bf16[1024,896]{1,0:T(8,128)(2,1)} async-done(((bf16[128,896]{1,0:T(8,128)(2,1)}), bf16[1024,896]{1,0:T(8,128)(2,1)}) %all-gather.3.cloned.1.call-update) | async-done | bytes 1835024 | tf_op jit(solution)/shard_map/all_gather | solution.py:81
  57.3 0.0 copy-start
  57.3 1.0 copy-done
  58.3 0.0 copy-start.1
  58.3 3.8 %blocks.3 = bf16[8,256,256]{2,1,0:T(8,128)(2,1)} custom-call(s32[2]{0:T(128)S(1)} %pad_add_fusion.1.where, bf16[256,896]{1,0:T(8,128)(2,1)S(1)} %copy-done, bf16[256,896]{1,0:T(8,128)(2,1)S(1)} %collective-permute-done.refs_1_, bf16[256,896]{1,0:T(8,128)(2,1)S(1)} %collective-permute-done.1.refs_2_, bf16[256,896]{1,0:T(8,128)(2,1)S(1)} %collective-permute-done.2.refs_3_, ...), custom_call_target="tpu_custom_call" | custom-call | tf_op jit(solution)/shard_map/blocks/pallas_call | solution.py:63
  62.1 1.9 %collective-permute-start.3 = (bf16[8,256,256]{2,1,0:T(8,128)(2,1)}, bf16[8,256,256]{2,1,0:T(8,128)(2,1)S(1)}, u32[]{:S(2)}, u32[]{:S(2)}) collective-permute-start(bf16[8,256,256]{2,1,0:T(8,128)(2,1)} %blocks.3), channel_id=1, source_target_pairs={{0,1},{1,0},{2,3},{3,2},{4,5},{5,4},{6,7},{7,6},{8,9},{9,8},{10,11... | collective-permute-start | bytes 3145736 | tf_op jit(solution)/shard_map/ppermute | solution.py:25
  64.1 0.1 pad_add_fusion.where
  64.1 0.0 copy-done.1
  64.1 3.8 %blocks.2 = bf16[8,256,256]{2,1,0:T(8,128)(2,1)} custom-call(s32[2]{0:T(128)S(1)} %pad_add_fusion.where, bf16[256,896]{1,0:T(8,128)(2,1)S(1)} %copy-done.1, bf16[256,896]{1,0:T(8,128)(2,1)S(1)} %collective-permute-done.refs_1_, bf16[256,896]{1,0:T(8,128)(2,1)S(1)} %collective-permute-done.1.refs_2_, bf16[256,896]{1,0:T(8,128)(2,1)S(1)} %collective-permute-done.2.refs_3_, ...), custom_call_target="tpu_custom_call" | custom-call | tf_op jit(solution)/shard_map/blocks/pallas_call | solution.py:63
  68.0 0.0 collective-permute-done.3
  68.0 2.5 %add_convert_fusion = bf16[8,256,256]{2,1,0:T(8,128)(2,1)} fusion(bf16[8,256,256]{2,1,0:T(8,128)(2,1)S(1)} %collective-permute-done.3, bf16[8,256,256]{2,1,0:T(8,128)(2,1)} %blocks.2), kind=kLoop, calls=%fused_computation | loop fusion | flops 2097152 | bytes 3145728 | tf_op jit(solution)/shard_map/convert_element_type | solution.py:89
  70.5 0.0 reduce-scatter.2.cloned.1.call-update
  70.5 2.1 %shard_map.67 = f32[16,4,256]{2,1,0:T(4,128)} custom-call(f32[64,896]{1,0:T(8,128)} %bitcast.9, bf16[256,896]{1,0:T(8,128)(2,1)} %grads.3), custom_call_target="tpu_custom_call" | custom-call | tf_op jit(solution)/shard_map/pallas_call | solution.py:236
  72.6 7.0 %all-to-all-start = ((f32[16,4,256]{2,1,0:T(4,128)}), f32[16,4,256]{2,1,0:T(4,128)S(1)}, u32[]{:S(2)}, u32[]{:S(2)}) async-start(f32[16,4,256]{2,1,0:T(4,128)} %shard_map.67), calls=%async_computation.1 | async-start | bytes 131072 | tf_op jit(solution)/shard_map/all_to_all | solution.py:20
  79.6 1.6 hold.1.activations
  81.2 0.0 copy-start.2
  81.2 6.2 %all-to-all-done.arrived = f32[16,4,256]{2,1,0:T(4,128)S(1)} async-done(((f32[16,4,256]{2,1,0:T(4,128)}), f32[16,4,256]{2,1,0:T(4,128)S(1)}, u32[]{:S(2)}, u32[]{:S(2)}) %all-to-all-start) | async-done | bytes 65568 | tf_op jit(solution)/shard_map/all_to_all | solution.py:20
  87.4 0.4 shard_map.68
  87.8 16.6 %all_to_all.30.arrived = f32[32,4,128]{2,1,0:T(4,128)S(1)} all-to-all(f32[32,4,128]{2,1,0:T(4,128)S(1)} %shard_map.68), channel_id=1, replica_groups=mesh['x'=4,'z'=8,'y'=8,'c'=2] {'x','z'}, dimensions={0} | all-to-all | bytes 131072 | tf_op jit(solution)/shard_map/all_to_all | solution.py:20
  104.4 0.7 shard_map.69
  105.1 13.8 %all_to_all.31.arrived = f32[32,4,128]{2,1,0:T(4,128)S(1)} all-to-all(f32[32,4,128]{2,1,0:T(4,128)} %get-tuple-element.10), channel_id=1, replica_groups=mesh['x'=4,'z'=8,'y'=8,'c'=2] {'x','z'}, dimensions={0} | all-to-all | bytes 131072 | tf_op jit(solution)/shard_map/all_to_all | solution.py:20
  118.8 0.0 copy-start.4
  118.8 0.7 copy-done.4
  119.5 0.0 copy-start.3
  119.5 0.7 shard_map.70
  120.2 10.8 %all_to_all.32.both = f32[16,4,384]{2,1,0:T(4,128)S(1)} all-to-all(f32[16,4,384]{2,1,0:T(4,128)S(1)} %shard_map.70), channel_id=1, replica_groups=mesh['x'=4,'z'=8,'y'=8,'c'=2] {'y','c'}, dimensions={0} | all-to-all | bytes 196608 | tf_op jit(solution)/shard_map/all_to_all | solution.py:20
  131.1 0.0 copy-done.2
  131.1 0.3 shard_map.71
  131.4 17.0 %all_to_all.33.arrived = f32[32,2,1024]{2,1,0:T(2,128)S(1)} all-to-all(f32[32,2,1024]{2,1,0:T(2,128)S(1)} %get-tuple-element.12), channel_id=1, replica_groups=mesh['x'=4,'z'=8,'y'=8,'c'=2] {'x','z'}, dimensions={0} | all-to-all | bytes 524288 | tf_op jit(solution)/shard_map/all_to_all | solution.py:20
  148.5 0.8 shard_map.72
  149.2 4.7 %all-to-all-start.5 = ((f32[32,2,1024]{2,1,0:T(2,128)}), f32[32,2,1024]{2,1,0:T(2,128)S(1)}, u32[]{:S(2)}, u32[]{:S(2)}) async-start(f32[32,2,1024]{2,1,0:T(2,128)} %get-tuple-element.13), calls=%async_computation.6 | async-start | bytes 524288 | tf_op jit(solution)/shard_map/all_to_all | solution.py:20
  153.9 0.0 reduce-scatter.2.cloned.1.call-done
  154.0 1.6 collective-permute-start.4
  155.5 10.7 %all-to-all-done.5.arrived = f32[32,2,1024]{2,1,0:T(2,128)S(1)} async-done(((f32[32,2,1024]{2,1,0:T(2,128)}), f32[32,2,1024]{2,1,0:T(2,128)S(1)}, u32[]{:S(2)}, u32[]{:S(2)}) %all-to-all-start.5) | async-done | bytes 262176 | tf_op jit(solution)/shard_map/all_to_all | solution.py:20
  166.2 0.0 copy-done.3
  166.2 7.2 %shard_map.73 = (f32[64,896]{1,0:T(8,128)}, f32[128,896]{1,0:T(8,128)}) custom-call(f32[32,2,1024]{2,1,0:T(2,128)S(1)} %all-to-all-done.5.arrived, f32[64,128]{1,0:T(8,128)S(1)} %get-tuple-element.14.left_rows, bf16[128,896]{1,0:T(8,128)(2,1)S(1)} %copy-done.3), custom_call_target="tpu_custom_call" | custom-call | tf_op jit(solution)/shard_map/pallas_call | solution.py:236
  173.4 0.0 collective-permute-done.4
  173.4 0.7 copy.8
Async XLA Ops:
  7.2 50.1 %all-gather.3.cloned.1.call-start = ((), (), s32[]{:S(2)}) async-start(), calls=%async_computation.8 | async-start | bytes 2064384 | tf_op jit(solution)/shard_map/all_gather | solution.py:81
  7.9 146.1 %reduce-scatter.2.cloned.1.call-start = ((), (), s32[]{:S(2)}) async-start(), calls=%async_computation.7 | async-start | bytes 1179648 | tf_op jit(solution)/shard_map/reduce_scatter | solution.py:90
  7.9 15.7 %collective-permute-start = (bf16[256,896]{1,0:T(8,128)(2,1)}, bf16[256,896]{1,0:T(8,128)(2,1)S(1)}, u32[]{:S(2)}, u32[]{:S(2)}) collective-permute-start(bf16[256,896]{1,0:T(8,128)(2,1)} %grads.3), channel_id=1, source_target_pairs={{0,128},{128,256},{256,384},{384,0},{1,129},{129,257},{257,385},{3... | collective-permute-start | bytes 1376264 | tf_op jit(solution)/shard_map/ppermute | solution.py:25
  11.4 23.0 %collective-permute-start.1 = (bf16[256,896]{1,0:T(8,128)(2,1)}, bf16[256,896]{1,0:T(8,128)(2,1)S(1)}, u32[]{:S(2)}, u32[]{:S(2)}) collective-permute-start(bf16[256,896]{1,0:T(8,128)(2,1)} %grads.3), channel_id=1, source_target_pairs={{0,256},{128,384},{256,0},{384,128},{1,257},{129,385},{257,1},{385... | collective-permute-start | bytes 1376264 | tf_op jit(solution)/shard_map/ppermute | solution.py:25
  16.0 19.9 %collective-permute-start.2 = (bf16[256,896]{1,0:T(8,128)(2,1)}, bf16[256,896]{1,0:T(8,128)(2,1)S(1)}, u32[]{:S(2)}, u32[]{:S(2)}) collective-permute-start(bf16[256,896]{1,0:T(8,128)(2,1)} %grads.3), channel_id=1, source_target_pairs={{0,384},{128,0},{256,128},{384,256},{1,385},{129,1},{257,129},{385... | collective-permute-start | bytes 1376264 | tf_op jit(solution)/shard_map/ppermute | solution.py:25
  57.3 1.0 copy-start
  58.3 5.8 %copy-start.1 = (bf16[256,896]{1,0:T(8,128)(2,1)S(1)}, bf16[256,896]{1,0:T(8,128)(2,1)}, u32[]{:S(2)}) copy-start(bf16[256,896]{1,0:T(8,128)(2,1)} %grads.3) | copy-start | bytes 1376260
  62.1 5.9 %collective-permute-start.3 = (bf16[8,256,256]{2,1,0:T(8,128)(2,1)}, bf16[8,256,256]{2,1,0:T(8,128)(2,1)S(1)}, u32[]{:S(2)}, u32[]{:S(2)}) collective-permute-start(bf16[8,256,256]{2,1,0:T(8,128)(2,1)} %blocks.3), channel_id=1, source_target_pairs={{0,1},{1,0},{2,3},{3,2},{4,5},{5,4},{6,7},{7,6},{8,9},{9,8},{10,11... | collective-permute-start | bytes 3145736 | tf_op jit(solution)/shard_map/ppermute | solution.py:25
  72.6 14.8 %all-to-all-start = ((f32[16,4,256]{2,1,0:T(4,128)}), f32[16,4,256]{2,1,0:T(4,128)S(1)}, u32[]{:S(2)}, u32[]{:S(2)}) async-start(f32[16,4,256]{2,1,0:T(4,128)} %shard_map.67), calls=%async_computation.1 | async-start | bytes 131072 | tf_op jit(solution)/shard_map/all_to_all | solution.py:20
  81.2 49.9 %copy-start.2 = (bf16[256,896]{1,0:T(8,128)(2,1)S(1)}, bf16[256,896]{1,0:T(8,128)(2,1)}, u32[]{:S(2)}) copy-start(bf16[256,896]{1,0:T(8,128)(2,1)} %grads.3) | copy-start | bytes 1376260
  118.8 0.7 copy-start.4
  119.5 46.7 %copy-start.3 = (bf16[128,896]{1,0:T(8,128)(2,1)S(1)}, bf16[128,896]{1,0:T(8,128)(2,1)}, u32[]{:S(2)}) copy-start(bf16[128,896]{1,0:T(8,128)(2,1)} %weight.1) | copy-start | bytes 688132
  149.2 17.0 %all-to-all-start.5 = ((f32[32,2,1024]{2,1,0:T(2,128)}), f32[32,2,1024]{2,1,0:T(2,128)S(1)}, u32[]{:S(2)}, u32[]{:S(2)}) async-start(f32[32,2,1024]{2,1,0:T(2,128)} %get-tuple-element.13), calls=%async_computation.6 | async-start | bytes 524288 | tf_op jit(solution)/shard_map/all_to_all | solution.py:20
  154.0 19.4 %collective-permute-start.4 = (bf16[256,256]{1,0:T(8,128)(2,1)}, bf16[256,256]{1,0:T(8,128)(2,1)S(1)}, u32[]{:S(2)}, u32[]{:S(2)}) collective-permute-start(bf16[256,256]{1,0:T(8,128)(2,1)} %bitcast.11), channel_id=1, source_target_pairs={{0,0},{1,1},{2,2},{3,3},{4,128},{5,129},{6,130},{7,131},{8,256},{9... | collective-permute-start | bytes 393224 | tf_op jit(solution)/shard_map/ppermute | solution.py:96
Sparse Core Ops, SparseCore 0:
  10.0 47.1 all-gather.2
  70.6 40.2 reduce-scatter.1
